TPU v7x, 256 devices: a whole 4x4x8 slice. The times are simulated.
256 devices in a mesh: seq: 64 (over x, z, core), head: 4 (over y).
Axes of the slice: x: 4, y: 4, z: 8, core: 2. Of those that a mesh axis runs over, the one named last changes fastest.
Arguments:
- face_rows: bfloat16 [16384, 1024], P('seq', 'head'), may hold values from -400 to 400
- norm_gain: float32 [1024], replicated, may hold values from 0.25 to 1.75
- w_qkv: bfloat16 [1024, 3, 1024], P(None, None, 'head'), may hold values from -1.875 to 1.875
- w_out: bfloat16 [1024, 1024], P('head'), may hold values from -0.1875 to 0.1875
- segments: int32 [16384], P('seq'), may hold values from 0 to 3, never falling along the last dimension, each value on 1 to 8192 neighbouring positions
Outputs:
- mixed: bfloat16 [16384, 1024], P('seq', 'head')
All inputs are finite; a program needn't handle non-finite values.
Results may differ from a plain program's by a relative error of at most 0.004.
The roundings to bfloat16 on the way count: a program that leaves them out, or rounds other values in their place, can miss the bound.
Values may be sent and summed in bfloat16 or wider, within the bound.
A program may use at most 128 MiB of HBM per device.

v0:
```python
import functools
import math

import jax
import jax.numpy as jnp
from jax import lax
from jax.sharding import PartitionSpec as P

HD = 128


epsilon = 1e-05
masked_score = -1e30


def attend_piece(states, piece, start, groups, head_count):
    keys_vals, key_segments = piece
    key_count = keys_vals.shape[1]
    head_size = keys_vals.shape[2] // head_count
    key_rows = keys_vals[0].reshape(key_count, head_count, head_size)
    value_rows = keys_vals[1].reshape(key_count, head_count, head_size)
    key_positions = lax.iota(jnp.int32, key_count)
    key_seg = key_segments[0].astype(jnp.float32)
    updated = []
    for group, state in zip(groups, states):
        group_queries, query_positions, query_seg = group

        def update(
            current,
            group_queries=group_queries,
            query_positions=query_positions,
            query_seg=query_seg,
        ):
            run_max, run_total, run_acc = current
            scores = jnp.einsum(
                "qhd,khd->hqk", group_queries, key_rows, preferred_element_type=jnp.float32
            )
            allowed = (key_positions[None, :] <= query_positions[:, None]) & (
                key_seg[None, :] == query_seg[:, None]
            )
            scores = jnp.where(allowed[None], scores, masked_score)
            new_max = jnp.maximum(run_max, jnp.max(scores, axis=2))
            factor = jnp.exp(run_max - new_max)
            weights = jnp.where(allowed[None], jnp.exp(scores - new_max[:, :, None]), 0.0)
            new_total = jnp.sum(weights, axis=2)
            new_acc = jnp.einsum(
                "hqk,khd->hqd",
                weights.astype(jnp.bfloat16),
                value_rows,
                preferred_element_type=jnp.float32,
            )
            return (new_max, new_total, new_acc)

        needed = (start <= jnp.max(query_positions)) & (
            key_seg[key_count - 1] >= jnp.min(query_seg)
        )
        updated.append(lax.cond(needed, update, lambda current: current, state))
    return tuple(updated)


def finish(state, width):
    run_max, run_total, run_acc = state
    result = run_acc / run_total[:, :, None]
    return jnp.transpose(result, (1, 0, 2)).reshape(result.shape[1], width).astype(jnp.bfloat16)


def per_device(face_rows, norm_gain, w_qkv, w_out, segments):
    whole = lax.all_gather(face_rows, "head", axis=1, tiled=True)
    row_count, model_width = whole.shape
    width = w_qkv.shape[2]
    head_count = width // HD
    half = row_count // 2
    values32 = whole.astype(jnp.float32)
    normed = (
        values32
        * lax.rsqrt(jnp.mean(values32 * values32, axis=1, keepdims=True) + epsilon)
        * norm_gain
    ).astype(jnp.bfloat16)
    projected = jnp.dot(
        normed, w_qkv.reshape(model_width, 3 * width), preferred_element_type=jnp.float32
    )
    queries = (projected[:, :width] * (1.0 / math.sqrt(HD))).astype(jnp.bfloat16)
    keys_vals = jnp.stack([projected[:, width : 2 * width], projected[:, 2 * width :]]).astype(
        jnp.bfloat16
    )
    shard_index = lax.axis_index("seq")
    positions = shard_index * row_count + lax.iota(jnp.int32, row_count)
    seg_values = segments.astype(jnp.float32)
    seg_wire = seg_values.astype(jnp.bfloat16)[None, :]
    lower = (queries[:half].reshape(half, head_count, HD), positions[:half], seg_values[:half])
    upper = (queries[half:].reshape(half, head_count, HD), positions[half:], seg_values[half:])
    groups = (lower, upper)
    start_state = (
        jnp.full((head_count, half), masked_score, jnp.float32),
        jnp.zeros((head_count, half), jnp.float32),
        jnp.zeros((head_count, half, HD), jnp.float32),
    )
    attend = functools.partial(attend_piece, groups=groups, head_count=head_count)
    states = attend(
        (start_state, start_state),
        (
            lax.all_gather(keys_vals, "seq", axis=1, tiled=True),
            lax.all_gather(seg_wire, "seq", axis=1, tiled=True),
        ),
        jnp.int32(0),
    )
    lower_out = finish(states[0], width)
    upper_out = finish(states[1], width)
    attended = jnp.concatenate([lower_out, upper_out], axis=0)
    partial_sums = jnp.dot(attended, w_out, preferred_element_type=jnp.float32)
    return lax.psum_scatter(partial_sums, "head", scatter_dimension=1, tiled=True).astype(
        jnp.bfloat16
    )


def solution(mesh):
    in_specs = (P("seq", "head"), P(), P(None, None, "head"), P("head", None), P("seq"))
    out_specs = P("seq", "head")
    return jax.shard_map(
        per_device, mesh=mesh, in_specs=in_specs, out_specs=out_specs, check_vma=False
    )
```

profile of v0, /device:TPU:5, one launch (start us, length us, event | category | flops | bytes accessed | tf_op | source)
XLA Modules:
  0.0 260.3 jit_solution(16025028984586071454)
XLA Ops:
  6.5 12.1 %all_gather.10 = bf16[256,1024]{1,0:T(8,128)(2,1)S(1)} all-gather(bf16[256,256]{1,0:T(8,128)(2,1)} %param.9), channel_id=1, replica_groups=mesh['seq'=64,'head'=4] {'head'}, dimensions={1}, use_global_device_ids=true | all-gather | bytes 655360 | tf_op jit(solution)/shard_map/all_gather | solution.py:68
  18.6 0.2 fusion.20
  18.8 1.7 copy.23
  20.6 1.3 fusion.37
  21.9 0.7 pad_maximum_fusion
  22.6 0.0 all-gather.4.cloned.1.call-update
  22.7 0.0 reduce-scatter.2.cloned.1.call-start
  22.8 47.4 %all-gather.1 = bf16[64,1,256]{2,1,0:T(2,128)(2,1)S(1)} all-gather(bf16[1,1,256]{2,1,0:T(2,128)(2,1)S(1)} %reshape.149), channel_id=2, replica_groups=mesh['seq'=64,'head'=4] {'seq'}, dimensions={0}, use_global_device_ids=true | all-gather | bytes 33280 | tf_op jit(solution)/shard_map/all_gather | solution.py:103
  70.2 0.1 convert_element_type.72
  70.3 0.7 slice.54
  70.9 0.7 slice_reduce_fusion.2
  73.0 0.7 slice_reduce_fusion.3
  76.4 48.9 %all-gather.4.cloned.1.call-done = bf16[2,16384,256]{2,1,0:T(8,128)(2,1)} async-done(((bf16[2,256,256]{2,1,0:T(8,128)(2,1)}), bf16[2,16384,256]{2,1,0:T(8,128)(2,1)}) %all-gather.4.cloned.1.call-update) | async-done | bytes 16777232 | tf_op jit(solution)/shard_map/all_gather | solution.py:102
  125.3 11.3 %fusion.35 = (bf16[1,16384,256]{2,1,0:T(8,128)(2,1)}, bf16[1,16384,256]{2,1,0:T(8,128)(2,1)}) fusion(bf16[2,16384,256]{2,1,0:T(8,128)(2,1)} %all-gather.4.cloned.1.call-done), kind=kLoop, calls=%fused_computation.55 | loop fusion | bytes 33554432 | tf_op jit(solution)/shard_map/slice | solution.py:21
  136.6 12.5 %reshape_squeeze.6 = bf16[16384,2,128]{2,1,0:T(2,128)(2,1)} reshape(bf16[1,16384,256]{2,1,0:T(8,128)(2,1)} %get-tuple-element.112) | data formatting | bytes 16777216 | tf_op jit(solution)/shard_map/reshape;squeeze | solution.py:20
  149.1 12.6 %reshape_squeeze.7 = bf16[16384,2,128]{2,1,0:T(2,128)(2,1)} reshape(bf16[1,16384,256]{2,1,0:T(8,128)(2,1)} %get-tuple-element.111) | data formatting | bytes 16777216 | tf_op jit(solution)/shard_map/reshape;squeeze | solution.py:21
  161.7 33.0 %conditional.2 = (f32[2,128]{1,0:T(2,128)S(1)}, f32[2,128,128]{1,2,0:T(8,128)S(1)}) conditional(s32[]{:T(128)} %convert_element_type.58, () %tuple.21, (s32[16384]{0:T(1024)S(1)}, s32[128]{0:T(128)S(1)}, f32[16384]{0:T(1024)S(1)}, f32[128]{0:T(128)S(1)}, bf16[256,256]{1,0:T(8,128)(2,1)S(1)}, /*index=5*/bf16[16384,2,128]{2,1,0:T(2,128)(2,1)}, ...), branch_computations={%region_3.0_spmd, %region_4.7_spmd} | conditional | flops 2187329280 | bytes 76487728 | solution.py:57
  161.7 0.6 copy-done.2
  162.3 2.5 compare_and_fusion
  164.8 0.1 copy.24
  165.0 10.7 %fusion.33 = (f32[2,128]{1,0:T(2,128)S(1)}, f32[2,128,16384]{2,1,0:T(8,128)}) fusion(bf16[128,2,128]{0,2,1:T(8,128)(2,1)S(1)} %bitcast.24, bf16[16384,2,128]{2,1,0:T(2,128)(2,1)} %get-tuple-element.92, pred[128,16384]{1,0:T(8,128)(4,1)S(1)} %compare_and_fusion), kind=kOutput, calls=%fused_computation.53 | convolution fusion | flops 1082130176 | bytes 27329536 | tf_op jit(solution)/shard_map/cond/branch_1_fun/qhd,khd->hqk/dot_general | solution.py:35
  175.6 11.1 %fusion.2 = f32[2,128,128]{1,2,0:T(8,128)S(1)} fusion(f32[2,128,16384]{2,1,0:T(8,128)} %get-tuple-element.108, bf16[16384,2,128]{2,1,0:T(2,128)(2,1)} %get-tuple-element.93, f32[2,128]{1,0:T(2,128)S(1)} %broadcast_maximum_fusion, pred[128,16384]{1,0:T(8,128)(4,1)S(1)} %compare_and_fusion), kind=kOutput, calls=%fused_computation.4 | convolution fusion | flops 1086324736 | bytes 27395072 | tf_op jit(solution)/shard_map/cond | solution.py:57
  186.7 8.0 %fusion.1 = f32[2,128]{1,0:T(2,128)S(1)} fusion(f32[2,128,16384]{2,1,0:T(8,128)} %get-tuple-element.108, f32[2,128]{1,0:T(2,128)S(1)} %broadcast_maximum_fusion, pred[128,16384]{1,0:T(8,128)(4,1)S(1)} %compare_and_fusion), kind=kLoop, calls=%fused_computation.3 | loop fusion | flops 12582656 | bytes 18876416 | tf_op jit(solution)/shard_map/cond/branch_1_fun/reduce_sum | solution.py:45
  194.8 32.6 %conditional.3 = (f32[2,128]{1,0:T(2,128)S(1)}, f32[2,128,128]{1,2,0:T(8,128)S(1)}) conditional(s32[]{:T(128)} %convert_element_type.66, () %tuple.23, (s32[16384]{0:T(1024)S(1)}, s32[128]{0:T(128)S(1)}, f32[16384]{0:T(1024)}, f32[128]{0:T(128)S(1)}, bf16[256,256]{1,0:T(8,128)(2,1)S(1)}, /*index=5*/bf16[16384,2,128]{2,1,0:T(2,128)(2,1)}, ...), branch_computations={%region_9.10_spmd, %region_10.13_spmd} | conditional | flops 2187329280 | bytes 76225552 | solution.py:57
  195.0 2.5 compare_and_fusion.1
  197.5 0.1 copy.28
  197.6 10.7 %fusion.34 = (f32[2,128]{1,0:T(2,128)S(1)}, f32[2,128,16384]{2,1,0:T(8,128)}) fusion(bf16[128,2,128]{0,2,1:T(8,128)(2,1)S(1)} %bitcast.25, bf16[16384,2,128]{2,1,0:T(2,128)(2,1)} %get-tuple-element.99, pred[128,16384]{1,0:T(8,128)(4,1)S(1)} %compare_and_fusion.1), kind=kOutput, calls=%fused_computation.54 | convolution fusion | flops 1082130176 | bytes 27329536 | tf_op jit(solution)/shard_map/cond/branch_1_fun/qhd,khd->hqk/dot_general | solution.py:35
  208.3 11.1 %fusion.12 = f32[2,128,128]{1,2,0:T(8,128)S(1)} fusion(f32[2,128,16384]{2,1,0:T(8,128)} %get-tuple-element.110, bf16[16384,2,128]{2,1,0:T(2,128)(2,1)} %get-tuple-element.100, f32[2,128]{1,0:T(2,128)S(1)} %broadcast_maximum_fusion.1, pred[128,16384]{1,0:T(8,128)(4,1)S(1)} %compare_and_fusion.1), kind=kOutput, calls=%fused_computation.17 | convolution fusion | flops 1086324736 | bytes 27395072 | tf_op jit(solution)/shard_map/cond | solution.py:57
  219.3 8.0 %fusion.11 = f32[2,128]{1,0:T(2,128)S(1)} fusion(f32[2,128,16384]{2,1,0:T(8,128)} %get-tuple-element.110, f32[2,128]{1,0:T(2,128)S(1)} %broadcast_maximum_fusion.1, pred[128,16384]{1,0:T(8,128)(4,1)S(1)} %compare_and_fusion.1), kind=kLoop, calls=%fused_computation.16 | loop fusion | flops 12582656 | bytes 18876416 | tf_op jit(solution)/shard_map/cond/branch_1_fun/reduce_sum | solution.py:45
  227.4 1.3 fusion.28
  228.7 23.1 %reduce-scatter.2.cloned.1.call-done = f32[256,256]{1,0:T(8,128)} async-done(((f32[256,1024]{1,0:T(8,128)}), f32[256,256]{1,0:T(8,128)}) %reduce-scatter.2.cloned.1.call-update) | async-done | bytes 262160 | tf_op jit(solution)/shard_map/reduce_scatter | solution.py:111
  251.9 1.6 convert_element_type.70
  (23 shorter events, 0.2 us)
Async XLA Ops:
  6.5 220.9 %copy-start = (bf16[256,1024]{1,0:T(8,128)(2,1)S(1)}, bf16[256,1024]{1,0:T(8,128)(2,1)}, u32[]{:S(2)}) copy-start(bf16[256,1024]{1,0:T(8,128)(2,1)} %param.12) | copy-start | bytes 1572868
  6.5 16.2 %copy-start.3 = (s32[256]{0:T(256)S(1)}, s32[256]{0:T(256)}, u32[]{:S(2)}) copy-start(s32[256]{0:T(256)} %param.13) | copy-start | bytes 3076
  6.5 118.7 %all-gather.4.cloned.1.call-start = ((), (), s32[]{:S(2)}) async-start(), calls=%async_computation.1 | async-start | bytes 17039360 | tf_op jit(solution)/shard_map/all_gather | solution.py:102
  22.7 229.2 %reduce-scatter.2.cloned.1.call-start = ((), (), s32[]{:S(2)}) async-start(), calls=%async_computation.2 | async-start | bytes 1310720 | tf_op jit(solution)/shard_map/reduce_scatter | solution.py:111
  70.3 91.4 %copy-start.1 = (f32[64,1,256]{2,1,0:T(1,128)}, f32[64,1,256]{2,1,0:T(1,128)S(1)}, u32[]{:S(2)}) copy-start(f32[64,1,256]{2,1,0:T(1,128)S(1)} %convert_element_type.72) | copy-start | bytes 196612
  161.7 0.6 copy-start.2
Sparse Core Ops, SparseCore 0:
  22.8 102.4 all-gather.3
  228.9 22.9 reduce-scatter.1
where the time goes:
time: 263 us; the launch traced here: 260 us
  waiting for transfers between devices  72 us (27%)
  blocking collectives  59.5 us (23%)
  matrix products  46 us (17%)
  local copies, waits for them, and re-layouts  39.6 us (15%)
  other arithmetic  25.2 us (10%)
  between operations  17.5 us (7%)
    all_gather x1, waiting for transfers between devices, per_device(): lax.all_gather(keys_vals, 'seq', axis=1, tiled=True)  48.9 us
    all_gather x1, blocking collectives, per_device(): lax.all_gather(seg_wire, 'seq', axis=1, tiled=True)  47.4 us
    reduce_scatter x1, waiting for transfers between devices, per_device(): lax.psum_scatter(partial_sums, 'head', scatter_dimension=1, tiled=True)  23.1 us
    cond x2, matrix products, attend_piece(): updated.append(lax.cond(needed, update, lambda current: current, state))  22.1 us
    dot_general x2, matrix products, update(): jnp.einsum('qhd,khd->hqk', group_queries, key_rows, preferred_element_typ...  21.3 us
    reduce_sum x2, other arithmetic, update(): new_total = jnp.sum(weights, axis=2)  16 us
    another operation x1, local copies, waits for them, and re-layouts, attend_piece(): value_rows = keys_vals[1].reshape(key_count, head_count, head_size)  12.6 us
    another operation x1, local copies, waits for them, and re-layouts, attend_piece(): key_rows = keys_vals[0].reshape(key_count, head_count, head_size)  12.5 us
  transfers between devices with their start and end apart: 2, of which 2 were waited for; matrix products, arithmetic and copies ran while one was open for 1% of the time, Pallas kernels for 0%

commit v1 on v0

v1 whole, which is shorter than its diff:
```python
import functools
import math

import jax
import jax.numpy as jnp
from jax import lax
from jax.experimental import pallas as pl
from jax.experimental.pallas import tpu as pltpu
from jax.sharding import PartitionSpec as P

MESH = pl.DeviceIdType.MESH
HD = 128
epsilon = 1e-05
masked_score = -1e30
PLAN = (
    (870258657, 812574466, 850160585, 871119793, 829180757, 541631245, 7),
    (882874144, 870062881, 887908237, 896281557, 824998833, 533274, 5),
    (1021257508, 839658277, 820774869, 829180829, 900496153, 785, 5),
    (958347176, 815545124, 839685973, 829384530, 837711706, 769, 5),
    (895436588, 1033653160, 849173284, 806319877, 871118618, 833, 5),
    (1033852720, 866999212, 940390237, 907842344, 811345681, 798, 5),
    (1037952948, 873224112, 891091756, 848107290, 807179017, 781, 5),
    (937190208, 827123457, 857621317, 952957769, 828154733, 804, 4),
    (613287492, 1012665149, 815536926, 828323769, 854354698, 829180817, 7),
    (1012826696, 840702921, 883767229, 1000143633, 896297877, 801554, 7),
    (1021257636, 839730954, 854546213, 829224737, 832338770, 794, 7),
    (1025324968, 1029449508, 839732005, 820930358, 970812161, 798, 5),
    (895469484, 819743656, 849307396, 836528901, 837606272, 769, 5),
    (1033721648, 867087121, 819733469, 944601984, 811345697, 790, 5),
    (990734260, 873428757, 824095684, 811475742, 815544090, 769, 5),
    (1071539136, 807211838, 1015867284, 811483957, 857487113, 780, 4),
)
EVENTS = 3 * len(PLAN[0])
ROWS = 256
BLOCK = 512
INFO = 16
SLOT = 2 * BLOCK + 2 * INFO


def pick(values, index):
    result = jnp.int32(values[0])
    for at in range(1, len(values)):
        result = jnp.where(index == at, jnp.int32(values[at]), result)
    return result


def kernel(
    x_hbm, gain_ref, wqkv_hbm, wout_hbm, seg_ref, out_ref,
    xbuf, wqkv, wcol, kv, give, qrows, qmask, acc, run_max, run_sum, ogive, att,
    local_sem, x_send, x_recv, w_send, w_recv, s_send, s_recv, kv_send, kv_recv, o_send, o_recv,
):
    f32, bf16 = jnp.float32, jnp.bfloat16
    seq, head = lax.axis_index("seq"), lax.axis_index("head")
    core = lax.rem(seq, 2)
    chip = lax.div(seq, 2)
    z = lax.rem(chip, 8)
    x = lax.div(chip, 8)
    other = 1 - core

    def at(xx, zz, cc):
        return (xx * 8 + zz) * 2 + cc

    z_up, z_down = lax.rem(z + 1, 8), lax.rem(z + 7, 8)
    x_up, x_down = lax.rem(x + 1, 4), lax.rem(x + 3, 4)
    up = (at(x, z_up, core), head)
    down = (at(x, z_down, core), head)
    right = (at(x_up, z, core), head)
    left = (at(x_down, z, core), head)
    partner = (at(x, z, other), head)
    y_of = [lax.rem(head + j, 4) for j in range(4)]

    barrier = pltpu.get_barrier_semaphore()
    greeted = [up, down, right, left, partner]
    for j in range(1, 4):
        greeted.append((seq, y_of[j]))
        greeted.append((at(x, z, other), y_of[j]))
    for device in greeted:
        pl.semaphore_signal(barrier, inc=1, device_id=device, device_id_type=MESH)

    mine = pltpu.make_async_copy(x_hbm, xbuf.at[head], local_sem.at[0])
    mine.start()
    weights_in = pltpu.make_async_copy(wqkv_hbm, wqkv, local_sem.at[1])
    weights_in.start()
    columns = pl.ds(pl.multiple_of(head * ROWS, ROWS), ROWS)
    wcol_in = pltpu.make_async_copy(wout_hbm.at[:, columns], wcol.at[head], local_sem.at[2])
    wcol_in.start()

    seg = seg_ref[...]
    lane = lax.broadcasted_iota(jnp.int32, (1, HD), 1)
    sub = lax.broadcasted_iota(jnp.int32, (INFO, HD), 0)
    lower = jnp.zeros((1, HD), f32)
    upper = jnp.zeros((1, HD), f32)
    for t in range(1, 5):
        before = jnp.sum(jnp.where(seg < t, 1.0, 0.0).astype(f32), axis=1, keepdims=True)
        before = before[0:1] + before[1:2]
        lower = jnp.where(lane == t, before, lower)
        upper = jnp.where(lane == t - 1, before, upper)
    lower = jnp.where(lane < 4, lower, 0.0)
    info = jnp.where(sub == 0, lower, jnp.where(sub == 1, upper, 0.0)).astype(bf16)

    pl.semaphore_wait(barrier, len(greeted))

    x_copies = []
    for j in range(1, 4):
        copy = pltpu.make_async_remote_copy(
            src_ref=x_hbm, dst_ref=xbuf.at[head], send_sem=x_send.at[j], recv_sem=x_recv.at[head],
            device_id=(seq, y_of[j]), device_id_type=MESH)
        copy.start()
        x_copies.append(copy)
    mine.wait()
    weights_in.wait()
    wcol_in.wait()
    for j in range(1, 4):
        pltpu.make_async_remote_copy(
            src_ref=x_hbm, dst_ref=xbuf.at[y_of[j]], send_sem=x_send.at[j], recv_sem=x_recv.at[y_of[j]],
            device_id=(seq, y_of[j]), device_id_type=MESH).wait_recv()

    w_copies = []
    for j in range(1, 4):
        theirs = pl.ds(pl.multiple_of(y_of[j] * ROWS, ROWS), ROWS)
        copy = pltpu.make_async_remote_copy(
            src_ref=wout_hbm.at[:, theirs], dst_ref=wcol.at[head], send_sem=w_send.at[j],
            recv_sem=w_recv.at[head], device_id=(seq, y_of[j]), device_id_type=MESH)
        copy.start()
        w_copies.append(copy)

    squares = jnp.zeros((ROWS, 1), f32)
    for y in range(4):
        part = xbuf[y].astype(f32)
        squares = squares + jnp.sum(part * part, axis=1, keepdims=True)
    scale = lax.rsqrt(squares * (1.0 / 1024.0) + epsilon)
    normed = []
    for y in range(4):
        gain = gain_ref[:, y * ROWS : (y + 1) * ROWS]
        normed.append((xbuf[y].astype(f32) * scale * gain).astype(bf16))

    def project(which):
        total = None
        for y in range(4):
            term = jnp.dot(
                normed[y], wqkv[which, y * ROWS : (y + 1) * ROWS, :], preferred_element_type=f32)
            total = term if total is None else total + term
        return total

    own = pl.ds(pl.multiple_of(core * ROWS, ROWS), ROWS)
    own_values = pl.ds(pl.multiple_of(BLOCK + core * ROWS, ROWS), ROWS)
    own_info = pl.ds(pl.multiple_of(2 * BLOCK + core * INFO, INFO), INFO)

    def swap(j, source, target):
        return pltpu.make_async_remote_copy(
            src_ref=source, dst_ref=target, send_sem=s_send.at[j], recv_sem=s_recv.at[j],
            device_id=partner, device_id_type=MESH)

    s_copies = []
    give[3, 0:INFO, :] = info
    kv[chip, own_info, :] = info
    for j, target in ((1, kv.at[chip, own]), (2, kv.at[chip, own_values]), (0, qrows.at[own])):
        columns_of = project(j)
        if j == 0:
            columns_of = columns_of * (1.0 / math.sqrt(HD))
        columns_of = columns_of.astype(bf16)
        first, second = columns_of[:, :HD], columns_of[:, HD:]
        give[j] = jnp.where(core == 0, second, first)
        copy = swap(j, give.at[j], target)
        copy.start()
        s_copies.append(copy)
        if j == 1:
            copy = swap(3, give.at[3, 0:INFO], kv.at[chip, own_info])
            copy.start()
            s_copies.append(copy)
        target[...] = jnp.where(core == 0, first, second)
    for copy in s_copies:
        copy.wait_recv()

    mine_at = core * 8 + z
    words = [pick([row[i] for row in PLAN], mine_at) for i in range(len(PLAN[0]))]

    def event(e):
        third = lax.div(e, 3)
        word = words[0]
        for i in range(1, len(words)):
            word = jnp.where(third == i, words[i], word)
        place = lax.rem(e, 3)
        word = jnp.where(place == 0, word, jnp.where(place == 1, lax.div(word, 1024), lax.div(word, 1024 * 1024)))
        code = lax.rem(word, 1024)
        back = lax.rem(code, 4)
        source_z = lax.rem(lax.div(code, 4), 8)
        flag = [lax.rem(lax.div(code, 32 << i), 2) == 1 for i in range(5)]
        column = x - back
        valid = flag[4] & (column >= 0)
        slot = jnp.where(column >= 0, column, 0) * 8 + source_z
        return valid, slot, flag

    def hand_on(direction, slot):
        device = (up, down, right)[direction]
        return pltpu.make_async_remote_copy(
            src_ref=kv.at[slot], dst_ref=kv.at[slot], send_sem=kv_send.at[direction, slot],
            recv_sem=kv_recv.at[slot], device_id=device, device_id_type=MESH)

    def ways(flag):
        return (flag[0], flag[1], flag[2] & (x < 3))

    own_words = [pick([row[-1] for row in PLAN], mine_at)]
    own_flag = [lax.rem(lax.div(own_words[0], 1 << i), 2) == 1 for i in range(3)]
    for direction, go in enumerate(ways(own_flag)):
        @pl.when(go)
        def _(direction=direction):
            hand_on(direction, chip).start()

    row = lax.broadcasted_iota(jnp.int32, (ROWS, HD), 0).astype(f32)
    lanes = lax.broadcasted_iota(jnp.int32, (ROWS, HD), 1)

    def inside(slot, half):
        bounds = kv[slot, 2 * BLOCK + half * INFO : 2 * BLOCK + (half + 1) * INFO, :].astype(f32)
        return (row >= bounds[0:1, :]) & (row < bounds[1:2, :])

    for half in range(2):
        qmask[half * ROWS : (half + 1) * ROWS, :] = jnp.where(
            inside(chip, half) | (lanes >= 4), 0.0, masked_score).astype(bf16)

    def attend(slot, first):
        key_mask = jnp.concatenate(
            [jnp.where(inside(slot, half), 1.0, 0.0).astype(bf16) for half in range(2)], axis=0)
        keys = jnp.concatenate([kv[slot, 0:BLOCK, :], key_mask], axis=1)
        values = kv[slot, BLOCK : 2 * BLOCK, :]
        for part in range(2):
            rows = slice(part * ROWS, (part + 1) * ROWS)
            queries = jnp.concatenate([qrows[rows, :], qmask[rows, :]], axis=1)
            scores = lax.dot_general(
                queries, keys, (((1,), (1,)), ((), ())), preferred_element_type=f32)
            if first:
                q_at = lax.broadcasted_iota(jnp.int32, (ROWS, BLOCK), 0) + part * ROWS
                k_at = lax.broadcasted_iota(jnp.int32, (ROWS, BLOCK), 1)
                scores = jnp.where(k_at <= q_at, scores, masked_score)
                new_max = jnp.max(scores, axis=1, keepdims=True)
            else:
                old_max = run_max[rows, 0:1]
                new_max = jnp.maximum(old_max, jnp.max(scores, axis=1, keepdims=True))
            weights = jnp.exp(scores - new_max)
            total = jnp.sum(weights, axis=1, keepdims=True)
            product = jnp.dot(weights.astype(bf16), values, preferred_element_type=f32)
            if not first:
                factor = jnp.exp(old_max - new_max)
                total = total + run_sum[rows, 0:1] * factor
                product = product + acc[rows, :] * factor
            run_max[rows, :] = jnp.broadcast_to(new_max, (ROWS, HD))
            run_sum[rows, :] = jnp.broadcast_to(total, (ROWS, HD))
            acc[rows, :] = product

    attend(chip, True)

    def step(e, carry):
        valid, slot, flag = event(e)

        @pl.when(valid)
        def _():
            hand_on(0, slot).wait_recv()
            for direction, go in enumerate(ways(flag)):
                @pl.when(go)
                def _(direction=direction):
                    hand_on(direction, slot).start()

            @pl.when(flag[3])
            def _():
                attend(slot, False)

        return carry

    lax.fori_loop(0, EVENTS - 3, step, 0)

    for half in range(2):
        rows = slice(half * ROWS, (half + 1) * ROWS)
        ogive[half] = (acc[rows, :] / run_sum[rows, 0:1]).astype(bf16)

    o_copies = []
    lot = head * 2 + core
    for j in range(4):
        for c in range(2):
            if j == 0 and c == 0:
                continue
            row_core = core if c == 0 else other
            copy = pltpu.make_async_remote_copy(
                src_ref=ogive.at[row_core], dst_ref=att.at[lot], send_sem=o_send.at[j * 2 + c],
                recv_sem=o_recv.at[lot], device_id=(at(x, z, row_core), y_of[j]), device_id_type=MESH)
            copy.start()
            o_copies.append(copy)
    att[lot] = ogive[core]

    for j in range(1, 4):
        pltpu.make_async_remote_copy(
            src_ref=wout_hbm.at[:, columns], dst_ref=wcol.at[y_of[j]], send_sem=w_send.at[j],
            recv_sem=w_recv.at[y_of[j]], device_id=(seq, y_of[j]), device_id_type=MESH).wait_recv()
    for j in range(4):
        for c in range(2):
            if j == 0 and c == 0:
                continue
            lot_of = y_of[j] * 2 + (core if c == 0 else other)
            pltpu.make_async_remote_copy(
                src_ref=ogive.at[core], dst_ref=att.at[lot_of], send_sem=o_send.at[j * 2 + c],
                recv_sem=o_recv.at[lot_of], device_id=partner, device_id_type=MESH).wait_recv()

    total = None
    for y in range(4):
        both = jnp.concatenate([att[2 * y], att[2 * y + 1]], axis=1)
        term = jnp.dot(both, wcol[y], preferred_element_type=f32)
        total = term if total is None else total + term
    out_ref[...] = total.astype(bf16)

    for copy in x_copies + w_copies + s_copies + o_copies:
        copy.wait_send()
    for direction, go in enumerate(ways(own_flag)):
        @pl.when(go)
        def _(direction=direction):
            hand_on(direction, chip).wait_send()

    def drain(e, carry):
        valid, slot, flag = event(e)
        for direction, go in enumerate(ways(flag)):
            @pl.when(valid & go)
            def _(direction=direction):
                hand_on(direction, slot).wait_send()
        return carry

    lax.fori_loop(0, EVENTS - 3, drain, 0)


def per_device(face_rows, norm_gain, w_qkv, w_out, segments):
    bf16, f32 = jnp.bfloat16, jnp.float32
    vmem = pl.BlockSpec(memory_space=pltpu.VMEM)
    hbm = pl.BlockSpec(memory_space=pl.ANY)
    dma = pltpu.SemaphoreType.DMA
    return pl.pallas_call(
        kernel,
        name="face_attention",
        out_shape=jax.ShapeDtypeStruct((ROWS, ROWS), bf16),
        in_specs=[hbm, vmem, hbm, hbm, vmem],
        out_specs=vmem,
        scratch_shapes=[
            pltpu.VMEM((4, ROWS, ROWS), bf16),
            pltpu.VMEM((3, 1024, ROWS), bf16),
            pltpu.VMEM((4, ROWS, ROWS), bf16),
            pltpu.VMEM((32, SLOT, HD), bf16),
            pltpu.VMEM((4, ROWS, HD), bf16),
            pltpu.VMEM((BLOCK, HD), bf16),
            pltpu.VMEM((BLOCK, HD), bf16),
            pltpu.VMEM((BLOCK, HD), f32),
            pltpu.VMEM((BLOCK, HD), f32),
            pltpu.VMEM((BLOCK, HD), f32),
            pltpu.VMEM((2, ROWS, HD), bf16),
            pltpu.VMEM((8, ROWS, HD), bf16),
            dma((3,)),
            dma((4,)), dma((4,)),
            dma((4,)), dma((4,)),
            dma((4,)), dma((4,)),
            dma((3, 32)), dma((32,)),
            dma((8,)), dma((8,)),
        ],
        compiler_params=pltpu.CompilerParams(
            collective_id=0, has_side_effects=True, vmem_limit_bytes=48 * 2**20),
    )(
        face_rows,
        norm_gain.reshape(1, 1024),
        jnp.transpose(w_qkv, (1, 0, 2)),
        w_out,
        segments.reshape(2, HD),
    )


def solution(mesh):
    in_specs = (P("seq", "head"), P(), P(None, None, "head"), P("head", None), P("seq"))
    out_specs = P("seq", "head")
    return jax.shard_map(
        per_device, mesh=mesh, in_specs=in_specs, out_specs=out_specs, check_vma=False
    )
```

time: 263 us -> 94.6 us (0.36)
  Pallas kernels: 0 us -> 88.7 us
  waiting for transfers between devices: 72 us -> 0 us
  blocking collectives: 59.5 us -> 0 us
  matrix products: 46 us -> 0 us
  local copies, waits for them, and re-layouts: 39.6 us -> 5.37 us
  other arithmetic: 25.2 us -> 0 us
  between operations: 17.5 us -> 0.01 us
    pallas_call x0 -> x1, Pallas kernels: none -> 88.7 us  [per_device(): pl.pallas_call(kernel, name='face_attention', out_shape=jax.ShapeDtypeStr...]
    all_gather x2 -> x0, blocking collectives: 59.5 us -> none  [the longest x1 47.4 us: per_device(): lax.all_gather(seg_wire, 'seq', axis=1, tiled=True)]
    all_gather x1 -> x0, waiting for transfers between devices: 48.9 us -> none  [per_device(): lax.all_gather(keys_vals, 'seq', axis=1, tiled=True)]
    another operation x5 -> x0, local copies, waits for them, and re-layouts: 25.3 us -> none  [the longest x1 12.6 us: attend_piece(): value_rows = keys_vals[1].reshape(key_count, head_count, head_size)]
    dot_general x4 -> x0, matrix products: 23.9 us -> none  [the longest x2 21.3 us: update(): jnp.einsum('qhd,khd->hqk', group_queries, key_rows, preferred_element_typ...]
    reduce_scatter x1 -> x0, waiting for transfers between devices: 23.1 us -> none  [per_device(): lax.psum_scatter(partial_sums, 'head', scatter_dimension=1, tiled=True)]
    cond x2 -> x0, matrix products: 22.1 us -> none  [attend_piece(): updated.append(lax.cond(needed, update, lambda current: current, state))]
    reduce_sum x3 -> x0, other arithmetic: 16.2 us -> none  [the longest x2 16 us: update(): new_total = jnp.sum(weights, axis=2)]
  transfers between devices with their start and end apart: 2 -> 0, of which waited for: 2 -> 0; matrix products, arithmetic and copies ran while one was open for 1% -> 0% of each run, Pallas kernels for 0% -> 0%
where the time goes in v1:
time: 94.6 us; the launch traced here: 94.1 us
  Pallas kernels  88.7 us (94%)
  local copies, waits for them, and re-layouts  5.37 us (6%)
    pallas_call x1, Pallas kernels, per_device(): pl.pallas_call(kernel, name='face_attention', out_shape=jax.ShapeDtypeStr...  88.7 us
    unnamed x11, local copies, waits for them, and re-layouts  5.37 us

profile of v1, /device:TPU:5, one launch (start us, length us, event | category | flops | bytes accessed | tf_op | source)
XLA Modules:
  0.0 94.1 jit_solution(4337478558047568708)
XLA Ops:
  0.0 0.0 copy-start
  0.0 1.4 %copy-done = bf16[1024,3,256]{2,0,1:T(8,128)(2,1)S(1)} copy-done((bf16[1024,3,256]{2,0,1:T(8,128)(2,1)S(1)}, bf16[1024,3,256]{2,0,1:T(8,128)(2,1)}, u32[]{:S(2)}) %copy-start) | copy-done | bytes 1572888
  1.4 0.0 copy-start.1
  1.4 1.0 %copy-done.1 = bf16[256,1024]{1,0:T(8,128)(2,1)S(1)} copy-done((bf16[256,1024]{1,0:T(8,128)(2,1)S(1)}, bf16[256,1024]{1,0:T(8,128)(2,1)}, u32[]{:S(2)}) %copy-start.1) | copy-done | bytes 524312
  2.5 0.0 copy-start.2
  2.5 0.9 copy-done.2
  3.4 0.0 copy-start.3
  3.4 0.7 copy-done.3
  4.0 0.0 copy-start.4
  4.0 0.7 copy-done.4
  4.7 88.7 %face_attention.1 = bf16[256,256]{1,0:T(8,128)(2,1)S(1)} custom-call(bf16[256,256]{1,0:T(8,128)(2,1)S(1)} %copy-done.2, f32[1,1024]{1,0:T(1,128)S(1)} %bitcast.4, bf16[3,1024,256]{2,1,0:T(8,128)(2,1)S(1)} %bitcast.3, bf16[256,1024]{1,0:T(8,128)(2,1)S(1)} %copy-done.1, s32[2,128]{1,0:T(2,128)S(1)} %bitcast.5), custom_call_target="tpu_custom_call" | custom-call | tf_op jit(solution)/shard_map/face_attention/pallas_call | solution.py:332
  93.4 0.7 copy.7
Async XLA Ops:
  0.0 1.4 %copy-start = (bf16[1024,3,256]{2,0,1:T(8,128)(2,1)S(1)}, bf16[1024,3,256]{2,0,1:T(8,128)(2,1)}, u32[]{:S(2)}) copy-start(bf16[1024,3,256]{2,0,1:T(8,128)(2,1)} %param.7) | copy-start | bytes 4718596
  1.4 1.0 %copy-start.1 = (bf16[256,1024]{1,0:T(8,128)(2,1)S(1)}, bf16[256,1024]{1,0:T(8,128)(2,1)}, u32[]{:S(2)}) copy-start(bf16[256,1024]{1,0:T(8,128)(2,1)} %wout_hbm.1) | copy-start | bytes 1572868
  2.5 0.9 copy-start.2
  3.4 0.7 copy-start.3
  4.0 0.7 copy-start.4

commit v2 on v1

--- a/solution.py
+++ b/solution.py
@@ -13,24 +13,72 @@
 epsilon = 1e-05
 masked_score = -1e30
 PLAN = (
-    (870258657, 812574466, 850160585, 871119793, 829180757, 541631245, 7),
-    (882874144, 870062881, 887908237, 896281557, 824998833, 533274, 5),
-    (1021257508, 839658277, 820774869, 829180829, 900496153, 785, 5),
-    (958347176, 815545124, 839685973, 829384530, 837711706, 769, 5),
-    (895436588, 1033653160, 849173284, 806319877, 871118618, 833, 5),
-    (1033852720, 866999212, 940390237, 907842344, 811345681, 798, 5),
-    (1037952948, 873224112, 891091756, 848107290, 807179017, 781, 5),
-    (937190208, 827123457, 857621317, 952957769, 828154733, 804, 4),
-    (613287492, 1012665149, 815536926, 828323769, 854354698, 829180817, 7),
-    (1012826696, 840702921, 883767229, 1000143633, 896297877, 801554, 7),
-    (1021257636, 839730954, 854546213, 829224737, 832338770, 794, 7),
-    (1025324968, 1029449508, 839732005, 820930358, 970812161, 798, 5),
-    (895469484, 819743656, 849307396, 836528901, 837606272, 769, 5),
-    (1033721648, 867087121, 819733469, 944601984, 811345697, 790, 5),
-    (990734260, 873428757, 824095684, 811475742, 815544090, 769, 5),
-    (1071539136, 807211838, 1015867284, 811483957, 857487113, 780, 4),
+    (198721, 0, 0, 0, 0, 0, 7),
+    (557122, 0, 0, 0, 0, 0, 7),
+    (557601, 0, 0, 0, 0, 0, 7),
+    (705332898, 0, 0, 0, 0, 0, 5),
+    (707300485, 524801, 0, 0, 0, 0, 5),
+    (671780516, 525826, 0, 0, 0, 0, 7),
+    (604541605, 673877569, 0, 0, 0, 0, 5),
+    (739777088, 541657733, 643, 0, 0, 0, 4),
+    (772316233, 711591114, 710414018, 644, 0, 0, 7),
+    (579503178, 571083431, 676860611, 550, 0, 0, 7),
+    (607849001, 544776705, 542839296, 518, 0, 0, 7),
+    (714779331, 572136132, 713627138, 524935, 0, 0, 5),
+    (608742541, 609950378, 546867911, 537429507, 520, 0, 5),
+    (575280812, 612019910, 546843272, 539591235, 513, 0, 7),
+    (746239718, 542712364, 538481225, 540682923, 526848, 0, 5),
+    (552149735, 639146697, 576337408, 575156810, 539496075, 0, 4),
+    (780713041, 719987922, 548931274, 537434797, 540684802, 541597189, 7),
+    (587899986, 579480239, 607690443, 538456578, 543734413, 529924, 7),
+    (616245809, 587729417, 545787407, 544749260, 543692356, 526, 7),
+    (723176139, 686502467, 618146345, 609927716, 545856143, 519, 5),
+    (617139349, 618347186, 581647941, 548936209, 578294313, 541192, 5),
+    (583677620, 620416718, 688396869, 616056338, 546843240, 519, 7),
+    (754636526, 621335046, 622343687, 725100076, 545795730, 522, 5),
+    (578372335, 585844246, 693641833, 558451245, 549080620, 522, 4),
+    (654892121, 594035802, 557327954, 545831477, 548950538, 549993997, 3),
+    (596165722, 587745847, 616087123, 546853386, 552131093, 538124, 3),
+    (624511545, 596126225, 554184215, 553145940, 552089164, 534, 3),
+    (597224019, 560550475, 626543153, 618193452, 554252823, 527, 1),
+    (598299195, 618223190, 563661399, 588795406, 554221068, 536, 1),
+    (591943228, 628682326, 562575949, 624453146, 555240048, 527, 1),
+    (628684406, 629731854, 630740495, 599279156, 554192410, 530, 1),
+    (586769015, 594109982, 567820913, 566848053, 557346356, 530, 0),
+    (135, 0, 0, 0, 0, 0, 7),
+    (672, 0, 0, 0, 0, 0, 5),
+    (688673, 0, 0, 0, 0, 0, 5),
+    (571115170, 0, 0, 0, 0, 0, 5),
+    (706382499, 672, 0, 0, 0, 0, 5),
+    (707431972, 524961, 0, 0, 0, 0, 5),
+    (709362213, 574261383, 673, 0, 0, 0, 5),
+    (676993600, 540674692, 513, 0, 0, 0, 3),
+    (739836047, 539663079, 541658629, 0, 0, 0, 7),
+    (740886184, 711594563, 542769703, 0, 0, 0, 5),
+    (713598658, 571151043, 538614469, 551, 0, 0, 5),
+    (608767658, 579409577, 537462274, 531974, 0, 0, 5),
+    (744140356, 714608298, 713693698, 537396743, 0, 0, 5),
+    (716747333, 574167722, 537599657, 545785346, 516, 0, 5),
+    (717759021, 612046991, 582658624, 714674693, 538446339, 0, 5),
+    (577387080, 538588736, 682242789, 548966919, 539502083, 0, 3),
+    (748232855, 572177135, 551132682, 543692363, 541592067, 524812, 7),
+    (749282992, 684264011, 538492590, 578429507, 67703309, 529926, 5),
+    (539543242, 751513264, 575245864, 547011277, 578338373, 518, 5),
+    (617164466, 587806385, 545859082, 552078853, 553130532, 519, 5),
+    (752537164, 643313330, 686303921, 553196208, 544743945, 516, 5),
+    (725144141, 582564530, 754632197, 546843144, 645405200, 524, 5),
+    (726155829, 620443799, 591055432, 617159181, 547892913, 531977, 5),
+    (585783888, 546985544, 39473901, 583548562, 555232787, 535047, 3),
+    (662259280, 556312118, 624449135, 548944397, 558379530, 520, 3),
+    (623461944, 558443091, 546889270, 586695243, 76100117, 538126, 1),
+    (547939922, 625561144, 583642672, 555276885, 586735181, 526, 1),
+    (625561146, 596203065, 554255890, 560475661, 561527340, 527, 1),
+    (626585172, 651710010, 560482873, 561592888, 553140753, 524, 1),
+    (599323221, 590961210, 628680205, 555239952, 653802008, 532, 1),
+    (600334909, 621370966, 559476282, 597250638, 555239955, 527, 1),
+    (594049624, 555251280, 47739509, 591945242, 563629595, 543247, 0),
 )
-EVENTS = 3 * len(PLAN[0])
+EVENTS = 3 * (len(PLAN[0]) - 1)
 ROWS = 256
 BLOCK = 512
 INFO = 16
@@ -98,6 +146,8 @@
     lower = jnp.where(lane < 4, lower, 0.0)
     info = jnp.where(sub == 0, lower, jnp.where(sub == 1, upper, 0.0)).astype(bf16)
 
+    mine_at = core * 32 + chip
+    words = [pick([row[i] for row in PLAN], mine_at) for i in range(len(PLAN[0]))]
     pl.semaphore_wait(barrier, len(greeted))
 
     x_copies = []
@@ -172,38 +222,27 @@
     for copy in s_copies:
         copy.wait_recv()
 
-    mine_at = core * 8 + z
-    words = [pick([row[i] for row in PLAN], mine_at) for i in range(len(PLAN[0]))]
-
     def event(e):
         third = lax.div(e, 3)
         word = words[0]
-        for i in range(1, len(words)):
+        for i in range(1, len(words) - 1):
             word = jnp.where(third == i, words[i], word)
         place = lax.rem(e, 3)
         word = jnp.where(place == 0, word, jnp.where(place == 1, lax.div(word, 1024), lax.div(word, 1024 * 1024)))
         code = lax.rem(word, 1024)
-        back = lax.rem(code, 4)
-        source_z = lax.rem(lax.div(code, 4), 8)
+        slot = lax.rem(code, 32)
         flag = [lax.rem(lax.div(code, 32 << i), 2) == 1 for i in range(5)]
-        column = x - back
-        valid = flag[4] & (column >= 0)
-        slot = jnp.where(column >= 0, column, 0) * 8 + source_z
-        return valid, slot, flag
+        return code >= 32, slot, flag
 
     def hand_on(direction, slot):
-        device = (up, down, right)[direction]
+        device = (up, down, right, left)[direction]
         return pltpu.make_async_remote_copy(
             src_ref=kv.at[slot], dst_ref=kv.at[slot], send_sem=kv_send.at[direction, slot],
             recv_sem=kv_recv.at[slot], device_id=device, device_id_type=MESH)
 
-    def ways(flag):
-        return (flag[0], flag[1], flag[2] & (x < 3))
-
-    own_words = [pick([row[-1] for row in PLAN], mine_at)]
-    own_flag = [lax.rem(lax.div(own_words[0], 1 << i), 2) == 1 for i in range(3)]
-    for direction, go in enumerate(ways(own_flag)):
-        @pl.when(go)
+    own_flag = [lax.rem(lax.div(words[-1], 1 << i), 2) == 1 for i in range(4)]
+    for direction in range(4):
+        @pl.when(own_flag[direction])
         def _(direction=direction):
             hand_on(direction, chip).start()
 
@@ -255,18 +294,18 @@
         @pl.when(valid)
         def _():
             hand_on(0, slot).wait_recv()
-            for direction, go in enumerate(ways(flag)):
-                @pl.when(go)
+            for direction in range(4):
+                @pl.when(flag[direction])
                 def _(direction=direction):
                     hand_on(direction, slot).start()
 
-            @pl.when(flag[3])
+            @pl.when(flag[4])
             def _():
                 attend(slot, False)
 
         return carry
 
-    lax.fori_loop(0, EVENTS - 3, step, 0)
+    lax.fori_loop(0, EVENTS, step, 0)
 
     for half in range(2):
         rows = slice(half * ROWS, (half + 1) * ROWS)
@@ -286,6 +325,23 @@
             o_copies.append(copy)
     att[lot] = ogive[core]
 
+    for direction in range(4):
+        @pl.when(own_flag[direction])
+        def _(direction=direction):
+            hand_on(direction, chip).wait_send()
+
+    def drain(e, carry):
+        valid, slot, flag = event(e)
+        for direction in range(4):
+            @pl.when(flag[direction])
+            def _(direction=direction):
+                hand_on(direction, slot).wait_send()
+        return carry
+
+    lax.fori_loop(0, EVENTS, drain, 0)
+    for copy in x_copies + w_copies + s_copies:
+        copy.wait_send()
+
     for j in range(1, 4):
         pltpu.make_async_remote_copy(
             src_ref=wout_hbm.at[:, columns], dst_ref=wcol.at[y_of[j]], send_sem=w_send.at[j],
@@ -306,22 +362,8 @@
         total = term if total is None else total + term
     out_ref[...] = total.astype(bf16)
 
-    for copy in x_copies + w_copies + s_copies + o_copies:
+    for copy in o_copies:
         copy.wait_send()
-    for direction, go in enumerate(ways(own_flag)):
-        @pl.when(go)
-        def _(direction=direction):
-            hand_on(direction, chip).wait_send()
-
-    def drain(e, carry):
-        valid, slot, flag = event(e)
-        for direction, go in enumerate(ways(flag)):
-            @pl.when(valid & go)
-            def _(direction=direction):
-                hand_on(direction, slot).wait_send()
-        return carry
-
-    lax.fori_loop(0, EVENTS - 3, drain, 0)
 
 
 def per_device(face_rows, norm_gain, w_qkv, w_out, segments):
@@ -352,11 +394,11 @@
             dma((4,)), dma((4,)),
             dma((4,)), dma((4,)),
             dma((4,)), dma((4,)),
-            dma((3, 32)), dma((32,)),
+            dma((4, 32)), dma((32,)),
             dma((8,)), dma((8,)),
         ],
         compiler_params=pltpu.CompilerParams(
-            collective_id=0, has_side_effects=True, vmem_limit_bytes=48 * 2**20),
+            collective_id=0, has_side_effects=True, vmem_limit_bytes=67043328),
     )(
         face_rows,
         norm_gain.reshape(1, 1024),

time: 94.6 us -> 78.2 us (0.83)
  Pallas kernels: 88.7 us -> 75.6 us
  local copies, waits for them, and re-layouts: 5.37 us -> 1.57 us
    pallas_call x1, Pallas kernels: 88.7 us -> 75.6 us  [per_device(): pl.pallas_call(kernel, name='face_attention', out_shape=jax.ShapeDtypeStr...]
    unnamed x11 -> x1, local copies, waits for them, and re-layouts: 5.37 us -> 1.57 us
where the time goes in v2:
time: 78.2 us; the launch traced here: 77.1 us
  Pallas kernels  75.6 us (97%)
  local copies, waits for them, and re-layouts  1.57 us (2%)
    pallas_call x1, Pallas kernels, per_device(): pl.pallas_call(kernel, name='face_attention', out_shape=jax.ShapeDtypeStr...  75.6 us
    unnamed x1, local copies, waits for them, and re-layouts  1.57 us

profile of v2, /device:TPU:5, one launch (start us, length us, event | category | flops | bytes accessed | tf_op | source)
XLA Modules:
  0.0 77.1 jit_solution(8649259644578832650)
XLA Ops:
  0.0 75.6 %face_attention.1 = bf16[256,256]{1,0:T(8,128)(2,1)} custom-call(bf16[256,256]{1,0:T(8,128)(2,1)} %x_hbm.1, f32[1,1024]{1,0:T(1,128)} %bitcast.4, bf16[3,1024,256]{2,1,0:T(8,128)(2,1)} %bitcast.3, bf16[256,1024]{1,0:T(8,128)(2,1)} %wout_hbm.1, s32[2,128]{1,0:T(2,128)} %bitcast.5), custom_call_target="tpu_custom_call" | custom-call | tf_op jit(solution)/shard_map/face_attention/pallas_call | solution.py:374
  75.6 1.6 %copy.7 = bf16[256,256]{1,0:T(8,128)(2,1)} copy(bf16[256,256]{1,0:T(8,128)(2,1)} %face_attention.1) | data formatting | bytes 262144

commit v3 on v1

v3 whole, which is shorter than its diff:
```python
import functools
import math

import jax
import jax.numpy as jnp
from jax import lax
from jax.experimental import pallas as pl
from jax.experimental.pallas import tpu as pltpu
from jax.sharding import PartitionSpec as P

MESH = pl.DeviceIdType.MESH
HD = 128
epsilon = 1e-05
masked_score = -1e30
PLAN = (
    (1131137, 734113, 1075723, 683, 0, 0, 0, 0, 0, 0, 0, 0, 0, 0, 0, 0, 0, 0, 0, 103),
    (1134656, 1073803, 2294054, 2731, 2049, 2049, 2049, 2049, 2049, 2049, 2049, 2049, 2049, 2049, 2049, 2049, 2049, 2049, 2049, 255),
    (657962, 2820747, 131755, 2163340, 4098, 4098, 4098, 4098, 4098, 4098, 4098, 4098, 4098, 4098, 4098, 4098, 4098, 4098, 4098, 221),
    (660107, 2298539, 600204, 2296129, 2162688, 6147, 6147, 6147, 6147, 6147, 6147, 6147, 6147, 6147, 6147, 6147, 6147, 6147, 6147, 85),
    (137868, 2824613, 2822466, 2689281, 2949120, 8196, 8196, 8196, 8196, 8196, 8196, 8196, 8196, 8196, 8196, 8196, 8196, 8196, 8196, 93),
    (2826564, 2300227, 786727, 2424898, 3426, 11297, 10245, 10245, 10245, 10245, 10245, 10245, 10245, 10245, 10245, 10245, 10245, 10245, 10245, 188),
    (731559, 664111, 1091712, 2303392, 265285, 2824259, 660641, 13346, 12294, 12294, 12294, 12294, 12294, 12294, 12294, 12294, 12294, 12294, 12294, 85),
    (786694, 2425391, 265574, 2427173, 8269, 2108708, 530731, 2168834, 15394, 14343, 14343, 14343, 14343, 14343, 14343, 14343, 14343, 14343, 14343, 228),
    (280640, 611808, 346183, 2308257, 2175302, 858242, 667042, 2103556, 2171905, 17445, 16392, 16392, 16392, 16392, 16392, 16392, 16392, 16392, 16392, 246),
    (2730, 2164840, 655490, 2246240, 7586, 2308423, 734371, 2240772, 601124, 19461, 18441, 18441, 18441, 18441, 18441, 18441, 18441, 18441, 18441, 119),
    (266569, 2430057, 2435, 2431272, 2295872, 795744, 2958344, 862279, 603239, 2110469, 20490, 20490, 20490, 20490, 20490, 20490, 20490, 20490, 20490, 245),
    (268362, 2839971, 270338, 2312521, 339108, 3205, 536576, 2167841, 2164006, 16647, 2180391, 22539, 22539, 22539, 22539, 22539, 22539, 22539, 22539, 153),
    (270667, 2958635, 2697605, 2314570, 798819, 2428994, 216486, 133383, 2297097, 279555, 66855, 2098472, 24588, 24588, 24588, 24588, 24588, 24588, 24588, 93),
    (680133, 9324, 153990, 2172070, 801829, 675971, 2963592, 19491, 2707584, 2966560, 2101346, 2181121, 2165803, 26637, 26637, 26637, 26637, 26637, 26637, 85),
    (158086, 2189871, 1093030, 1190279, 2178085, 680328, 2441284, 805932, 2181280, 2097483, 20515, 4129, 2167844, 2184193, 2186243, 28686, 28686, 28686, 28686, 69),
    (553415, 2441608, 1600615, 804934, 263337, 207904, 25669, 4164, 546977, 2190820, 21697, 400554, 3216430, 2188323, 2176043, 30735, 30735, 30735, 30735, 228),
    (821576, 228584, 870833, 873807, 212106, 749600, 143489, 2164738, 7502, 747691, 2640995, 2167819, 2124076, 205964, 2106368, 2176007, 2172933, 32784, 32784, 119),
    (2326608, 807401, 1196338, 687497, 2848898, 2183201, 212008, 2243585, 284803, 24942, 2782636, 262150, 2438178, 337924, 2123821, 2169861, 2171947, 34833, 34833, 119),
    (690314, 267306, 19825, 689186, 2313520, 286731, 147651, 2974824, 2168900, 556075, 2324749, 80996, 2111525, 2369838, 2713638, 2110478, 36882, 36882, 36882, 117),
    (811122, 2266540, 2787697, 217251, 557453, 553065, 272395, 2452489, 274984, 2245642, 621611, 2128934, 9219, 2171950, 80944, 2112549, 38931, 38931, 38931, 85),
    (287059, 3104772, 814451, 22926, 2316402, 2171950, 818349, 273746, 557105, 2788517, 2719882, 13354, 2194470, 14377, 2178121, 2179080, 40980, 40980, 40980, 85),
    (565645, 2977934, 1125869, 818548, 295251, 2332780, 2982002, 2456581, 14374, 1268775, 2265096, 35852, 2722822, 21515, 2180138, 2181129, 43029, 43029, 43029, 85),
    (815383, 3109461, 818549, 223376, 239024, 341167, 24615, 2318675, 2112518, 559240, 2858417, 2443273, 284714, 103437, 2139146, 2180651, 46098, 45078, 45078, 85),
    (948502, 2324880, 2732103, 1275312, 2570517, 344209, 2114869, 1397838, 347569, 2386541, 2117514, 1050932, 37139, 204811, 2200108, 2186291, 2122772, 47127, 47127, 70),
    (313424, 1050809, 2340951, 1116305, 177201, 30866, 86057, 2194610, 2326536, 1136819, 1207414, 95272, 2137099, 2126348, 40981, 2118765, 2206772, 2188297, 49176, 51),
    (180737, 300152, 84513, 1071658, 367794, 2398295, 2248753, 3233940, 287863, 2203734, 2115695, 94224, 1076342, 2467861, 2196524, 2128913, 2190350, 51225, 51225, 51),
    (430594, 1118297, 2331769, 34858, 1071251, 2463832, 3234936, 304177, 2465804, 305264, 30743, 2130988, 2468874, 2340877, 28694, 2208815, 2190382, 53274, 53274, 17),
    (301146, 304307, 2347531, 38443, 25780, 2187413, 34905, 2468985, 46194, 27761, 181302, 32910, 3241080, 48688, 31863, 2190383, 55323, 55323, 55323, 17),
    (303620, 2349147, 40116, 184469, 2468979, 307244, 2348214, 116910, 354455, 168079, 101490, 2126861, 2280460, 2131984, 2146360, 2196527, 58423, 57372, 57372, 17),
    (188933, 1124501, 2468988, 186518, 2469901, 172056, 357499, 2211930, 310445, 105588, 31758, 2456698, 117779, 34864, 2129938, 2210866, 2198553, 59421, 59421, 17),
    (307293, 2354358, 188568, 310456, 2351246, 2192047, 186421, 2140185, 2129081, 99451, 1220698, 296979, 2473104, 2198580, 2201618, 2348082, 61470, 61470, 61470, 17),
    (178328, 1128478, 2604216, 177214, 59545, 2222191, 2477071, 294940, 2338833, 56380, 2196114, 3510357, 2219061, 2197555, 151578, 3186804, 2216979, 63519, 63519, 0),
    (854568, 1132673, 266402, 1135366, 65568, 65568, 65568, 65568, 65568, 65568, 65568, 65568, 65568, 65568, 65568, 65568, 65568, 65568, 65568, 247),
    (1133474, 197129, 2752642, 1397027, 68364, 67617, 67617, 67617, 67617, 67617, 67617, 67617, 67617, 67617, 67617, 67617, 67617, 67617, 67617, 127),
    (334378, 2754913, 2228576, 1077900, 69666, 69666, 69666, 69666, 69666, 69666, 69666, 69666, 69666, 69666, 69666, 69666, 69666, 69666, 69666, 119),
    (725515, 1649986, 199181, 66188, 2622094, 72769, 71715, 71715, 71715, 71715, 71715, 71715, 71715, 71715, 71715, 71715, 71715, 71715, 71715, 223),
    (727205, 2759180, 1143437, 2232674, 199310, 2230304, 75008, 73764, 73764, 73764, 73764, 73764, 73764, 73764, 73764, 73764, 73764, 73764, 73764, 85),
    (1337700, 2237102, 727182, 853059, 2101602, 68992, 77121, 75813, 75813, 75813, 75813, 75813, 75813, 75813, 75813, 75813, 75813, 75813, 75813, 87),
    (731687, 1340078, 328773, 1079396, 2884932, 2759011, 528417, 2624802, 77862, 77862, 77862, 77862, 77862, 77862, 77862, 77862, 77862, 77862, 77862, 92),
    (1341856, 2883654, 330021, 2624517, 69668, 2888742, 597252, 80899, 79911, 79911, 79911, 79911, 79911, 79911, 79911, 79911, 79911, 79911, 79911, 70),
    (1919328, 735393, 281927, 857345, 348230, 2831360, 732162, 532618, 2696453, 2103331, 81960, 81960, 81960, 81960, 81960, 81960, 81960, 81960, 81960, 123),
    (738218, 2244641, 66945, 2097314, 2887843, 2242663, 337027, 548934, 77158, 2632836, 84009, 84009, 84009, 84009, 84009, 84009, 84009, 84009, 84009, 191),
    (739618, 2364681, 213283, 2244705, 2366529, 604324, 2367584, 601415, 668805, 2176000, 86058, 86058, 86058, 86058, 86058, 86058, 86058, 86058, 86058, 91),
    (1073315, 2365802, 740682, 135588, 2168196, 2893989, 2408, 262182, 2296840, 2294023, 2110537, 89127, 88107, 88107, 88107, 88107, 88107, 88107, 88107, 213),
    (219437, 2498980, 601163, 217123, 2235525, 865610, 84002, 2233350, 342312, 97, 2163719, 2640904, 91137, 90156, 90156, 90156, 90156, 90156, 90156, 245),
    (862510, 3025260, 2253103, 340068, 2105707, 2776454, 606243, 151591, 2103392, 69929, 2898944, 2315266, 2117000, 2164865, 92205, 92205, 92205, 92205, 92205, 147),
    (471471, 3027309, 2779560, 108, 870437, 2238564, 2177415, 2254216, 2902123, 69699, 2250785, 87075, 2100234, 2163716, 95234, 94254, 94254, 94254, 94254, 155),
    (868455, 3029294, 66574, 346413, 2097766, 208141, 331144, 2378753, 528684, 87074, 2105380, 2118725, 2110476, 88099, 2104331, 96303, 96303, 96303, 96303, 134),
    (671921, 65809, 752640, 2179241, 67687, 1856583, 547118, 144385, 70827, 2176170, 2129033, 747621, 71724, 2782477, 2102275, 2107396, 2171916, 98352, 98352, 99),
    (330096, 2183306, 809064, 2448456, 2130057, 876583, 135535, 2365603, 2167809, 74764, 2259975, 92198, 76841, 95236, 2126853, 2110477, 100401, 100401, 100401, 119),
    (807025, 2787499, 71051, 2183536, 2246697, 82348, 2365603, 2131016, 751661, 335911, 881676, 2368514, 11271, 2126885, 2385926, 2176015, 102450, 102450, 102450, 85),
    (758187, 2790603, 876579, 217201, 2264195, 2121833, 878896, 2117796, 2498734, 2173061, 2244648, 3164199, 621581, 341008, 2110535, 2128910, 104499, 104499, 104499, 85),
    (759980, 2516243, 758189, 357714, 624746, 88743, 96292, 2250065, 85003, 2123920, 2371750, 76942, 83248, 2391045, 2114564, 2112521, 106548, 106548, 106548, 85),
    (2793844, 77998, 90149, 26995, 1391692, 758917, 819631, 2265195, 2651270, 2250794, 2268592, 2914344, 2189649, 2112522, 2114609, 2181129, 108597, 108597, 108597, 85),
    (174246, 1522997, 2109812, 2793616, 2519086, 761008, 292877, 2111858, 16460, 625938, 2189387, 2193545, 21544, 2182186, 2186284, 2137105, 110646, 110646, 110646, 84),
    (885103, 2392342, 886824, 225301, 79913, 2111796, 2128950, 224532, 2257997, 2205834, 105480, 2132140, 135211, 103594, 2253833, 2120722, 113683, 112695, 112695, 68),
    (1048761, 1130704, 243865, 2113722, 298071, 96297, 1061897, 241842, 3308074, 367762, 2143242, 2195467, 109715, 2271342, 107569, 224299, 91156, 2122765, 115726, 51),
    (245946, 1116273, 1119320, 99345, 364585, 3311241, 2396339, 243754, 23639, 2399242, 1210486, 2447532, 2194572, 108596, 2125870, 27669, 2143277, 117780, 116793, 51),
    (364665, 2396714, 367705, 2379889, 181395, 2264184, 1212587, 2119735, 1073332, 2401328, 371756, 2275982, 97301, 2192013, 2190415, 2404406, 118842, 118842, 118842, 19),
    (367139, 1054842, 2399322, 368875, 102521, 2401291, 1125394, 371801, 1337452, 2122901, 94257, 49206, 99342, 2452536, 2132023, 2405392, 97303, 121935, 120891, 17),
    (252084, 2284692, 370700, 249907, 1076314, 2268309, 356907, 116918, 2280557, 103950, 375852, 2405458, 2132081, 114735, 33815, 2147376, 123919, 122940, 122940, 17),
    (370812, 2534492, 373261, 106619, 2283566, 118967, 2281523, 3316886, 377007, 102425, 3239063, 2134577, 2214096, 2127000, 2128944, 2133012, 124989, 124989, 124989, 17),
    (256550, 1128694, 254478, 376366, 240790, 377359, 2407509, 41083, 379996, 105524, 2194584, 119899, 2288730, 102448, 2137106, 35865, 2130993, 127038, 127038, 17),
    (127223, 378071, 2408623, 2158777, 3308150, 32829, 2274544, 2410682, 123509, 2271889, 2328626, 2269300, 3183644, 1087547, 2202651, 2157594, 129087, 129087, 129087, 0),
)
EVENTS = 2 * (len(PLAN[0]) - 1)
ROWS = 256
BLOCK = 512
INFO = 16
SLOT = 2 * ROWS + INFO


def pick(values, index):
    result = jnp.int32(values[0])
    for at in range(1, len(values)):
        result = jnp.where(index == at, jnp.int32(values[at]), result)
    return result


def kernel(
    x_hbm, gain_hbm, wqkv_hbm, wout_hbm, seg_hbm, out_ref,
    xbuf, gain_ref, wqkv, wcol, seg_ref, kv, give, qgive, qrows, qmask, acc, run_max, run_sum, ogive, att,
    local_sem, x_send, x_recv, w_send, w_recv, s_send, s_recv, kv_send, kv_recv, o_send, o_recv,
):
    f32, bf16 = jnp.float32, jnp.bfloat16
    seq, head = lax.axis_index("seq"), lax.axis_index("head")
    core = lax.rem(seq, 2)
    chip = lax.div(seq, 2)
    z = lax.rem(chip, 8)
    x = lax.div(chip, 8)
    other = 1 - core

    def at(xx, zz, cc):
        return (xx * 8 + zz) * 2 + cc

    z_up, z_down = lax.rem(z + 1, 8), lax.rem(z + 7, 8)
    x_up, x_down = lax.rem(x + 1, 4), lax.rem(x + 3, 4)
    up = (at(x, z_up, core), head)
    down = (at(x, z_down, core), head)
    right = (at(x_up, z, core), head)
    left = (at(x_down, z, core), head)
    partner = (at(x, z, other), head)
    y_of = [lax.rem(head + j, 4) for j in range(4)]

    barrier = pltpu.get_barrier_semaphore()
    greeted = [up, down, right, left, partner]
    for j in range(1, 4):
        greeted.append((seq, y_of[j]))
        greeted.append((at(x, z, other), y_of[j]))
    for device in greeted:
        pl.semaphore_signal(barrier, inc=1, device_id=device, device_id_type=MESH)

    seg_in = pltpu.make_async_copy(seg_hbm, seg_ref, local_sem.at[3])
    seg_in.start()
    gain_in = pltpu.make_async_copy(gain_hbm, gain_ref, local_sem.at[4])
    gain_in.start()
    mine = pltpu.make_async_copy(x_hbm, xbuf.at[head], local_sem.at[0])
    mine.start()
    weights_in = pltpu.make_async_copy(wqkv_hbm, wqkv, local_sem.at[1])
    weights_in.start()
    columns = pl.ds(pl.multiple_of(head * ROWS, ROWS), ROWS)
    wcol_in = pltpu.make_async_copy(wout_hbm.at[:, columns], wcol.at[head], local_sem.at[2])
    wcol_in.start()

    seg_in.wait()
    seg = seg_ref[...]
    lane = lax.broadcasted_iota(jnp.int32, (1, HD), 1)
    sub = lax.broadcasted_iota(jnp.int32, (INFO, HD), 0)
    lower = jnp.zeros((1, HD), f32)
    upper = jnp.zeros((1, HD), f32)
    for t in range(1, 5):
        before = jnp.sum(jnp.where(seg < t, 1.0, 0.0).astype(f32), axis=1, keepdims=True)
        before = before[0:1] + before[1:2]
        lower = jnp.where(lane == t, before, lower)
        upper = jnp.where(lane == t - 1, before, upper)
    lower = jnp.where(lane < 4, lower, 0.0)
    info = jnp.where(sub == 0, lower, jnp.where(sub == 1, upper, 0.0)).astype(bf16)

    mine_at = core * 32 + chip
    words = [pick([row[i] for row in PLAN], mine_at) for i in range(len(PLAN[0]))]
    pl.semaphore_wait(barrier, len(greeted))

    x_copies = []
    for j in range(1, 4):
        copy = pltpu.make_async_remote_copy(
            src_ref=x_hbm, dst_ref=xbuf.at[head], send_sem=x_send.at[j], recv_sem=x_recv.at[head],
            device_id=(seq, y_of[j]), device_id_type=MESH)
        copy.start()
        x_copies.append(copy)
    gain_in.wait()
    mine.wait()
    weights_in.wait()
    wcol_in.wait()
    for j in range(1, 4):
        pltpu.make_async_remote_copy(
            src_ref=x_hbm, dst_ref=xbuf.at[y_of[j]], send_sem=x_send.at[j], recv_sem=x_recv.at[y_of[j]],
            device_id=(seq, y_of[j]), device_id_type=MESH).wait_recv()

    w_copies = []
    for j in range(1, 4):
        theirs = pl.ds(pl.multiple_of(y_of[j] * ROWS, ROWS), ROWS)
        copy = pltpu.make_async_remote_copy(
            src_ref=wout_hbm.at[:, theirs], dst_ref=wcol.at[head], send_sem=w_send.at[j],
            recv_sem=w_recv.at[head], device_id=(seq, y_of[j]), device_id_type=MESH)
        copy.start()
        w_copies.append(copy)

    squares = jnp.zeros((ROWS, 1), f32)
    for y in range(4):
        part = xbuf[y].astype(f32)
        squares = squares + jnp.sum(part * part, axis=1, keepdims=True)
    scale = lax.rsqrt(squares * (1.0 / 1024.0) + epsilon)
    normed = []
    for y in range(4):
        gain = gain_ref[:, y * ROWS : (y + 1) * ROWS]
        normed.append((xbuf[y].astype(f32) * scale * gain).astype(bf16))

    def project(which):
        total = None
        for y in range(4):
            term = jnp.dot(
                normed[y], wqkv[which, y * ROWS : (y + 1) * ROWS, :], preferred_element_type=f32)
            total = term if total is None else total + term
        return total

    def hand_on(direction, piece):
        device = (up, down, right, left)[direction]
        return pltpu.make_async_remote_copy(
            src_ref=kv.at[piece], dst_ref=kv.at[piece], send_sem=kv_send.at[direction, piece],
            recv_sem=kv_recv.at[piece], device_id=device, device_id_type=MESH)

    own = pl.ds(pl.multiple_of(core * ROWS, ROWS), ROWS)
    own_piece = core * 32 + chip
    other_piece = other * 32 + chip

    def swap(j, source, target, landing):
        return pltpu.make_async_remote_copy(
            src_ref=source, dst_ref=target, send_sem=s_send.at[j], recv_sem=landing,
            device_id=partner, device_id_type=MESH)

    give[2 * ROWS : SLOT, :] = info
    kv[own_piece, 2 * ROWS : SLOT, :] = info
    for j in (1, 2):
        both = project(j).astype(bf16)
        first, second = both[:, :HD], both[:, HD:]
        give[(j - 1) * ROWS : j * ROWS, :] = jnp.where(core == 0, second, first)
        kv[own_piece, (j - 1) * ROWS : j * ROWS, :] = jnp.where(core == 0, first, second)

    own_flag = [lax.rem(lax.div(words[-1], 1 << i), 2) == 1 for i in range(8)]
    s_copies = [swap(0, give, kv.at[own_piece], kv_recv.at[own_piece])]
    s_copies[0].start()
    for direction in range(4):
        @pl.when(own_flag[direction])
        def _(direction=direction):
            hand_on(direction, own_piece).start()

    both = (project(0) * (1.0 / math.sqrt(HD))).astype(bf16)
    first, second = both[:, :HD], both[:, HD:]
    qgive[...] = jnp.where(core == 0, second, first)
    s_copies.append(swap(1, qgive, qrows.at[own], s_recv.at[1]))
    s_copies[1].start()
    qrows[own, :] = jnp.where(core == 0, first, second)

    swap(0, give, kv.at[other_piece], kv_recv.at[other_piece]).wait_recv()
    for direction in range(4):
        @pl.when(own_flag[4 + direction])
        def _(direction=direction):
            hand_on(direction, other_piece).start()
    s_copies[1].wait_recv()

    def event(e):
        pair = lax.div(e, 2)
        word = words[0]
        for i in range(1, len(words) - 1):
            word = jnp.where(pair == i, words[i], word)
        code = jnp.where(lax.rem(e, 2) == 0, lax.rem(word, 2048), lax.div(word, 2048))
        piece = lax.rem(code, 64)
        flag = [lax.rem(lax.div(code, 64 << i), 2) == 1 for i in range(5)]
        source = lax.rem(piece, 32)
        return source != chip, piece, source, flag

    row = lax.broadcasted_iota(jnp.int32, (ROWS, HD), 0).astype(f32)
    lanes = lax.broadcasted_iota(jnp.int32, (ROWS, HD), 1)

    def inside(piece):
        bounds = kv[piece, 2 * ROWS : SLOT, :].astype(f32)
        return (row >= bounds[0:1, :]) & (row < bounds[1:2, :])

    for half in range(2):
        qmask[half * ROWS : (half + 1) * ROWS, :] = jnp.where(
            inside(half * 32 + chip) | (lanes >= 4), 0.0, masked_score).astype(bf16)

    def keys_of(piece):
        return jnp.concatenate(
            [kv[piece, 0:ROWS, :], jnp.where(inside(piece), 1.0, 0.0).astype(bf16)], axis=1)

    def scores_of(part, keys):
        rows = slice(part * ROWS, (part + 1) * ROWS)
        queries = jnp.concatenate([qrows[rows, :], qmask[rows, :]], axis=1)
        return lax.dot_general(queries, keys, (((1,), (1,)), ((), ())), preferred_element_type=f32)

    def keep(part, new_max, total, product):
        rows = slice(part * ROWS, (part + 1) * ROWS)
        run_max[rows, :] = jnp.broadcast_to(new_max, (ROWS, HD))
        run_sum[rows, :] = jnp.broadcast_to(total, (ROWS, HD))
        acc[rows, :] = product

    own_keys = [keys_of(chip), keys_of(32 + chip)]
    own_values = [kv[half * 32 + chip, ROWS : 2 * ROWS, :] for half in range(2)]
    q_at = lax.broadcasted_iota(jnp.int32, (ROWS, ROWS), 0)
    k_at = lax.broadcasted_iota(jnp.int32, (ROWS, ROWS), 1)
    for part in range(2):
        scores = [scores_of(part, own_keys[half]) for half in range(part + 1)]
        scores[part] = jnp.where(k_at <= q_at, scores[part], masked_score)
        new_max = jnp.max(scores[part], axis=1, keepdims=True)
        if part == 1:
            new_max = jnp.maximum(new_max, jnp.max(scores[0], axis=1, keepdims=True))
        total, product = 0.0, 0.0
        for half in range(part + 1):
            weights = jnp.exp(scores[half] - new_max)
            total = total + jnp.sum(weights, axis=1, keepdims=True)
            product = product + jnp.dot(
                weights.astype(bf16), own_values[half], preferred_element_type=f32)
        keep(part, new_max, total, product)

    def attend(source):
        keys = jnp.concatenate([keys_of(source), keys_of(32 + source)], axis=0)
        values = jnp.concatenate(
            [kv[half * 32 + source, ROWS : 2 * ROWS, :] for half in range(2)], axis=0)
        for part in range(2):
            rows = slice(part * ROWS, (part + 1) * ROWS)
            scores = scores_of(part, keys)
            old_max = run_max[rows, 0:1]
            new_max = jnp.maximum(old_max, jnp.max(scores, axis=1, keepdims=True))
            weights = jnp.exp(scores - new_max)
            factor = jnp.exp(old_max - new_max)
            total = run_sum[rows, 0:1] * factor + jnp.sum(weights, axis=1, keepdims=True)
            product = acc[rows, :] * factor + jnp.dot(
                weights.astype(bf16), values, preferred_element_type=f32)
            keep(part, new_max, total, product)

    def step(e, carry):
        valid, piece, source, flag = event(e)

        @pl.when(valid)
        def _():
            hand_on(0, piece).wait_recv()
            for direction in range(4):
                @pl.when(flag[direction])
                def _(direction=direction):
                    hand_on(direction, piece).start()

            @pl.when(flag[4])
            def _():
                attend(source)

        return carry

    lax.fori_loop(0, EVENTS, step, 0)

    for half in range(2):
        rows = slice(half * ROWS, (half + 1) * ROWS)
        ogive[half] = (acc[rows, :] / run_sum[rows, 0:1]).astype(bf16)

    o_copies = []
    lot = head * 2 + core
    for j in range(4):
        for c in range(2):
            if j == 0 and c == 0:
                continue
            row_core = core if c == 0 else other
            copy = pltpu.make_async_remote_copy(
                src_ref=ogive.at[row_core], dst_ref=att.at[lot], send_sem=o_send.at[j * 2 + c],
                recv_sem=o_recv.at[lot], device_id=(at(x, z, row_core), y_of[j]), device_id_type=MESH)
            copy.start()
            o_copies.append(copy)
    att[lot] = ogive[core]

    for direction in range(8):
        @pl.when(own_flag[direction])
        def _(direction=direction):
            hand_on(direction % 4, own_piece if direction < 4 else other_piece).wait_send()

    def drain(e, carry):
        valid, piece, source, flag = event(e)
        for direction in range(4):
            @pl.when(flag[direction])
            def _(direction=direction):
                hand_on(direction, piece).wait_send()
        return carry

    lax.fori_loop(0, EVENTS, drain, 0)
    for copy in x_copies + w_copies + s_copies:
        copy.wait_send()

    for j in range(1, 4):
        pltpu.make_async_remote_copy(
            src_ref=wout_hbm.at[:, columns], dst_ref=wcol.at[y_of[j]], send_sem=w_send.at[j],
            recv_sem=w_recv.at[y_of[j]], device_id=(seq, y_of[j]), device_id_type=MESH).wait_recv()
    for j in range(4):
        for c in range(2):
            if j == 0 and c == 0:
                continue
            lot_of = y_of[j] * 2 + (core if c == 0 else other)
            pltpu.make_async_remote_copy(
                src_ref=ogive.at[core], dst_ref=att.at[lot_of], send_sem=o_send.at[j * 2 + c],
                recv_sem=o_recv.at[lot_of], device_id=partner, device_id_type=MESH).wait_recv()

    total = None
    for y in range(4):
        both = jnp.concatenate([att[2 * y], att[2 * y + 1]], axis=1)
        term = jnp.dot(both, wcol[y], preferred_element_type=f32)
        total = term if total is None else total + term
    out_ref[...] = total.astype(bf16)

    for copy in o_copies:
        copy.wait_send()


def per_device(face_rows, norm_gain, w_qkv, w_out, segments):
    bf16, f32 = jnp.bfloat16, jnp.float32
    vmem = pl.BlockSpec(memory_space=pltpu.VMEM)
    hbm = pl.BlockSpec(memory_space=pl.ANY)
    dma = pltpu.SemaphoreType.DMA
    return pl.pallas_call(
        kernel,
        name="face_attention",
        out_shape=jax.ShapeDtypeStruct((ROWS, ROWS), bf16),
        in_specs=[hbm, hbm, hbm, hbm, hbm],
        out_specs=vmem,
        scratch_shapes=[
            pltpu.VMEM((4, ROWS, ROWS), bf16),
            pltpu.VMEM((1, 1024), f32),
            pltpu.VMEM((3, 1024, ROWS), bf16),
            pltpu.VMEM((4, ROWS, ROWS), bf16),
            pltpu.VMEM((2, HD), jnp.int32),
            pltpu.VMEM((64, SLOT, HD), bf16),
            pltpu.VMEM((SLOT, HD), bf16),
            pltpu.VMEM((ROWS, HD), bf16),
            pltpu.VMEM((BLOCK, HD), bf16),
            pltpu.VMEM((BLOCK, HD), bf16),
            pltpu.VMEM((BLOCK, HD), f32),
            pltpu.VMEM((BLOCK, HD), f32),
            pltpu.VMEM((BLOCK, HD), f32),
            pltpu.VMEM((2, ROWS, HD), bf16),
            pltpu.VMEM((8, ROWS, HD), bf16),
            dma((5,)),
            dma((4,)), dma((4,)),
            dma((4,)), dma((4,)),
            dma((4,)), dma((4,)),
            dma((4, 64)), dma((64,)),
            dma((8,)), dma((8,)),
        ],
        compiler_params=pltpu.CompilerParams(
            collective_id=0, has_side_effects=True, vmem_limit_bytes=67043328),
    )(
        face_rows,
        norm_gain.reshape(1, 1024),
        jnp.transpose(w_qkv, (1, 0, 2)),
        w_out,
        segments.reshape(2, HD),
    )


def solution(mesh):
    in_specs = (P("seq", "head"), P(), P(None, None, "head"), P("head", None), P("seq"))
    out_specs = P("seq", "head")
    return jax.shard_map(
        per_device, mesh=mesh, in_specs=in_specs, out_specs=out_specs, check_vma=False
    )
```

time: 94.6 us -> 73.7 us (0.78)
  the two profiles are of different devices: /device:TPU:5 before, /device:TPU:7 now
where the time goes in v3:
time: 73.7 us; the launch traced here: 73.6 us
  Pallas kernels  72 us (98%)
  local copies, waits for them, and re-layouts  1.57 us (2%)
    pallas_call x1, Pallas kernels, per_device(): pl.pallas_call(kernel, name='face_attention', out_shape=jax.ShapeDtypeStr...  72 us
    unnamed x1, local copies, waits for them, and re-layouts  1.57 us

profile of v3, /device:TPU:7, one launch (start us, length us, event | category | flops | bytes accessed | tf_op | source)
XLA Modules:
  0.0 73.6 jit_solution(16879809754593303068)
XLA Ops:
  0.0 72.0 %face_attention.1 = bf16[256,256]{1,0:T(8,128)(2,1)} custom-call(bf16[256,256]{1,0:T(8,128)(2,1)} %x_hbm.1, f32[1,1024]{1,0:T(1,128)} %bitcast.4, bf16[3,1024,256]{2,1,0:T(8,128)(2,1)} %bitcast.3, bf16[256,1024]{1,0:T(8,128)(2,1)} %wout_hbm.1, s32[2,128]{1,0:T(2,128)} %bitcast.5), custom_call_target="tpu_custom_call" | custom-call | tf_op jit(solution)/shard_map/face_attention/pallas_call | solution.py:400
  72.0 1.6 %copy.7 = bf16[256,256]{1,0:T(8,128)(2,1)} copy(bf16[256,256]{1,0:T(8,128)(2,1)} %face_attention.1) | data formatting | bytes 262144

commit v4 on v3

v4 whole, which is shorter than its diff:
```python
import functools
import math

import jax
import jax.numpy as jnp
from jax import lax
from jax.experimental import pallas as pl
from jax.experimental.pallas import tpu as pltpu
from jax.sharding import PartitionSpec as P

MESH = pl.DeviceIdType.MESH
HD = 128
epsilon = 1e-05
masked_score = -1e30
PLAN = (
    (1130881, 854311, 1147408, 856450, 1069862, 1274019, 1075883, 557, 0, 0, 0, 0, 0, 0, 0, 0, 0, 0, 0, 183),
    (1133065, 131202, 1069474, 2293923, 1399313, 2606, 2049, 2049, 2049, 2049, 2049, 2049, 2049, 2049, 2049, 2049, 2049, 2049, 2049, 183),
    (858177, 1071658, 1400161, 1083456, 1154400, 4652, 4098, 4098, 4098, 4098, 4098, 4098, 4098, 4098, 4098, 4098, 4098, 4098, 4098, 183),
    (660107, 1073835, 1401954, 1085697, 2820653, 2818048, 6147, 6147, 6147, 6147, 6147, 6147, 6147, 6147, 6147, 6147, 6147, 6147, 6147, 189),
    (662156, 1075884, 1404259, 1077314, 1158434, 1085793, 1079296, 2100256, 8753, 8196, 8196, 8196, 8196, 8196, 8196, 8196, 8196, 8196, 8196, 85),
    (664077, 1141262, 605284, 371246, 1079619, 263459, 237826, 2162945, 2692129, 10245, 10245, 10245, 10245, 10245, 10245, 10245, 10245, 10245, 10245, 221),
    (1915205, 2828974, 663936, 2827424, 137601, 1156129, 2429186, 13347, 12294, 12294, 12294, 12294, 12294, 12294, 12294, 12294, 12294, 12294, 12294, 212),
    (209280, 11680, 2427265, 2110501, 532610, 2172322, 612515, 1090563, 14343, 14343, 14343, 14343, 14343, 14343, 14343, 14343, 14343, 14343, 14343, 180),
    (655888, 346672, 1855745, 2308423, 2427438, 266566, 2306435, 2168227, 1075204, 2163565, 666788, 17701, 16392, 16392, 16392, 16392, 16392, 16392, 16392, 247),
    (1331457, 213521, 132424, 268546, 146851, 2162820, 2958439, 2167841, 616454, 2175045, 19749, 18441, 18441, 18441, 18441, 18441, 18441, 18441, 18441, 189),
    (673922, 1084777, 1153155, 2299299, 67944, 2244996, 2433088, 146464, 863233, 537639, 2632998, 20490, 20490, 20490, 20490, 20490, 20490, 20490, 20490, 151),
    (548938, 1085571, 271466, 673858, 2313636, 11299, 2959553, 274440, 132200, 556065, 2961735, 2168103, 23584, 22539, 22539, 22539, 22539, 22539, 22539, 157),
    (678413, 1665412, 1602788, 7275, 675973, 2839717, 275491, 1866258, 149538, 2962537, 2296321, 82343, 2114562, 561, 2112544, 24588, 24588, 24588, 24588, 223),
    (273294, 2435404, 8582, 1342828, 2437451, 2171303, 803847, 138603, 2168842, 4096, 2180202, 2057, 2165920, 2299177, 26637, 26637, 26637, 26637, 26637, 191),
    (682438, 294118, 142701, 802828, 2304391, 2844072, 84096, 677892, 2172064, 21803, 2164737, 7274, 2116647, 2168834, 29730, 28686, 28686, 28686, 28686, 215),
    (932232, 2846734, 1192, 870982, 158944, 283687, 2174977, 2845857, 4628, 532549, 2377731, 2167909, 25763, 2187307, 2120740, 31786, 30735, 30735, 30735, 70),
    (541073, 886880, 2572623, 365935, 280577, 145546, 70759, 685089, 2097587, 13353, 2102374, 2184302, 350243, 877635, 2646061, 2644037, 2123812, 2106405, 32784, 187),
    (561289, 164274, 1379696, 2099744, 890952, 2494626, 2179407, 71722, 2118767, 2181388, 2242663, 468396, 551182, 2906155, 2190382, 78851, 2105381, 2108422, 34833, 59),
    (676433, 1381043, 689265, 2850825, 2445315, 812137, 148515, 285868, 2310415, 2101645, 2848964, 2189351, 2185253, 2171911, 274446, 2176046, 37893, 36882, 36882, 115),
    (23122, 2855043, 3217548, 560300, 21739, 2852937, 813328, 204805, 2452848, 17513, 2172934, 816232, 2454532, 2175087, 15375, 2178090, 38931, 38931, 38931, 117),
    (2857299, 22700, 272525, 2122322, 2174258, 2185350, 2189454, 8753, 149578, 2577444, 31790, 99369, 17446, 2133008, 15400, 2178095, 40980, 40980, 40980, 85),
    (289108, 2859141, 155662, 2173011, 2857094, 2188334, 2176045, 22866, 80272, 31792, 821384, 21547, 2199561, 2315399, 2194472, 2198569, 43029, 43029, 43029, 85),
    (174414, 2454901, 555174, 2109780, 80272, 2334797, 2190768, 16460, 694417, 2722951, 2442547, 85167, 2187602, 154674, 21513, 2315307, 45078, 45078, 45078, 85),
    (948502, 2732432, 2849968, 1259598, 821269, 2729992, 2112945, 2191892, 27688, 364777, 2729609, 1204362, 2136115, 140333, 89106, 2120748, 48170, 47127, 47127, 68),
    (1114265, 82007, 163857, 2114679, 176274, 2458737, 31922, 2193958, 2338825, 2181130, 3232302, 1136725, 367669, 2126995, 1075220, 2190388, 2121772, 50187, 49176, 51),
    (1116248, 431224, 281778, 3491888, 348247, 3167248, 34963, 2329719, 31275, 45204, 2338926, 2187276, 2204750, 2123821, 2202635, 2193461, 52245, 51225, 51225, 19),
    (1118297, 2345010, 2118314, 180371, 33291, 2196600, 34964, 2135091, 2466859, 178188, 2341932, 161813, 2197677, 95245, 46319, 2468982, 54286, 53274, 53274, 17),
    (184835, 22675, 2347555, 3233940, 182284, 103604, 167033, 306220, 180909, 2202642, 308273, 2124981, 33912, 47662, 31856, 2126903, 2208879, 55323, 55323, 17),
    (303195, 2465804, 306299, 185388, 26707, 2189861, 2348083, 307214, 2467865, 233495, 3503225, 2134033, 31798, 2209880, 99384, 2198544, 58415, 57372, 57372, 17),
    (188933, 1386709, 27957, 308348, 309339, 3237902, 631931, 2471086, 2471955, 2201690, 115215, 52346, 37908, 296562, 2346031, 2146321, 2197041, 59421, 59421, 17),
    (190614, 309798, 2471037, 188967, 94232, 175118, 2206903, 2352312, 313359, 41051, 3505275, 2457616, 184337, 2347027, 2460724, 2201650, 2135161, 61470, 61470, 17),
    (61655, 1128600, 2475255, 177214, 313359, 32797, 2339901, 58543, 296978, 2195541, 2221173, 56370, 2219057, 2138228, 104474, 2137146, 64569, 63519, 63519, 0),
    (330280, 332582, 537097, 1069186, 1075757, 65568, 65568, 65568, 65568, 65568, 65568, 65568, 65568, 65568, 65568, 65568, 65568, 65568, 65568, 127),
    (856416, 266793, 1070400, 68139, 67617, 67617, 67617, 67617, 67617, 67617, 67617, 67617, 67617, 67617, 67617, 67617, 67617, 67617, 67617, 91),
    (596522, 1136993, 1072193, 721156, 70976, 69666, 69666, 69666, 69666, 69666, 69666, 69666, 69666, 69666, 69666, 69666, 69666, 69666, 69666, 127),
    (201092, 1140034, 723468, 66881, 72768, 71715, 71715, 71715, 71715, 71715, 71715, 71715, 71715, 71715, 71715, 71715, 71715, 71715, 71715, 87),
    (1583203, 724291, 2756898, 1145363, 2754592, 75008, 73764, 73764, 73764, 73764, 73764, 73764, 73764, 73764, 73764, 73764, 73764, 73764, 73764, 181),
    (729645, 728132, 2759343, 592439, 327682, 1154048, 2168065, 76304, 75813, 75813, 75813, 75813, 75813, 75813, 75813, 75813, 75813, 75813, 75813, 245),
    (731694, 1408069, 205216, 2884279, 68676, 727567, 2759189, 1081908, 1149346, 1154306, 78849, 77862, 77862, 77862, 77862, 77862, 77862, 77862, 77862, 89),
    (328239, 1079654, 2765367, 601216, 1159585, 857349, 74256, 1150082, 597252, 2362371, 79911, 79911, 79911, 79911, 79911, 79911, 79911, 79911, 79911, 76),
    (1853609, 2883744, 211594, 2242689, 790630, 2165293, 793926, 2169613, 598277, 2698274, 82948, 81960, 81960, 81960, 81960, 81960, 81960, 81960, 81960, 123),
    (1855848, 1661313, 66632, 2691458, 2098209, 268391, 2956359, 8294, 2766244, 2632101, 84009, 84009, 84009, 84009, 84009, 84009, 84009, 84009, 84009, 123),
    (740011, 1071234, 68937, 2955651, 794696, 2180260, 1058, 736288, 2369957, 2636801, 2109734, 86058, 86058, 86058, 86058, 86058, 86058, 86058, 86058, 125),
    (1073708, 792938, 2773252, 216484, 337922, 265507, 2894881, 147718, 2168137, 2176104, 65543, 2178048, 88107, 88107, 88107, 88107, 88107, 88107, 88107, 119),
    (743844, 339019, 2369898, 2236947, 621898, 6278, 2437417, 2168994, 2232359, 67912, 2099360, 2360585, 2704775, 90156, 90156, 90156, 90156, 90156, 90156, 119),
    (862316, 2239564, 204975, 799083, 2251878, 866467, 1153386, 328707, 68612, 2643079, 2097680, 5121, 84008, 2167816, 93193, 92205, 92205, 92205, 92205, 93),
    (1931382, 1603693, 2254982, 76343, 866412, 1092684, 2107956, 2898080, 2359952, 16484, 743985, 2175401, 2179107, 68683, 611331, 332339, 2379018, 2102273, 95236, 77),
    (606903, 618727, 2901447, 78390, 747945, 2109968, 2780169, 66097, 329765, 2125868, 2239488, 808204, 2183202, 3409956, 613572, 72706, 2104331, 96303, 96303, 238),
    (887095, 65864, 96401, 80009, 1117224, 873472, 210191, 5121, 2242894, 2110766, 2118060, 7714, 2646059, 2181133, 11309, 74763, 2106403, 99365, 98352, 119),
    (348833, 688232, 2244873, 877697, 2232482, 2384043, 2196491, 2117635, 2432041, 12295, 97318, 2367524, 29711, 2178350, 26661, 2108461, 100401, 100401, 100401, 119),
    (755882, 347402, 2116689, 557228, 2908264, 2244739, 2169133, 23600, 2386052, 2101282, 881700, 474155, 2172933, 2242607, 2109478, 2128910, 102450, 102450, 102450, 85),
    (874610, 2790731, 86188, 6257, 9356, 355409, 2911242, 1131684, 2169262, 273416, 2502694, 19598, 2173040, 621584, 2181159, 2112655, 104499, 104499, 104499, 85),
    (236012, 3317132, 354820, 2911268, 757765, 2185291, 2789806, 1388586, 2912369, 2436433, 358672, 80906, 2914537, 148486, 2247728, 2180103, 106548, 106548, 106548, 85),
    (762029, 2794957, 1388974, 221349, 2388997, 2792051, 96299, 295218, 2251846, 2391314, 100519, 86568, 2254097, 2118663, 2113577, 2116656, 108597, 108597, 108597, 85),
    (633006, 340247, 3321294, 1286448, 3440815, 2390029, 2269745, 1392679, 2373676, 1285393, 88585, 2110803, 2182152, 2122827, 87085, 2117682, 111634, 110646, 110646, 92),
    (227504, 569447, 1412752, 345167, 1209745, 568391, 2322569, 1134644, 2663560, 2206774, 103529, 628973, 2137101, 91282, 2122762, 2119723, 112695, 112695, 112695, 105),
    (492064, 2130105, 243865, 381480, 2197521, 2275506, 1127432, 18543, 177193, 87186, 2340362, 240719, 301134, 2201645, 2124846, 90635, 42027, 2204684, 115733, 51),
    (1116346, 114897, 2277554, 346224, 2130039, 2116754, 2117674, 2275475, 1334451, 2447983, 368684, 2122772, 306767, 2142262, 1141877, 2197518, 2192397, 116793, 116793, 51),
    (1118386, 2396281, 2279594, 231603, 2118737, 2398251, 3430488, 1278132, 2261036, 2400375, 306316, 1145879, 110765, 95373, 2143247, 2206734, 119864, 118842, 118842, 19),
    (250099, 2399322, 368683, 2119801, 2400428, 2279442, 232460, 2402357, 2132150, 1277976, 2385965, 95760, 113714, 2389142, 97464, 2145295, 120891, 120891, 120891, 17),
    (252084, 2400772, 371803, 90629, 2402355, 2252922, 26806, 2452570, 247986, 95251, 2134063, 2149526, 35982, 2328760, 2195472, 113688, 2407567, 122940, 122940, 17),
    (1058997, 255125, 373852, 354427, 2284557, 2404404, 97364, 94392, 2408506, 374803, 1073202, 2282647, 2202639, 117778, 2125841, 1147953, 2149392, 124989, 124989, 17),
    (256550, 94390, 240733, 96440, 255126, 310424, 2391095, 2388025, 2285691, 361493, 2138228, 119961, 2131035, 35378, 39985, 2282514, 128051, 127038, 127038, 17),
    (377383, 178238, 2158703, 2129048, 126007, 176176, 2156729, 382105, 1289846, 35506, 2129980, 2199186, 121877, 38996, 2202652, 2204699, 130074, 129087, 129087, 0),
)
EVENTS = 2 * (len(PLAN[0]) - 1)
ROWS = 256
BLOCK = 512
INFO = 16
SLOT = 2 * ROWS + INFO


def pick(values, index):
    result = jnp.int32(values[0])
    for at in range(1, len(values)):
        result = jnp.where(index == at, jnp.int32(values[at]), result)
    return result


def kernel(
    x_hbm, gain_hbm, wqkv_hbm, wout_hbm, seg_hbm, out_ref,
    xbuf, gain_ref, wqkv, wcol, seg_ref, kv, give, qgive, qrows, qmask, acc, run_max, run_sum, ogive, att,
    local_sem, x_send, x_recv, w_send, w_recv, s_send, s_recv, kv_send, kv_recv, o_send, o_recv,
):
    f32, bf16 = jnp.float32, jnp.bfloat16
    seq, head = lax.axis_index("seq"), lax.axis_index("head")
    core = lax.rem(seq, 2)
    chip = lax.div(seq, 2)
    z = lax.rem(chip, 8)
    x = lax.div(chip, 8)
    other = 1 - core

    def at(xx, zz, cc):
        return (xx * 8 + zz) * 2 + cc

    z_up, z_down = lax.rem(z + 1, 8), lax.rem(z + 7, 8)
    x_up, x_down = lax.rem(x + 1, 4), lax.rem(x + 3, 4)
    up = (at(x, z_up, core), head)
    down = (at(x, z_down, core), head)
    right = (at(x_up, z, core), head)
    left = (at(x_down, z, core), head)
    partner = (at(x, z, other), head)
    y_of = [lax.rem(head + j, 4) for j in range(4)]

    barrier = pltpu.get_barrier_semaphore()
    greeted = [up, down, right, left, partner]
    for j in range(1, 4):
        greeted.append((seq, y_of[j]))
        greeted.append((at(x, z, other), y_of[j]))
    for device in greeted:
        pl.semaphore_signal(barrier, inc=1, device_id=device, device_id_type=MESH)

    seg_in = pltpu.make_async_copy(seg_hbm, seg_ref, local_sem.at[3])
    seg_in.start()
    gain_in = pltpu.make_async_copy(gain_hbm, gain_ref, local_sem.at[4])
    gain_in.start()
    mine = pltpu.make_async_copy(x_hbm, xbuf.at[head], local_sem.at[0])
    mine.start()
    weights_in = pltpu.make_async_copy(wqkv_hbm, wqkv, local_sem.at[1])
    weights_in.start()
    columns = pl.ds(pl.multiple_of(head * ROWS, ROWS), ROWS)
    wcol_in = pltpu.make_async_copy(wout_hbm.at[:, columns], wcol.at[head], local_sem.at[2])
    wcol_in.start()

    pl.semaphore_wait(barrier, len(greeted))

    x_copies = []
    for j in (2, 1, 3):
        copy = pltpu.make_async_remote_copy(
            src_ref=x_hbm, dst_ref=xbuf.at[head], send_sem=x_send.at[j], recv_sem=x_recv.at[head],
            device_id=(seq, y_of[j]), device_id_type=MESH)
        copy.start()
        x_copies.append(copy)
    seg_in.wait()
    seg = seg_ref[...]
    lane = lax.broadcasted_iota(jnp.int32, (1, HD), 1)
    sub = lax.broadcasted_iota(jnp.int32, (INFO, HD), 0)
    lower = jnp.zeros((1, HD), f32)
    upper = jnp.zeros((1, HD), f32)
    for t in range(1, 5):
        before = jnp.sum(jnp.where(seg < t, 1.0, 0.0).astype(f32), axis=1, keepdims=True)
        before = before[0:1] + before[1:2]
        lower = jnp.where(lane == t, before, lower)
        upper = jnp.where(lane == t - 1, before, upper)
    lower = jnp.where(lane < 4, lower, 0.0)
    info = jnp.where(sub == 0, lower, jnp.where(sub == 1, upper, 0.0)).astype(bf16)

    mine_at = core * 32 + chip
    words = [pick([row[i] for row in PLAN], mine_at) for i in range(len(PLAN[0]))]
    gain_in.wait()
    mine.wait()
    weights_in.wait()
    wcol_in.wait()
    for j in range(1, 4):
        pltpu.make_async_remote_copy(
            src_ref=x_hbm, dst_ref=xbuf.at[y_of[j]], send_sem=x_send.at[j], recv_sem=x_recv.at[y_of[j]],
            device_id=(seq, y_of[j]), device_id_type=MESH).wait_recv()

    w_copies = []
    for j in range(1, 4):
        theirs = pl.ds(pl.multiple_of(y_of[j] * ROWS, ROWS), ROWS)
        copy = pltpu.make_async_remote_copy(
            src_ref=wout_hbm.at[:, theirs], dst_ref=wcol.at[head], send_sem=w_send.at[j],
            recv_sem=w_recv.at[head], device_id=(seq, y_of[j]), device_id_type=MESH)
        copy.start()
        w_copies.append(copy)

    parts = [xbuf[y].astype(f32) for y in range(4)]
    squares = sum(jnp.sum(part * part, axis=1, keepdims=True) for part in parts)
    scale = lax.rsqrt(squares * (1.0 / 1024.0) + epsilon)
    normed = jnp.concatenate(
        [(parts[y] * scale * gain_ref[:, y * ROWS : (y + 1) * ROWS]).astype(bf16) for y in range(4)], axis=1)

    def project(which):
        return jnp.dot(normed, wqkv[which], preferred_element_type=f32)

    def hand_on(direction, piece):
        device = (up, down, right, left)[direction]
        return pltpu.make_async_remote_copy(
            src_ref=kv.at[piece], dst_ref=kv.at[piece], send_sem=kv_send.at[direction, piece],
            recv_sem=kv_recv.at[piece], device_id=device, device_id_type=MESH)

    own = pl.ds(pl.multiple_of(core * ROWS, ROWS), ROWS)
    own_piece = core * 32 + chip
    other_piece = other * 32 + chip

    def swap(j, source, target, landing):
        return pltpu.make_async_remote_copy(
            src_ref=source, dst_ref=target, send_sem=s_send.at[j], recv_sem=landing,
            device_id=partner, device_id_type=MESH)

    give[2 * ROWS : SLOT, :] = info
    kv[own_piece, 2 * ROWS : SLOT, :] = info
    for j in (1, 2):
        both = project(j).astype(bf16)
        first, second = both[:, :HD], both[:, HD:]
        give[(j - 1) * ROWS : j * ROWS, :] = jnp.where(core == 0, second, first)
        kv[own_piece, (j - 1) * ROWS : j * ROWS, :] = jnp.where(core == 0, first, second)

    own_flag = [lax.rem(lax.div(words[-1], 1 << i), 2) == 1 for i in range(8)]
    s_copies = [swap(0, give, kv.at[own_piece], kv_recv.at[own_piece])]
    s_copies[0].start()
    for direction in range(4):
        @pl.when(own_flag[direction])
        def _(direction=direction):
            hand_on(direction, own_piece).start()

    both = (project(0) * (1.0 / math.sqrt(HD))).astype(bf16)
    first, second = both[:, :HD], both[:, HD:]
    qgive[...] = jnp.where(core == 0, second, first)
    s_copies.append(swap(1, qgive, qrows.at[own], s_recv.at[1]))
    s_copies[1].start()
    qrows[own, :] = jnp.where(core == 0, first, second)

    swap(0, give, kv.at[other_piece], kv_recv.at[other_piece]).wait_recv()
    for direction in range(4):
        @pl.when(own_flag[4 + direction])
        def _(direction=direction):
            hand_on(direction, other_piece).start()
    s_copies[1].wait_recv()

    def event(e):
        pair = lax.div(e, 2)
        word = words[0]
        for i in range(1, len(words) - 1):
            word = jnp.where(pair == i, words[i], word)
        code = jnp.where(lax.rem(e, 2) == 0, lax.rem(word, 2048), lax.div(word, 2048))
        piece = lax.rem(code, 64)
        flag = [lax.rem(lax.div(code, 64 << i), 2) == 1 for i in range(5)]
        source = lax.rem(piece, 32)
        return source != chip, piece, source, flag

    row = lax.broadcasted_iota(jnp.int32, (ROWS, HD), 0).astype(f32)
    lanes = lax.broadcasted_iota(jnp.int32, (ROWS, HD), 1)

    def inside(piece):
        bounds = kv[piece, 2 * ROWS : SLOT, :].astype(f32)
        return (row >= bounds[0:1, :]) & (row < bounds[1:2, :])

    for half in range(2):
        qmask[half * ROWS : (half + 1) * ROWS, :] = jnp.where(
            inside(half * 32 + chip) | (lanes >= 4), 0.0, masked_score).astype(bf16)

    def keys_of(piece):
        return jnp.concatenate(
            [kv[piece, 0:ROWS, :], jnp.where(inside(piece), 1.0, 0.0).astype(bf16)], axis=1)

    def scores_of(part, keys):
        rows = slice(part * ROWS, (part + 1) * ROWS)
        queries = jnp.concatenate([qrows[rows, :], qmask[rows, :]], axis=1)
        return lax.dot_general(queries, keys, (((1,), (1,)), ((), ())), preferred_element_type=f32)

    def keep(part, new_max, total, product):
        rows = slice(part * ROWS, (part + 1) * ROWS)
        run_max[rows, :] = jnp.broadcast_to(new_max, (ROWS, HD))
        run_sum[rows, :] = jnp.broadcast_to(total, (ROWS, HD))
        acc[rows, :] = product

    own_keys = [keys_of(chip), keys_of(32 + chip)]
    own_values = [kv[half * 32 + chip, ROWS : 2 * ROWS, :] for half in range(2)]
    q_at = lax.broadcasted_iota(jnp.int32, (ROWS, ROWS), 0)
    k_at = lax.broadcasted_iota(jnp.int32, (ROWS, ROWS), 1)
    for part in range(2):
        scores = [scores_of(part, own_keys[half]) for half in range(part + 1)]
        scores[part] = jnp.where(k_at <= q_at, scores[part], masked_score)
        new_max = jnp.max(scores[part], axis=1, keepdims=True)
        if part == 1:
            new_max = jnp.maximum(new_max, jnp.max(scores[0], axis=1, keepdims=True))
        total, product = 0.0, 0.0
        for half in range(part + 1):
            weights = jnp.exp(scores[half] - new_max)
            total = total + jnp.sum(weights, axis=1, keepdims=True)
            product = product + jnp.dot(
                weights.astype(bf16), own_values[half], preferred_element_type=f32)
        keep(part, new_max, total, product)

    def attend(source):
        keys = jnp.concatenate([keys_of(source), keys_of(32 + source)], axis=0)
        values = jnp.concatenate(
            [kv[half * 32 + source, ROWS : 2 * ROWS, :] for half in range(2)], axis=0)
        queries = jnp.concatenate([qrows[...], qmask[...]], axis=1)
        scores = lax.dot_general(
            queries, keys, (((1,), (1,)), ((), ())), preferred_element_type=f32)
        old_max = run_max[...]
        new_max = jnp.maximum(old_max, jnp.max(scores, axis=1, keepdims=True))
        weights = jnp.exp(scores - jnp.concatenate([new_max] * (BLOCK // HD), axis=1))
        factor = jnp.exp(old_max - new_max)
        run_max[...] = new_max
        run_sum[...] = run_sum[...] * factor + jnp.sum(weights, axis=1, keepdims=True)
        acc[...] = acc[...] * factor + jnp.dot(
            weights.astype(bf16), values, preferred_element_type=f32)

    def step(e, carry):
        valid, piece, source, flag = event(e)

        @pl.when(valid)
        def _():
            hand_on(0, piece).wait_recv()
            for direction in range(4):
                @pl.when(flag[direction])
                def _(direction=direction):
                    hand_on(direction, piece).start()

            @pl.when(flag[4])
            def _():
                attend(source)

        return carry

    lax.fori_loop(0, EVENTS, step, 0)

    for half in range(2):
        rows = slice(half * ROWS, (half + 1) * ROWS)
        ogive[half] = (acc[rows, :] / run_sum[rows, 0:1]).astype(bf16)

    o_copies = []
    lot = head * 2 + core
    for j in (2, 1, 3, 0):
        for c in range(2):
            if j == 0 and c == 0:
                continue
            row_core = core if c == 0 else other
            copy = pltpu.make_async_remote_copy(
                src_ref=ogive.at[row_core], dst_ref=att.at[lot], send_sem=o_send.at[j * 2 + c],
                recv_sem=o_recv.at[lot], device_id=(at(x, z, row_core), y_of[j]), device_id_type=MESH)
            copy.start()
            o_copies.append(copy)
    att[lot] = ogive[core]

    for direction in range(8):
        @pl.when(own_flag[direction])
        def _(direction=direction):
            hand_on(direction % 4, own_piece if direction < 4 else other_piece).wait_send()

    def drain(e, carry):
        valid, piece, source, flag = event(e)
        for direction in range(4):
            @pl.when(flag[direction])
            def _(direction=direction):
                hand_on(direction, piece).wait_send()
        return carry

    lax.fori_loop(0, EVENTS, drain, 0)
    for copy in x_copies + w_copies + s_copies:
        copy.wait_send()

    for j in range(1, 4):
        pltpu.make_async_remote_copy(
            src_ref=wout_hbm.at[:, columns], dst_ref=wcol.at[y_of[j]], send_sem=w_send.at[j],
            recv_sem=w_recv.at[y_of[j]], device_id=(seq, y_of[j]), device_id_type=MESH).wait_recv()
    total = None
    for j in (0, 1, 3, 2):
        for c in range(2):
            if j == 0 and c == 0:
                continue
            lot_of = y_of[j] * 2 + (core if c == 0 else other)
            pltpu.make_async_remote_copy(
                src_ref=ogive.at[core], dst_ref=att.at[lot_of], send_sem=o_send.at[j * 2 + c],
                recv_sem=o_recv.at[lot_of], device_id=partner, device_id_type=MESH).wait_recv()
        both = jnp.concatenate([att[2 * y_of[j]], att[2 * y_of[j] + 1]], axis=1)
        term = jnp.dot(both, wcol[y_of[j]], preferred_element_type=f32)
        total = term if total is None else total + term
    out_ref[...] = total.astype(bf16)

    for copy in o_copies:
        copy.wait_send()


def per_device(face_rows, norm_gain, w_qkv, w_out, segments):
    bf16, f32 = jnp.bfloat16, jnp.float32
    vmem = pl.BlockSpec(memory_space=pltpu.VMEM)
    hbm = pl.BlockSpec(memory_space=pl.ANY)
    dma = pltpu.SemaphoreType.DMA
    return pl.pallas_call(
        kernel,
        name="face_attention",
        out_shape=jax.ShapeDtypeStruct((ROWS, ROWS), bf16),
        in_specs=[hbm, hbm, hbm, hbm, hbm],
        out_specs=vmem,
        scratch_shapes=[
            pltpu.VMEM((4, ROWS, ROWS), bf16),
            pltpu.VMEM((1, 1024), f32),
            pltpu.VMEM((3, 1024, ROWS), bf16),
            pltpu.VMEM((4, ROWS, ROWS), bf16),
            pltpu.VMEM((2, HD), jnp.int32),
            pltpu.VMEM((64, SLOT, HD), bf16),
            pltpu.VMEM((SLOT, HD), bf16),
            pltpu.VMEM((ROWS, HD), bf16),
            pltpu.VMEM((BLOCK, HD), bf16),
            pltpu.VMEM((BLOCK, HD), bf16),
            pltpu.VMEM((BLOCK, HD), f32),
            pltpu.VMEM((BLOCK, HD), f32),
            pltpu.VMEM((BLOCK, HD), f32),
            pltpu.VMEM((2, ROWS, HD), bf16),
            pltpu.VMEM((8, ROWS, HD), bf16),
            dma((5,)),
            dma((4,)), dma((4,)),
            dma((4,)), dma((4,)),
            dma((4,)), dma((4,)),
            dma((4, 64)), dma((64,)),
            dma((8,)), dma((8,)),
        ],
        compiler_params=pltpu.CompilerParams(
            collective_id=0, has_side_effects=True, vmem_limit_bytes=67043328),
    )(
        face_rows,
        norm_gain.reshape(1, 1024),
        jnp.transpose(w_qkv, (1, 0, 2)),
        w_out,
        segments.reshape(2, HD),
    )


def solution(mesh):
    in_specs = (P("seq", "head"), P(), P(None, None, "head"), P("head", None), P("seq"))
    out_specs = P("seq", "head")
    return jax.shard_map(
        per_device, mesh=mesh, in_specs=in_specs, out_specs=out_specs, check_vma=False
    )
```

time: 73.7 us -> 69.8 us (0.947)
  the two profiles are of different devices: /device:TPU:7 before, /device:TPU:5 now
where the time goes in v4:
time: 69.8 us; the launch traced here: 69.4 us
  Pallas kernels  67.8 us (97%)
  local copies, waits for them, and re-layouts  1.57 us (2%)
    pallas_call x1, Pallas kernels, per_device(): pl.pallas_call(kernel, name='face_attention', out_shape=jax.ShapeDtypeStr...  67.8 us
    unnamed x1, local copies, waits for them, and re-layouts  1.57 us

profile of v4, /device:TPU:5, one launch (start us, length us, event | category | flops | bytes accessed | tf_op | source)
XLA Modules:
  0.0 69.4 jit_solution(15348559765156553331)
XLA Ops:
  0.0 67.8 %face_attention.1 = bf16[256,256]{1,0:T(8,128)(2,1)} custom-call(bf16[256,256]{1,0:T(8,128)(2,1)} %x_hbm.1, f32[1,1024]{1,0:T(1,128)} %bitcast.4, bf16[3,1024,256]{2,1,0:T(8,128)(2,1)} %bitcast.3, bf16[256,1024]{1,0:T(8,128)(2,1)} %wout_hbm.1, s32[2,128]{1,0:T(2,128)} %bitcast.5), custom_call_target="tpu_custom_call" | custom-call | tf_op jit(solution)/shard_map/face_attention/pallas_call | solution.py:389
  67.8 1.6 %copy.7 = bf16[256,256]{1,0:T(8,128)(2,1)} copy(bf16[256,256]{1,0:T(8,128)(2,1)} %face_attention.1) | data formatting | bytes 262144

commit v5 on v4

--- a/solution.py
+++ b/solution.py
@@ -13,70 +13,70 @@
 epsilon = 1e-05
 masked_score = -1e30
 PLAN = (
-    (1130881, 854311, 1147408, 856450, 1069862, 1274019, 1075883, 557, 0, 0, 0, 0, 0, 0, 0, 0, 0, 0, 0, 183),
-    (1133065, 131202, 1069474, 2293923, 1399313, 2606, 2049, 2049, 2049, 2049, 2049, 2049, 2049, 2049, 2049, 2049, 2049, 2049, 2049, 183),
-    (858177, 1071658, 1400161, 1083456, 1154400, 4652, 4098, 4098, 4098, 4098, 4098, 4098, 4098, 4098, 4098, 4098, 4098, 4098, 4098, 183),
-    (660107, 1073835, 1401954, 1085697, 2820653, 2818048, 6147, 6147, 6147, 6147, 6147, 6147, 6147, 6147, 6147, 6147, 6147, 6147, 6147, 189),
-    (662156, 1075884, 1404259, 1077314, 1158434, 1085793, 1079296, 2100256, 8753, 8196, 8196, 8196, 8196, 8196, 8196, 8196, 8196, 8196, 8196, 85),
-    (664077, 1141262, 605284, 371246, 1079619, 263459, 237826, 2162945, 2692129, 10245, 10245, 10245, 10245, 10245, 10245, 10245, 10245, 10245, 10245, 221),
-    (1915205, 2828974, 663936, 2827424, 137601, 1156129, 2429186, 13347, 12294, 12294, 12294, 12294, 12294, 12294, 12294, 12294, 12294, 12294, 12294, 212),
-    (209280, 11680, 2427265, 2110501, 532610, 2172322, 612515, 1090563, 14343, 14343, 14343, 14343, 14343, 14343, 14343, 14343, 14343, 14343, 14343, 180),
-    (655888, 346672, 1855745, 2308423, 2427438, 266566, 2306435, 2168227, 1075204, 2163565, 666788, 17701, 16392, 16392, 16392, 16392, 16392, 16392, 16392, 247),
-    (1331457, 213521, 132424, 268546, 146851, 2162820, 2958439, 2167841, 616454, 2175045, 19749, 18441, 18441, 18441, 18441, 18441, 18441, 18441, 18441, 189),
-    (673922, 1084777, 1153155, 2299299, 67944, 2244996, 2433088, 146464, 863233, 537639, 2632998, 20490, 20490, 20490, 20490, 20490, 20490, 20490, 20490, 151),
-    (548938, 1085571, 271466, 673858, 2313636, 11299, 2959553, 274440, 132200, 556065, 2961735, 2168103, 23584, 22539, 22539, 22539, 22539, 22539, 22539, 157),
-    (678413, 1665412, 1602788, 7275, 675973, 2839717, 275491, 1866258, 149538, 2962537, 2296321, 82343, 2114562, 561, 2112544, 24588, 24588, 24588, 24588, 223),
-    (273294, 2435404, 8582, 1342828, 2437451, 2171303, 803847, 138603, 2168842, 4096, 2180202, 2057, 2165920, 2299177, 26637, 26637, 26637, 26637, 26637, 191),
-    (682438, 294118, 142701, 802828, 2304391, 2844072, 84096, 677892, 2172064, 21803, 2164737, 7274, 2116647, 2168834, 29730, 28686, 28686, 28686, 28686, 215),
-    (932232, 2846734, 1192, 870982, 158944, 283687, 2174977, 2845857, 4628, 532549, 2377731, 2167909, 25763, 2187307, 2120740, 31786, 30735, 30735, 30735, 70),
-    (541073, 886880, 2572623, 365935, 280577, 145546, 70759, 685089, 2097587, 13353, 2102374, 2184302, 350243, 877635, 2646061, 2644037, 2123812, 2106405, 32784, 187),
-    (561289, 164274, 1379696, 2099744, 890952, 2494626, 2179407, 71722, 2118767, 2181388, 2242663, 468396, 551182, 2906155, 2190382, 78851, 2105381, 2108422, 34833, 59),
-    (676433, 1381043, 689265, 2850825, 2445315, 812137, 148515, 285868, 2310415, 2101645, 2848964, 2189351, 2185253, 2171911, 274446, 2176046, 37893, 36882, 36882, 115),
-    (23122, 2855043, 3217548, 560300, 21739, 2852937, 813328, 204805, 2452848, 17513, 2172934, 816232, 2454532, 2175087, 15375, 2178090, 38931, 38931, 38931, 117),
-    (2857299, 22700, 272525, 2122322, 2174258, 2185350, 2189454, 8753, 149578, 2577444, 31790, 99369, 17446, 2133008, 15400, 2178095, 40980, 40980, 40980, 85),
-    (289108, 2859141, 155662, 2173011, 2857094, 2188334, 2176045, 22866, 80272, 31792, 821384, 21547, 2199561, 2315399, 2194472, 2198569, 43029, 43029, 43029, 85),
-    (174414, 2454901, 555174, 2109780, 80272, 2334797, 2190768, 16460, 694417, 2722951, 2442547, 85167, 2187602, 154674, 21513, 2315307, 45078, 45078, 45078, 85),
-    (948502, 2732432, 2849968, 1259598, 821269, 2729992, 2112945, 2191892, 27688, 364777, 2729609, 1204362, 2136115, 140333, 89106, 2120748, 48170, 47127, 47127, 68),
-    (1114265, 82007, 163857, 2114679, 176274, 2458737, 31922, 2193958, 2338825, 2181130, 3232302, 1136725, 367669, 2126995, 1075220, 2190388, 2121772, 50187, 49176, 51),
-    (1116248, 431224, 281778, 3491888, 348247, 3167248, 34963, 2329719, 31275, 45204, 2338926, 2187276, 2204750, 2123821, 2202635, 2193461, 52245, 51225, 51225, 19),
-    (1118297, 2345010, 2118314, 180371, 33291, 2196600, 34964, 2135091, 2466859, 178188, 2341932, 161813, 2197677, 95245, 46319, 2468982, 54286, 53274, 53274, 17),
-    (184835, 22675, 2347555, 3233940, 182284, 103604, 167033, 306220, 180909, 2202642, 308273, 2124981, 33912, 47662, 31856, 2126903, 2208879, 55323, 55323, 17),
-    (303195, 2465804, 306299, 185388, 26707, 2189861, 2348083, 307214, 2467865, 233495, 3503225, 2134033, 31798, 2209880, 99384, 2198544, 58415, 57372, 57372, 17),
-    (188933, 1386709, 27957, 308348, 309339, 3237902, 631931, 2471086, 2471955, 2201690, 115215, 52346, 37908, 296562, 2346031, 2146321, 2197041, 59421, 59421, 17),
-    (190614, 309798, 2471037, 188967, 94232, 175118, 2206903, 2352312, 313359, 41051, 3505275, 2457616, 184337, 2347027, 2460724, 2201650, 2135161, 61470, 61470, 17),
-    (61655, 1128600, 2475255, 177214, 313359, 32797, 2339901, 58543, 296978, 2195541, 2221173, 56370, 2219057, 2138228, 104474, 2137146, 64569, 63519, 63519, 0),
-    (330280, 332582, 537097, 1069186, 1075757, 65568, 65568, 65568, 65568, 65568, 65568, 65568, 65568, 65568, 65568, 65568, 65568, 65568, 65568, 127),
-    (856416, 266793, 1070400, 68139, 67617, 67617, 67617, 67617, 67617, 67617, 67617, 67617, 67617, 67617, 67617, 67617, 67617, 67617, 67617, 91),
-    (596522, 1136993, 1072193, 721156, 70976, 69666, 69666, 69666, 69666, 69666, 69666, 69666, 69666, 69666, 69666, 69666, 69666, 69666, 69666, 127),
-    (201092, 1140034, 723468, 66881, 72768, 71715, 71715, 71715, 71715, 71715, 71715, 71715, 71715, 71715, 71715, 71715, 71715, 71715, 71715, 87),
-    (1583203, 724291, 2756898, 1145363, 2754592, 75008, 73764, 73764, 73764, 73764, 73764, 73764, 73764, 73764, 73764, 73764, 73764, 73764, 73764, 181),
-    (729645, 728132, 2759343, 592439, 327682, 1154048, 2168065, 76304, 75813, 75813, 75813, 75813, 75813, 75813, 75813, 75813, 75813, 75813, 75813, 245),
-    (731694, 1408069, 205216, 2884279, 68676, 727567, 2759189, 1081908, 1149346, 1154306, 78849, 77862, 77862, 77862, 77862, 77862, 77862, 77862, 77862, 89),
-    (328239, 1079654, 2765367, 601216, 1159585, 857349, 74256, 1150082, 597252, 2362371, 79911, 79911, 79911, 79911, 79911, 79911, 79911, 79911, 79911, 76),
-    (1853609, 2883744, 211594, 2242689, 790630, 2165293, 793926, 2169613, 598277, 2698274, 82948, 81960, 81960, 81960, 81960, 81960, 81960, 81960, 81960, 123),
-    (1855848, 1661313, 66632, 2691458, 2098209, 268391, 2956359, 8294, 2766244, 2632101, 84009, 84009, 84009, 84009, 84009, 84009, 84009, 84009, 84009, 123),
-    (740011, 1071234, 68937, 2955651, 794696, 2180260, 1058, 736288, 2369957, 2636801, 2109734, 86058, 86058, 86058, 86058, 86058, 86058, 86058, 86058, 125),
-    (1073708, 792938, 2773252, 216484, 337922, 265507, 2894881, 147718, 2168137, 2176104, 65543, 2178048, 88107, 88107, 88107, 88107, 88107, 88107, 88107, 119),
-    (743844, 339019, 2369898, 2236947, 621898, 6278, 2437417, 2168994, 2232359, 67912, 2099360, 2360585, 2704775, 90156, 90156, 90156, 90156, 90156, 90156, 119),
-    (862316, 2239564, 204975, 799083, 2251878, 866467, 1153386, 328707, 68612, 2643079, 2097680, 5121, 84008, 2167816, 93193, 92205, 92205, 92205, 92205, 93),
-    (1931382, 1603693, 2254982, 76343, 866412, 1092684, 2107956, 2898080, 2359952, 16484, 743985, 2175401, 2179107, 68683, 611331, 332339, 2379018, 2102273, 95236, 77),
-    (606903, 618727, 2901447, 78390, 747945, 2109968, 2780169, 66097, 329765, 2125868, 2239488, 808204, 2183202, 3409956, 613572, 72706, 2104331, 96303, 96303, 238),
-    (887095, 65864, 96401, 80009, 1117224, 873472, 210191, 5121, 2242894, 2110766, 2118060, 7714, 2646059, 2181133, 11309, 74763, 2106403, 99365, 98352, 119),
-    (348833, 688232, 2244873, 877697, 2232482, 2384043, 2196491, 2117635, 2432041, 12295, 97318, 2367524, 29711, 2178350, 26661, 2108461, 100401, 100401, 100401, 119),
-    (755882, 347402, 2116689, 557228, 2908264, 2244739, 2169133, 23600, 2386052, 2101282, 881700, 474155, 2172933, 2242607, 2109478, 2128910, 102450, 102450, 102450, 85),
-    (874610, 2790731, 86188, 6257, 9356, 355409, 2911242, 1131684, 2169262, 273416, 2502694, 19598, 2173040, 621584, 2181159, 2112655, 104499, 104499, 104499, 85),
-    (236012, 3317132, 354820, 2911268, 757765, 2185291, 2789806, 1388586, 2912369, 2436433, 358672, 80906, 2914537, 148486, 2247728, 2180103, 106548, 106548, 106548, 85),
-    (762029, 2794957, 1388974, 221349, 2388997, 2792051, 96299, 295218, 2251846, 2391314, 100519, 86568, 2254097, 2118663, 2113577, 2116656, 108597, 108597, 108597, 85),
-    (633006, 340247, 3321294, 1286448, 3440815, 2390029, 2269745, 1392679, 2373676, 1285393, 88585, 2110803, 2182152, 2122827, 87085, 2117682, 111634, 110646, 110646, 92),
-    (227504, 569447, 1412752, 345167, 1209745, 568391, 2322569, 1134644, 2663560, 2206774, 103529, 628973, 2137101, 91282, 2122762, 2119723, 112695, 112695, 112695, 105),
-    (492064, 2130105, 243865, 381480, 2197521, 2275506, 1127432, 18543, 177193, 87186, 2340362, 240719, 301134, 2201645, 2124846, 90635, 42027, 2204684, 115733, 51),
-    (1116346, 114897, 2277554, 346224, 2130039, 2116754, 2117674, 2275475, 1334451, 2447983, 368684, 2122772, 306767, 2142262, 1141877, 2197518, 2192397, 116793, 116793, 51),
-    (1118386, 2396281, 2279594, 231603, 2118737, 2398251, 3430488, 1278132, 2261036, 2400375, 306316, 1145879, 110765, 95373, 2143247, 2206734, 119864, 118842, 118842, 19),
-    (250099, 2399322, 368683, 2119801, 2400428, 2279442, 232460, 2402357, 2132150, 1277976, 2385965, 95760, 113714, 2389142, 97464, 2145295, 120891, 120891, 120891, 17),
-    (252084, 2400772, 371803, 90629, 2402355, 2252922, 26806, 2452570, 247986, 95251, 2134063, 2149526, 35982, 2328760, 2195472, 113688, 2407567, 122940, 122940, 17),
-    (1058997, 255125, 373852, 354427, 2284557, 2404404, 97364, 94392, 2408506, 374803, 1073202, 2282647, 2202639, 117778, 2125841, 1147953, 2149392, 124989, 124989, 17),
-    (256550, 94390, 240733, 96440, 255126, 310424, 2391095, 2388025, 2285691, 361493, 2138228, 119961, 2131035, 35378, 39985, 2282514, 128051, 127038, 127038, 17),
-    (377383, 178238, 2158703, 2129048, 126007, 176176, 2156729, 382105, 1289846, 35506, 2129980, 2199186, 121877, 38996, 2202652, 2204699, 130074, 129087, 129087, 0),
+    (1067425, 1651074, 539177, 1073570, 1141292, 0, 0, 0, 0, 0, 0, 0, 0, 0, 0, 0, 0, 0, 0, 255),
+    (1067328, 1394818, 1070176, 1065378, 1336107, 2732, 2049, 2049, 2049, 2049, 2049, 2049, 2049, 2049, 2049, 2049, 2049, 2049, 2049, 117),
+    (2296129, 532771, 2818112, 1335979, 1141420, 4098, 4098, 4098, 4098, 4098, 4098, 4098, 4098, 4098, 4098, 4098, 4098, 4098, 4098, 255),
+    (135556, 1402210, 1141029, 65857, 1152353, 7168, 6147, 6147, 6147, 6147, 6147, 6147, 6147, 6147, 6147, 6147, 6147, 6147, 6147, 53),
+    (1073413, 862531, 2824748, 1087490, 1144162, 2296129, 1151232, 9504, 8196, 8196, 8196, 8196, 8196, 8196, 8196, 8196, 8196, 8196, 8196, 91),
+    (537101, 1091908, 540004, 137902, 2824320, 2949154, 2165057, 11266, 10245, 10245, 10245, 10245, 10245, 10245, 10245, 10245, 10245, 10245, 10245, 191),
+    (1077895, 2828357, 729472, 2950468, 661890, 2824720, 1087489, 2165794, 12294, 12294, 12294, 12294, 12294, 12294, 12294, 12294, 12294, 12294, 12294, 83),
+    (537103, 1144960, 2950246, 67845, 267301, 2429037, 2099492, 7428, 15651, 14343, 14343, 14343, 14343, 14343, 14343, 14343, 14343, 14343, 14343, 74),
+    (649, 2294185, 211329, 791969, 2765030, 530757, 2112674, 351523, 140645, 17700, 16392, 16392, 16392, 16392, 16392, 16392, 16392, 16392, 16392, 117),
+    (789002, 2835016, 131362, 269665, 735403, 210339, 861254, 2243616, 2173253, 2106370, 18441, 18441, 18441, 18441, 18441, 18441, 18441, 18441, 18441, 251),
+    (397641, 2312747, 2167308, 672131, 2834433, 1666531, 2957572, 2228320, 212001, 2633766, 535559, 21541, 20490, 20490, 20490, 20490, 20490, 20490, 20490, 87),
+    (151692, 1139075, 9578, 1402953, 71076, 2232882, 2172933, 148841, 537640, 3363, 2295840, 2700288, 2701575, 22539, 22539, 22539, 22539, 22539, 22539, 117),
+    (878923, 2840740, 1087877, 151619, 2173956, 2314374, 674851, 201266, 2102694, 2701447, 3113, 2179080, 2164736, 25632, 24588, 24588, 24588, 24588, 24588, 255),
+    (680469, 1667077, 930924, 677892, 2317348, 802214, 2963459, 2169162, 345125, 1130, 2181129, 70688, 2113601, 2165762, 26637, 26637, 26637, 26637, 26637, 61),
+    (2845005, 342182, 207180, 869740, 393744, 543750, 74759, 154793, 2106376, 2107923, 152875, 1378434, 138272, 2168106, 2100259, 28686, 28686, 28686, 28686, 109),
+    (997390, 280744, 143629, 2444295, 3762208, 1051656, 549061, 2192545, 2176101, 75052, 2097154, 2237602, 20491, 2710570, 2168835, 30735, 30735, 30735, 30735, 204),
+    (886920, 1320, 2324559, 282793, 2119, 2115918, 2178081, 2164138, 2715915, 682022, 2240514, 2190370, 137221, 2187276, 2173987, 9259, 33828, 32784, 32784, 87),
+    (215120, 2326666, 2969601, 5129, 809000, 2447439, 2429999, 1195016, 554017, 2308268, 2121830, 92195, 74765, 2110596, 2172933, 2192387, 34833, 34833, 34833, 117),
+    (166346, 2969907, 266379, 2448497, 688201, 2182178, 16387, 353648, 556136, 2122787, 2451469, 14532, 2170894, 2177701, 79022, 2194438, 37893, 36882, 36882, 85),
+    (692619, 3380651, 6412, 2449482, 167018, 206129, 18573, 338318, 164969, 2327597, 2453510, 2168872, 2176005, 97284, 2127943, 2178056, 38931, 38931, 38931, 117),
+    (286997, 2581075, 1057907, 813067, 3379538, 2976142, 2316325, 2453514, 2315397, 165897, 78255, 2391076, 2313222, 278567, 2719760, 2112561, 42024, 40980, 40980, 85),
+    (289108, 10550, 816500, 2453587, 91685, 359795, 153798, 2128908, 692872, 2200678, 623917, 101419, 2177031, 87312, 2442321, 2115625, 44042, 43029, 43029, 91),
+    (698574, 2323765, 172688, 1062925, 2859439, 1219757, 25224, 2178063, 2458668, 2857137, 85224, 2508806, 153610, 37931, 2176042, 2133042, 45078, 45078, 45078, 52),
+    (162192, 2586934, 1327623, 2570318, 362773, 3372054, 2195533, 2320553, 282644, 25908, 3232821, 2132243, 37939, 2180140, 23730, 2186249, 47127, 47127, 47127, 68),
+    (164352, 1114265, 380144, 363271, 2394199, 1067087, 2340904, 1257618, 177263, 2181130, 2338830, 2114738, 2183221, 38923, 2271756, 2188398, 27827, 2189332, 2186292, 51),
+    (428120, 1067154, 2329720, 33833, 2461834, 1328176, 178323, 31786, 2342067, 2447435, 1073702, 42095, 177196, 29748, 93302, 2191381, 2124853, 51225, 51225, 51),
+    (1052818, 1118297, 2346162, 301066, 2463768, 2183249, 88144, 2343060, 2198028, 2466860, 2326615, 43181, 31863, 3374091, 177333, 2386998, 2191374, 53274, 53274, 17),
+    (301146, 2333818, 182420, 2465803, 2345004, 1124370, 306219, 2199633, 2467885, 2121784, 2328630, 291981, 2453527, 2195536, 2147383, 2127919, 56342, 55323, 55323, 17),
+    (1056916, 2465883, 1387643, 305164, 2467930, 2348076, 288790, 2469939, 2267288, 356370, 47193, 1342478, 2210937, 35885, 2331704, 3247215, 2195472, 57372, 57372, 17),
+    (188933, 371365, 2351117, 172182, 2469979, 2204693, 2349208, 2125934, 184471, 2472591, 105594, 2137272, 36953, 101433, 99373, 2133042, 2194448, 59421, 59421, 17),
+    (438365, 2353671, 311310, 188437, 2351255, 2337423, 2472020, 187576, 2193968, 2208891, 2192436, 184377, 2348048, 2394289, 36915, 2149426, 62483, 61470, 61470, 17),
+    (311879, 440350, 2603215, 2475070, 2324509, 1224729, 3506192, 2602045, 58553, 363580, 2271861, 3442772, 1347611, 2335803, 54962, 39994, 64563, 63519, 63519, 0),
+    (670248, 1312929, 1380872, 1135153, 1141262, 1075493, 65568, 65568, 65568, 65568, 65568, 65568, 65568, 65568, 65568, 65568, 65568, 65568, 65568, 230),
+    (332034, 596530, 66218, 1073223, 2228747, 67617, 67617, 67617, 67617, 67617, 67617, 67617, 67617, 67617, 67617, 67617, 67617, 67617, 67617, 119),
+    (199338, 530851, 2230827, 539275, 1141388, 2163008, 69666, 69666, 69666, 69666, 69666, 69666, 69666, 69666, 69666, 69666, 69666, 69666, 69666, 247),
+    (1333803, 1057122, 2756748, 723629, 1217857, 328207, 72704, 71715, 71715, 71715, 71715, 71715, 71715, 71715, 71715, 71715, 71715, 71715, 71715, 127),
+    (203308, 1336643, 201478, 2757166, 852257, 1342465, 1086464, 73764, 73764, 73764, 73764, 73764, 73764, 73764, 73764, 73764, 73764, 73764, 73764, 117),
+    (274532, 2761229, 203438, 2759072, 70287, 1090944, 2626099, 1146881, 76833, 75813, 75813, 75813, 75813, 75813, 75813, 75813, 75813, 75813, 75813, 85),
+    (356453, 1145095, 853829, 2359396, 1079831, 68932, 728193, 70723, 1090064, 2626098, 77862, 77862, 77862, 77862, 77862, 77862, 77862, 77862, 77862, 101),
+    (602272, 732544, 1208737, 2633089, 1094198, 2109476, 2629794, 530509, 2169986, 79911, 79911, 79911, 79911, 79911, 79911, 79911, 79911, 79911, 79911, 116),
+    (555488, 211081, 2228785, 734279, 1272194, 2765858, 858145, 207140, 2100227, 2237765, 82091, 81960, 81960, 81960, 81960, 81960, 81960, 81960, 81960, 255),
+    (723048, 2245170, 1246465, 856423, 334978, 337408, 2891015, 616550, 2109797, 2106629, 84009, 84009, 84009, 84009, 84009, 84009, 84009, 84009, 84009, 116),
+    (332587, 737609, 2101283, 2365604, 3336, 196615, 13607, 2229252, 2164741, 2176041, 87077, 86058, 86058, 86058, 86058, 86058, 86058, 86058, 86058, 89),
+    (203114, 337155, 1142090, 149602, 2101778, 67973, 737574, 2493477, 2897028, 80937, 2635808, 2114560, 88107, 88107, 88107, 88107, 88107, 88107, 88107, 155),
+    (354788, 2775339, 797956, 217510, 2249893, 2371683, 2103719, 2898018, 555017, 67616, 83009, 2098568, 2182146, 90156, 90156, 90156, 90156, 90156, 90156, 157),
+    (862510, 2369900, 2777510, 2110351, 1089636, 867332, 1153355, 65576, 2898026, 1146883, 2376832, 2317642, 2168834, 1116169, 2100322, 93481, 92205, 92205, 92205, 215),
+    (340783, 1866093, 867782, 345165, 1097095, 10348, 2901068, 204832, 2097680, 1090564, 280843, 329763, 1151274, 2100261, 2444298, 201771, 2102275, 94254, 94254, 95),
+    (868839, 3174702, 1160455, 223334, 1094792, 263750, 3697033, 338081, 2163905, 615493, 1052740, 21772, 2168963, 2182180, 2166827, 2184203, 96303, 96303, 96303, 54),
+    (213681, 2507186, 65961, 2115951, 300495, 2087, 2098721, 209262, 135562, 2241543, 203435, 615458, 2445357, 2104397, 2256932, 11531, 2106636, 99365, 98352, 119),
+    (1002162, 230793, 2785426, 329768, 752010, 2100232, 2783330, 350247, 2183596, 77955, 2382919, 225316, 2102404, 2169862, 2121837, 2107621, 2126861, 100401, 100401, 87),
+    (807281, 72785, 350636, 3360841, 622632, 2383184, 335874, 2167151, 552068, 2122824, 29775, 77863, 2112558, 11270, 2190373, 2104362, 102450, 102450, 102450, 115),
+    (565618, 876579, 480850, 335883, 232491, 2788483, 3417162, 1264013, 2189445, 558348, 2173094, 96398, 2719784, 2247726, 2371623, 2128904, 105479, 104499, 104499, 85),
+    (759980, 2791701, 92324, 219506, 2266253, 338955, 217486, 2384900, 143792, 2107697, 2191407, 2264336, 343078, 82954, 1133575, 2114575, 107529, 106548, 106548, 117),
+    (762029, 3318925, 1284142, 2912421, 2267824, 882796, 208946, 1269136, 345164, 2129234, 86321, 2109479, 2108427, 2112529, 19466, 2182152, 108597, 108597, 108597, 117),
+    (239918, 2912791, 886101, 762031, 3319440, 344173, 760847, 2791857, 90118, 80434, 1133606, 273415, 2377771, 21640, 2133004, 2124875, 2184210, 110646, 110646, 85),
+    (752048, 2916918, 345622, 211121, 225714, 2730261, 1395720, 2242868, 2378770, 1331309, 2129101, 2662444, 2252843, 3232019, 2133006, 3169331, 112695, 112695, 112695, 100),
+    (378992, 1049089, 243866, 2459793, 241817, 18578, 225826, 82474, 2117811, 2114647, 3175474, 2273423, 2182163, 2129963, 108557, 2194453, 91181, 2119700, 2122804, 51),
+    (245809, 2277530, 99537, 280722, 367632, 21554, 350327, 97834, 369811, 91215, 3170357, 2119734, 225325, 2182231, 2143253, 2126861, 117780, 116793, 116793, 51),
+    (299129, 1120770, 87129, 231603, 245931, 2118803, 2278923, 2132148, 91186, 370736, 245260, 2401296, 227501, 111765, 2386959, 2191502, 2143255, 118842, 118842, 49),
+    (250531, 1136819, 2399322, 370187, 248324, 370866, 2280596, 90161, 246381, 2264213, 373848, 2135053, 2388526, 30775, 2122799, 2195472, 2405399, 120891, 120891, 17),
+    (368763, 371803, 91156, 249907, 27797, 2283020, 1061907, 247990, 234158, 2389081, 99437, 245775, 2132017, 310290, 2147344, 2405423, 123959, 122940, 122940, 17),
+    (289013, 186550, 253966, 2140211, 2285588, 2191511, 358416, 103547, 2405428, 2127994, 2195505, 52250, 2346066, 50359, 2133011, 2190392, 124989, 124989, 124989, 17),
+    (309430, 2404476, 311813, 96277, 2472027, 302133, 2127886, 107153, 2139182, 2285661, 2350205, 2201616, 249874, 2196536, 117809, 2151449, 128050, 127038, 127038, 17),
+    (1077495, 2275390, 241816, 1346646, 174137, 2337945, 2198712, 2269236, 122931, 32922, 2195506, 2159635, 97308, 2134043, 60475, 2128957, 130106, 129087, 129087, 0),
 )
 EVENTS = 2 * (len(PLAN[0]) - 1)
 ROWS = 256

time: 69.8 us -> 67.5 us (0.967)
  Pallas kernels: 67.8 us -> 65 us
    pallas_call x1, Pallas kernels: 67.8 us -> 65 us  [per_device(): pl.pallas_call(kernel, name='face_attention', out_shape=jax.ShapeDtypeStr...]
where the time goes in v5:
time: 67.5 us; the launch traced here: 66.6 us
  Pallas kernels  65 us (96%)
  local copies, waits for them, and re-layouts  1.57 us (2%)
    pallas_call x1, Pallas kernels, per_device(): pl.pallas_call(kernel, name='face_attention', out_shape=jax.ShapeDtypeStr...  65 us
    unnamed x1, local copies, waits for them, and re-layouts  1.57 us

profile of v5, /device:TPU:5, one launch (start us, length us, event | category | flops | bytes accessed | tf_op | source)
XLA Modules:
  0.0 66.6 jit_solution(16790844403599688165)
XLA Ops:
  0.0 65.0 %face_attention.1 = bf16[256,256]{1,0:T(8,128)(2,1)} custom-call(bf16[256,256]{1,0:T(8,128)(2,1)} %x_hbm.1, f32[1,1024]{1,0:T(1,128)} %bitcast.4, bf16[3,1024,256]{2,1,0:T(8,128)(2,1)} %bitcast.3, bf16[256,1024]{1,0:T(8,128)(2,1)} %wout_hbm.1, s32[2,128]{1,0:T(2,128)} %bitcast.5), custom_call_target="tpu_custom_call" | custom-call | tf_op jit(solution)/shard_map/face_attention/pallas_call | solution.py:389
  65.0 1.6 %copy.7 = bf16[256,256]{1,0:T(8,128)(2,1)} copy(bf16[256,256]{1,0:T(8,128)(2,1)} %face_attention.1) | data formatting | bytes 262144

commit v6 on v5

--- a/solution.py
+++ b/solution.py
@@ -13,70 +13,70 @@
 epsilon = 1e-05
 masked_score = -1e30
 PLAN = (
-    (1067425, 1651074, 539177, 1073570, 1141292, 0, 0, 0, 0, 0, 0, 0, 0, 0, 0, 0, 0, 0, 0, 255),
-    (1067328, 1394818, 1070176, 1065378, 1336107, 2732, 2049, 2049, 2049, 2049, 2049, 2049, 2049, 2049, 2049, 2049, 2049, 2049, 2049, 117),
-    (2296129, 532771, 2818112, 1335979, 1141420, 4098, 4098, 4098, 4098, 4098, 4098, 4098, 4098, 4098, 4098, 4098, 4098, 4098, 4098, 255),
-    (135556, 1402210, 1141029, 65857, 1152353, 7168, 6147, 6147, 6147, 6147, 6147, 6147, 6147, 6147, 6147, 6147, 6147, 6147, 6147, 53),
-    (1073413, 862531, 2824748, 1087490, 1144162, 2296129, 1151232, 9504, 8196, 8196, 8196, 8196, 8196, 8196, 8196, 8196, 8196, 8196, 8196, 91),
-    (537101, 1091908, 540004, 137902, 2824320, 2949154, 2165057, 11266, 10245, 10245, 10245, 10245, 10245, 10245, 10245, 10245, 10245, 10245, 10245, 191),
-    (1077895, 2828357, 729472, 2950468, 661890, 2824720, 1087489, 2165794, 12294, 12294, 12294, 12294, 12294, 12294, 12294, 12294, 12294, 12294, 12294, 83),
-    (537103, 1144960, 2950246, 67845, 267301, 2429037, 2099492, 7428, 15651, 14343, 14343, 14343, 14343, 14343, 14343, 14343, 14343, 14343, 14343, 74),
-    (649, 2294185, 211329, 791969, 2765030, 530757, 2112674, 351523, 140645, 17700, 16392, 16392, 16392, 16392, 16392, 16392, 16392, 16392, 16392, 117),
-    (789002, 2835016, 131362, 269665, 735403, 210339, 861254, 2243616, 2173253, 2106370, 18441, 18441, 18441, 18441, 18441, 18441, 18441, 18441, 18441, 251),
-    (397641, 2312747, 2167308, 672131, 2834433, 1666531, 2957572, 2228320, 212001, 2633766, 535559, 21541, 20490, 20490, 20490, 20490, 20490, 20490, 20490, 87),
-    (151692, 1139075, 9578, 1402953, 71076, 2232882, 2172933, 148841, 537640, 3363, 2295840, 2700288, 2701575, 22539, 22539, 22539, 22539, 22539, 22539, 117),
-    (878923, 2840740, 1087877, 151619, 2173956, 2314374, 674851, 201266, 2102694, 2701447, 3113, 2179080, 2164736, 25632, 24588, 24588, 24588, 24588, 24588, 255),
-    (680469, 1667077, 930924, 677892, 2317348, 802214, 2963459, 2169162, 345125, 1130, 2181129, 70688, 2113601, 2165762, 26637, 26637, 26637, 26637, 26637, 61),
-    (2845005, 342182, 207180, 869740, 393744, 543750, 74759, 154793, 2106376, 2107923, 152875, 1378434, 138272, 2168106, 2100259, 28686, 28686, 28686, 28686, 109),
-    (997390, 280744, 143629, 2444295, 3762208, 1051656, 549061, 2192545, 2176101, 75052, 2097154, 2237602, 20491, 2710570, 2168835, 30735, 30735, 30735, 30735, 204),
-    (886920, 1320, 2324559, 282793, 2119, 2115918, 2178081, 2164138, 2715915, 682022, 2240514, 2190370, 137221, 2187276, 2173987, 9259, 33828, 32784, 32784, 87),
-    (215120, 2326666, 2969601, 5129, 809000, 2447439, 2429999, 1195016, 554017, 2308268, 2121830, 92195, 74765, 2110596, 2172933, 2192387, 34833, 34833, 34833, 117),
-    (166346, 2969907, 266379, 2448497, 688201, 2182178, 16387, 353648, 556136, 2122787, 2451469, 14532, 2170894, 2177701, 79022, 2194438, 37893, 36882, 36882, 85),
-    (692619, 3380651, 6412, 2449482, 167018, 206129, 18573, 338318, 164969, 2327597, 2453510, 2168872, 2176005, 97284, 2127943, 2178056, 38931, 38931, 38931, 117),
-    (286997, 2581075, 1057907, 813067, 3379538, 2976142, 2316325, 2453514, 2315397, 165897, 78255, 2391076, 2313222, 278567, 2719760, 2112561, 42024, 40980, 40980, 85),
-    (289108, 10550, 816500, 2453587, 91685, 359795, 153798, 2128908, 692872, 2200678, 623917, 101419, 2177031, 87312, 2442321, 2115625, 44042, 43029, 43029, 91),
-    (698574, 2323765, 172688, 1062925, 2859439, 1219757, 25224, 2178063, 2458668, 2857137, 85224, 2508806, 153610, 37931, 2176042, 2133042, 45078, 45078, 45078, 52),
-    (162192, 2586934, 1327623, 2570318, 362773, 3372054, 2195533, 2320553, 282644, 25908, 3232821, 2132243, 37939, 2180140, 23730, 2186249, 47127, 47127, 47127, 68),
-    (164352, 1114265, 380144, 363271, 2394199, 1067087, 2340904, 1257618, 177263, 2181130, 2338830, 2114738, 2183221, 38923, 2271756, 2188398, 27827, 2189332, 2186292, 51),
-    (428120, 1067154, 2329720, 33833, 2461834, 1328176, 178323, 31786, 2342067, 2447435, 1073702, 42095, 177196, 29748, 93302, 2191381, 2124853, 51225, 51225, 51),
-    (1052818, 1118297, 2346162, 301066, 2463768, 2183249, 88144, 2343060, 2198028, 2466860, 2326615, 43181, 31863, 3374091, 177333, 2386998, 2191374, 53274, 53274, 17),
-    (301146, 2333818, 182420, 2465803, 2345004, 1124370, 306219, 2199633, 2467885, 2121784, 2328630, 291981, 2453527, 2195536, 2147383, 2127919, 56342, 55323, 55323, 17),
-    (1056916, 2465883, 1387643, 305164, 2467930, 2348076, 288790, 2469939, 2267288, 356370, 47193, 1342478, 2210937, 35885, 2331704, 3247215, 2195472, 57372, 57372, 17),
-    (188933, 371365, 2351117, 172182, 2469979, 2204693, 2349208, 2125934, 184471, 2472591, 105594, 2137272, 36953, 101433, 99373, 2133042, 2194448, 59421, 59421, 17),
-    (438365, 2353671, 311310, 188437, 2351255, 2337423, 2472020, 187576, 2193968, 2208891, 2192436, 184377, 2348048, 2394289, 36915, 2149426, 62483, 61470, 61470, 17),
-    (311879, 440350, 2603215, 2475070, 2324509, 1224729, 3506192, 2602045, 58553, 363580, 2271861, 3442772, 1347611, 2335803, 54962, 39994, 64563, 63519, 63519, 0),
-    (670248, 1312929, 1380872, 1135153, 1141262, 1075493, 65568, 65568, 65568, 65568, 65568, 65568, 65568, 65568, 65568, 65568, 65568, 65568, 65568, 230),
-    (332034, 596530, 66218, 1073223, 2228747, 67617, 67617, 67617, 67617, 67617, 67617, 67617, 67617, 67617, 67617, 67617, 67617, 67617, 67617, 119),
-    (199338, 530851, 2230827, 539275, 1141388, 2163008, 69666, 69666, 69666, 69666, 69666, 69666, 69666, 69666, 69666, 69666, 69666, 69666, 69666, 247),
-    (1333803, 1057122, 2756748, 723629, 1217857, 328207, 72704, 71715, 71715, 71715, 71715, 71715, 71715, 71715, 71715, 71715, 71715, 71715, 71715, 127),
-    (203308, 1336643, 201478, 2757166, 852257, 1342465, 1086464, 73764, 73764, 73764, 73764, 73764, 73764, 73764, 73764, 73764, 73764, 73764, 73764, 117),
-    (274532, 2761229, 203438, 2759072, 70287, 1090944, 2626099, 1146881, 76833, 75813, 75813, 75813, 75813, 75813, 75813, 75813, 75813, 75813, 75813, 85),
-    (356453, 1145095, 853829, 2359396, 1079831, 68932, 728193, 70723, 1090064, 2626098, 77862, 77862, 77862, 77862, 77862, 77862, 77862, 77862, 77862, 101),
-    (602272, 732544, 1208737, 2633089, 1094198, 2109476, 2629794, 530509, 2169986, 79911, 79911, 79911, 79911, 79911, 79911, 79911, 79911, 79911, 79911, 116),
-    (555488, 211081, 2228785, 734279, 1272194, 2765858, 858145, 207140, 2100227, 2237765, 82091, 81960, 81960, 81960, 81960, 81960, 81960, 81960, 81960, 255),
-    (723048, 2245170, 1246465, 856423, 334978, 337408, 2891015, 616550, 2109797, 2106629, 84009, 84009, 84009, 84009, 84009, 84009, 84009, 84009, 84009, 116),
-    (332587, 737609, 2101283, 2365604, 3336, 196615, 13607, 2229252, 2164741, 2176041, 87077, 86058, 86058, 86058, 86058, 86058, 86058, 86058, 86058, 89),
-    (203114, 337155, 1142090, 149602, 2101778, 67973, 737574, 2493477, 2897028, 80937, 2635808, 2114560, 88107, 88107, 88107, 88107, 88107, 88107, 88107, 155),
-    (354788, 2775339, 797956, 217510, 2249893, 2371683, 2103719, 2898018, 555017, 67616, 83009, 2098568, 2182146, 90156, 90156, 90156, 90156, 90156, 90156, 157),
-    (862510, 2369900, 2777510, 2110351, 1089636, 867332, 1153355, 65576, 2898026, 1146883, 2376832, 2317642, 2168834, 1116169, 2100322, 93481, 92205, 92205, 92205, 215),
-    (340783, 1866093, 867782, 345165, 1097095, 10348, 2901068, 204832, 2097680, 1090564, 280843, 329763, 1151274, 2100261, 2444298, 201771, 2102275, 94254, 94254, 95),
-    (868839, 3174702, 1160455, 223334, 1094792, 263750, 3697033, 338081, 2163905, 615493, 1052740, 21772, 2168963, 2182180, 2166827, 2184203, 96303, 96303, 96303, 54),
-    (213681, 2507186, 65961, 2115951, 300495, 2087, 2098721, 209262, 135562, 2241543, 203435, 615458, 2445357, 2104397, 2256932, 11531, 2106636, 99365, 98352, 119),
-    (1002162, 230793, 2785426, 329768, 752010, 2100232, 2783330, 350247, 2183596, 77955, 2382919, 225316, 2102404, 2169862, 2121837, 2107621, 2126861, 100401, 100401, 87),
-    (807281, 72785, 350636, 3360841, 622632, 2383184, 335874, 2167151, 552068, 2122824, 29775, 77863, 2112558, 11270, 2190373, 2104362, 102450, 102450, 102450, 115),
-    (565618, 876579, 480850, 335883, 232491, 2788483, 3417162, 1264013, 2189445, 558348, 2173094, 96398, 2719784, 2247726, 2371623, 2128904, 105479, 104499, 104499, 85),
-    (759980, 2791701, 92324, 219506, 2266253, 338955, 217486, 2384900, 143792, 2107697, 2191407, 2264336, 343078, 82954, 1133575, 2114575, 107529, 106548, 106548, 117),
-    (762029, 3318925, 1284142, 2912421, 2267824, 882796, 208946, 1269136, 345164, 2129234, 86321, 2109479, 2108427, 2112529, 19466, 2182152, 108597, 108597, 108597, 117),
-    (239918, 2912791, 886101, 762031, 3319440, 344173, 760847, 2791857, 90118, 80434, 1133606, 273415, 2377771, 21640, 2133004, 2124875, 2184210, 110646, 110646, 85),
-    (752048, 2916918, 345622, 211121, 225714, 2730261, 1395720, 2242868, 2378770, 1331309, 2129101, 2662444, 2252843, 3232019, 2133006, 3169331, 112695, 112695, 112695, 100),
-    (378992, 1049089, 243866, 2459793, 241817, 18578, 225826, 82474, 2117811, 2114647, 3175474, 2273423, 2182163, 2129963, 108557, 2194453, 91181, 2119700, 2122804, 51),
-    (245809, 2277530, 99537, 280722, 367632, 21554, 350327, 97834, 369811, 91215, 3170357, 2119734, 225325, 2182231, 2143253, 2126861, 117780, 116793, 116793, 51),
-    (299129, 1120770, 87129, 231603, 245931, 2118803, 2278923, 2132148, 91186, 370736, 245260, 2401296, 227501, 111765, 2386959, 2191502, 2143255, 118842, 118842, 49),
-    (250531, 1136819, 2399322, 370187, 248324, 370866, 2280596, 90161, 246381, 2264213, 373848, 2135053, 2388526, 30775, 2122799, 2195472, 2405399, 120891, 120891, 17),
-    (368763, 371803, 91156, 249907, 27797, 2283020, 1061907, 247990, 234158, 2389081, 99437, 245775, 2132017, 310290, 2147344, 2405423, 123959, 122940, 122940, 17),
-    (289013, 186550, 253966, 2140211, 2285588, 2191511, 358416, 103547, 2405428, 2127994, 2195505, 52250, 2346066, 50359, 2133011, 2190392, 124989, 124989, 124989, 17),
-    (309430, 2404476, 311813, 96277, 2472027, 302133, 2127886, 107153, 2139182, 2285661, 2350205, 2201616, 249874, 2196536, 117809, 2151449, 128050, 127038, 127038, 17),
-    (1077495, 2275390, 241816, 1346646, 174137, 2337945, 2198712, 2269236, 122931, 32922, 2195506, 2159635, 97308, 2134043, 60475, 2128957, 130106, 129087, 129087, 0),
+    (788743, 854536, 1585801, 1132930, 600994, 1153101, 564, 0, 0, 0, 0, 0, 0, 0, 0, 0, 0, 0, 0, 247),
+    (655490, 1905321, 214368, 1073331, 2573, 2049, 2049, 2049, 2049, 2049, 2049, 2049, 2049, 2049, 2049, 2049, 2049, 2049, 2049, 119),
+    (657930, 2820387, 1083456, 2687628, 606387, 4098, 4098, 4098, 4098, 4098, 4098, 4098, 4098, 4098, 4098, 4098, 4098, 4098, 4098, 123),
+    (659748, 1138018, 1335827, 657964, 1086561, 1141056, 7264, 6147, 6147, 6147, 6147, 6147, 6147, 6147, 6147, 6147, 6147, 6147, 6147, 181),
+    (286787, 1156451, 528941, 2298451, 2820353, 1079552, 9248, 8196, 8196, 8196, 8196, 8196, 8196, 8196, 8196, 8196, 8196, 8196, 8196, 125),
+    (139789, 2826797, 2824515, 594575, 595, 593184, 1084417, 11266, 10245, 10245, 10245, 10245, 10245, 10245, 10245, 10245, 10245, 10245, 10245, 217),
+    (665863, 2828847, 1341517, 663936, 2303136, 788547, 1082401, 543284, 1148195, 1087490, 13346, 12294, 12294, 12294, 12294, 12294, 12294, 12294, 12294, 213),
+    (786758, 2425391, 265254, 2427141, 266377, 158821, 533922, 531748, 15395, 14343, 14343, 14343, 14343, 14343, 14343, 14343, 14343, 14343, 14343, 203),
+    (346761, 2424832, 806983, 2951553, 2308166, 530562, 2432358, 142370, 1155332, 2696549, 16392, 16392, 16392, 16392, 16392, 16392, 16392, 16392, 16392, 127),
+    (147850, 3624, 525601, 268322, 2162759, 669091, 2833410, 368772, 2700708, 2697221, 18441, 18441, 18441, 18441, 18441, 18441, 18441, 18441, 18441, 247),
+    (69705, 1084777, 2435, 2431048, 2296834, 2957444, 669792, 144424, 2098471, 77094, 21509, 20490, 20490, 20490, 20490, 20490, 20490, 20490, 20490, 91),
+    (1087939, 1138762, 1086826, 4228, 1665353, 2170276, 2168169, 540673, 11297, 340096, 3343525, 2179143, 2110759, 22539, 22539, 22539, 22539, 22539, 22539, 213),
+    (551243, 1155268, 2695853, 1088619, 2168835, 135498, 272390, 2962538, 2435145, 16385, 343145, 1057, 2167840, 2112552, 24588, 24588, 24588, 24588, 24588, 125),
+    (76140, 154700, 205190, 2108582, 279556, 867691, 151619, 2183746, 1250, 1084840, 19491, 2182176, 3079, 27681, 26637, 26637, 26637, 26637, 26637, 251),
+    (1145222, 1731343, 2569325, 803143, 10572, 2964588, 2305448, 1155600, 678016, 8752, 2162985, 265252, 2316291, 2165795, 4106, 2167817, 29738, 28686, 28686, 68),
+    (473480, 13480, 18701, 2713600, 2307241, 2111502, 666784, 545036, 3372, 2173998, 5281, 2166795, 8739, 2186410, 2104356, 30735, 30735, 30735, 30735, 230),
+    (147857, 3097009, 686112, 281711, 146601, 2177290, 2969665, 12622, 2166126, 284674, 6413, 142701, 2098214, 2448418, 8204, 2173987, 2171948, 32784, 32784, 119),
+    (164233, 2444656, 147731, 2969866, 1315944, 2297889, 686219, 1679488, 2448751, 2562051, 8199, 2177094, 91137, 2121742, 2716710, 93220, 2123781, 35877, 34833, 119),
+    (1214867, 1315242, 810353, 893008, 85163, 2118768, 268296, 2310276, 2166956, 2171397, 2121807, 146441, 2324494, 2169133, 2911271, 2172934, 2192422, 36882, 36882, 85),
+    (809554, 2855348, 1121515, 165900, 271363, 2852970, 689324, 272585, 354446, 2172208, 2436237, 1262697, 2978888, 31754, 12295, 2176047, 39975, 38931, 38931, 91),
+    (942675, 2856964, 155052, 1321298, 2855054, 2185357, 2172581, 2978129, 2314442, 2189446, 2438513, 620560, 2195465, 2313231, 81959, 2245639, 40980, 40980, 40980, 181),
+    (92500, 1059214, 2436468, 2977875, 2121836, 2123814, 558214, 23923, 561167, 2317743, 1215858, 343216, 22151, 2722922, 81929, 2114601, 43029, 43029, 43029, 85),
+    (698830, 2338286, 2109478, 696976, 2455695, 28276, 278192, 90195, 16689, 2123123, 88201, 2190375, 2179122, 21521, 2182155, 2184210, 45078, 45078, 45078, 85),
+    (686480, 570607, 2732103, 2309552, 16974, 3371025, 568497, 2179149, 281653, 42221, 2203717, 156713, 563754, 2727050, 2318482, 2199563, 48171, 47127, 47127, 68),
+    (313424, 379424, 17456, 297047, 2340873, 300209, 2179590, 2127919, 2182322, 2338902, 1118218, 159763, 2192426, 88085, 2205805, 2123788, 2120755, 2187284, 50228, 51),
+    (180241, 2198648, 18578, 2181200, 2327074, 179378, 2341011, 21555, 1335467, 162858, 2325643, 176180, 2339860, 2449429, 27701, 2189326, 52270, 51225, 51225, 51),
+    (299522, 2345049, 1070258, 180243, 2184627, 2342961, 32939, 1074315, 2195604, 306257, 2203735, 2342060, 46261, 2127919, 95286, 2123821, 54286, 53274, 53274, 17),
+    (1120346, 2347187, 23044, 183467, 2203796, 306195, 25721, 2449458, 2467928, 2134065, 2189325, 164920, 2131990, 48240, 291894, 2210990, 2193423, 55323, 55323, 17),
+    (303748, 1058907, 306299, 24666, 105653, 2204794, 2187405, 3237913, 37014, 291961, 50226, 2469905, 47759, 33838, 2212913, 2327571, 2210991, 57372, 57372, 17),
+    (305797, 1124444, 2352373, 41510, 187021, 2189462, 2349198, 2470964, 2191450, 2347159, 32783, 104472, 168979, 117944, 2200623, 2149559, 2195505, 60433, 59421, 17),
+    (307878, 2353245, 2469980, 28823, 43160, 2475125, 2351151, 173071, 2473006, 313435, 101499, 2213978, 104464, 2335761, 2348080, 2134066, 62483, 61470, 61470, 17),
+    (440839, 311847, 2603038, 2475070, 313360, 59407, 2223215, 2476118, 58486, 298032, 175153, 1086581, 2221746, 172051, 56371, 54331, 2204730, 63519, 63519, 0),
+    (1130657, 1077775, 858241, 266761, 332334, 1073707, 610860, 66093, 65568, 65568, 65568, 65568, 65568, 65568, 65568, 65568, 65568, 65568, 65568, 119),
+    (197161, 2752898, 1083555, 1399338, 1142946, 1401392, 68492, 67617, 67617, 67617, 67617, 67617, 67617, 67617, 67617, 67617, 67617, 67617, 67617, 119),
+    (1397155, 1398881, 1072449, 1138720, 288064, 69666, 69666, 69666, 69666, 69666, 69666, 69666, 69666, 69666, 69666, 69666, 69666, 69666, 69666, 181),
+    (1137444, 1401186, 200002, 1140876, 537921, 1077312, 1084448, 72207, 71715, 71715, 71715, 71715, 71715, 71715, 71715, 71715, 71715, 71715, 71715, 91),
+    (727333, 1140035, 274572, 201261, 1339957, 328770, 2164737, 1084303, 74752, 73764, 73764, 73764, 73764, 73764, 73764, 73764, 73764, 73764, 73764, 151),
+    (1403270, 1419620, 204100, 1339552, 1342787, 2621538, 2232577, 77089, 75813, 75813, 75813, 75813, 75813, 75813, 75813, 75813, 75813, 75813, 75813, 87),
+    (731694, 1145486, 243525, 852589, 1341540, 2884676, 596501, 2759073, 2361634, 78850, 77862, 77862, 77862, 77862, 77862, 77862, 77862, 77862, 77862, 53),
+    (78511, 1472672, 2635136, 1208872, 600225, 2632240, 1081910, 2361869, 529261, 71716, 2167346, 2104580, 80404, 79911, 79911, 79911, 79911, 79911, 79911, 68),
+    (555488, 1274505, 736512, 2242594, 602497, 2625835, 335174, 75812, 2366625, 349445, 82948, 81960, 81960, 81960, 81960, 81960, 81960, 81960, 81960, 127),
+    (1083496, 1904993, 2245761, 1147051, 196899, 1663854, 212098, 336896, 2890823, 12325, 2107660, 2700676, 84009, 84009, 84009, 84009, 84009, 84009, 84009, 125),
+    (1399202, 1595753, 2771107, 860588, 2365537, 2102273, 196936, 862509, 211246, 2893127, 2229381, 537704, 87462, 86058, 86058, 86058, 86058, 86058, 86058, 93),
+    (217772, 336259, 201802, 740269, 2232485, 2169929, 200069, 2231428, 2371750, 1083656, 604192, 2098439, 89128, 88107, 88107, 88107, 88107, 88107, 88107, 127),
+    (743597, 2251044, 553125, 2894051, 2103402, 2367750, 2962506, 79970, 606313, 2636866, 556105, 68113, 2100488, 2162688, 90156, 90156, 90156, 90156, 90156, 207),
+    (600629, 745774, 2369678, 2437510, 743524, 2251175, 345156, 2252835, 2898947, 2900330, 263498, 70816, 67881, 2100226, 93193, 92205, 92205, 92205, 92205, 95),
+    (1141222, 867661, 10664, 2898453, 328840, 678252, 2316388, 2098252, 18530, 2173954, 86017, 2106401, 7178, 2182150, 95267, 94254, 94254, 94254, 94254, 251),
+    (997742, 3175080, 2901447, 209456, 1081376, 1076224, 806086, 264293, 1152069, 615465, 267309, 22563, 2165028, 2105876, 2186243, 2121738, 2184226, 96303, 96303, 156),
+    (886888, 365896, 2127983, 169, 824352, 210990, 2243105, 2230666, 88098, 2116622, 77859, 2102442, 2381868, 2241548, 93187, 11277, 9253, 99364, 98352, 119),
+    (346546, 1278098, 2261034, 2905353, 331937, 2113640, 465922, 94575, 210987, 2119852, 2128903, 2365476, 617473, 2122766, 2367653, 78853, 2124806, 100401, 100401, 151),
+    (624874, 2788554, 3412002, 84011, 2120048, 7504, 549961, 214060, 2113700, 27683, 97709, 2369765, 618535, 2106375, 13326, 2128934, 102450, 102450, 102450, 119),
+    (350578, 2658339, 91211, 2365482, 2908196, 93258, 1215492, 216205, 272688, 619792, 83057, 2247688, 79878, 2389029, 2112550, 2127919, 104499, 104499, 104499, 85),
+    (352627, 3039277, 1320275, 627853, 75819, 881700, 2126923, 622602, 275461, 80465, 2135206, 84143, 2129960, 2329615, 2114602, 2112521, 106548, 106548, 106548, 85),
+    (762029, 2794893, 356517, 2125939, 884780, 144972, 2792486, 342123, 2119855, 2112656, 2108431, 166058, 2179144, 37898, 2199593, 2116657, 108597, 108597, 108597, 89),
+    (764046, 886357, 2191526, 2916527, 80244, 2793485, 155781, 1133583, 823464, 2986323, 220297, 2333703, 2110508, 87048, 101387, 2118673, 111661, 110646, 110646, 85),
+    (1409135, 3440694, 226582, 362535, 2242613, 2128562, 2664456, 2126505, 2921673, 631848, 1332756, 155661, 2321452, 205994, 2132243, 2119723, 113715, 112695, 112695, 68),
+    (313529, 2261040, 81961, 362615, 102447, 105559, 1209423, 2134170, 2395144, 2115670, 2192170, 108587, 3169290, 2136653, 106540, 2272310, 2122772, 115757, 114744, 51),
+    (245809, 346266, 365656, 32947, 2135185, 349193, 244267, 2249875, 3431472, 2275374, 90292, 2325007, 3175572, 177164, 93238, 110093, 117781, 116793, 116793, 51),
+    (102521, 367106, 2397273, 245802, 2398321, 2512939, 2278417, 90292, 2400304, 44048, 2121847, 2117814, 93271, 228365, 2143413, 2191374, 120335, 118842, 118842, 49),
+    (367139, 2398330, 2282020, 102443, 247988, 2400300, 2280530, 2121877, 92216, 1280182, 2386955, 99416, 2467895, 2130574, 2133014, 1342510, 2194519, 120891, 120891, 17),
+    (368763, 2400772, 236635, 305274, 2187276, 2281654, 93203, 2386041, 2467954, 2405906, 2191374, 113753, 231439, 49200, 2212911, 2145297, 123920, 122940, 122940, 17),
+    (305276, 373852, 92212, 2386043, 2206870, 2139227, 2125870, 98419, 1079479, 2136186, 2456666, 376889, 2148402, 101399, 2393112, 2133010, 124989, 124989, 124989, 17),
+    (897149, 2288790, 375470, 254990, 240303, 1059000, 99420, 1141911, 2408571, 3177616, 107611, 2138169, 236565, 250905, 2150449, 2394258, 2200595, 127038, 127038, 17),
+    (127223, 2537656, 2408559, 3177502, 378941, 2410582, 98830, 240168, 2272272, 363085, 2156572, 2338875, 107053, 53298, 2154129, 2220051, 2139154, 2202682, 129087, 0),
 )
 EVENTS = 2 * (len(PLAN[0]) - 1)
 ROWS = 256

time: 67.5 us -> 65.5 us (0.970); the launches traced: 66.6 us -> 65.4 us
  Pallas kernels: 65 us -> 63.8 us
    pallas_call x1, Pallas kernels: 65 us -> 63.8 us  [per_device(): pl.pallas_call(kernel, name='face_attention', out_shape=jax.ShapeDtypeStr...]
where the time goes in v6:
time: 65.5 us; the launch traced here: 65.4 us
  Pallas kernels  63.8 us (97%)
  local copies, waits for them, and re-layouts  1.57 us (2%)
    pallas_call x1, Pallas kernels, per_device(): pl.pallas_call(kernel, name='face_attention', out_shape=jax.ShapeDtypeStr...  63.8 us
    unnamed x1, local copies, waits for them, and re-layouts  1.57 us

profile of v6, /device:TPU:5, one launch (start us, length us, event | category | flops | bytes accessed | tf_op | source)
XLA Modules:
  0.0 65.4 jit_solution(7355752648351873028)
XLA Ops:
  0.0 63.8 %face_attention.1 = bf16[256,256]{1,0:T(8,128)(2,1)} custom-call(bf16[256,256]{1,0:T(8,128)(2,1)} %x_hbm.1, f32[1,1024]{1,0:T(1,128)} %bitcast.4, bf16[3,1024,256]{2,1,0:T(8,128)(2,1)} %bitcast.3, bf16[256,1024]{1,0:T(8,128)(2,1)} %wout_hbm.1, s32[2,128]{1,0:T(2,128)} %bitcast.5), custom_call_target="tpu_custom_call" | custom-call | tf_op jit(solution)/shard_map/face_attention/pallas_call | solution.py:389
  63.8 1.6 %copy.7 = bf16[256,256]{1,0:T(8,128)(2,1)} copy(bf16[256,256]{1,0:T(8,128)(2,1)} %face_attention.1) | data formatting | bytes 262144

commit v7 on v6

--- a/solution.py
+++ b/solution.py
@@ -13,70 +13,70 @@
 epsilon = 1e-05
 masked_score = -1e30
 PLAN = (
-    (788743, 854536, 1585801, 1132930, 600994, 1153101, 564, 0, 0, 0, 0, 0, 0, 0, 0, 0, 0, 0, 0, 247),
-    (655490, 1905321, 214368, 1073331, 2573, 2049, 2049, 2049, 2049, 2049, 2049, 2049, 2049, 2049, 2049, 2049, 2049, 2049, 2049, 119),
-    (657930, 2820387, 1083456, 2687628, 606387, 4098, 4098, 4098, 4098, 4098, 4098, 4098, 4098, 4098, 4098, 4098, 4098, 4098, 4098, 123),
-    (659748, 1138018, 1335827, 657964, 1086561, 1141056, 7264, 6147, 6147, 6147, 6147, 6147, 6147, 6147, 6147, 6147, 6147, 6147, 6147, 181),
-    (286787, 1156451, 528941, 2298451, 2820353, 1079552, 9248, 8196, 8196, 8196, 8196, 8196, 8196, 8196, 8196, 8196, 8196, 8196, 8196, 125),
-    (139789, 2826797, 2824515, 594575, 595, 593184, 1084417, 11266, 10245, 10245, 10245, 10245, 10245, 10245, 10245, 10245, 10245, 10245, 10245, 217),
-    (665863, 2828847, 1341517, 663936, 2303136, 788547, 1082401, 543284, 1148195, 1087490, 13346, 12294, 12294, 12294, 12294, 12294, 12294, 12294, 12294, 213),
-    (786758, 2425391, 265254, 2427141, 266377, 158821, 533922, 531748, 15395, 14343, 14343, 14343, 14343, 14343, 14343, 14343, 14343, 14343, 14343, 203),
-    (346761, 2424832, 806983, 2951553, 2308166, 530562, 2432358, 142370, 1155332, 2696549, 16392, 16392, 16392, 16392, 16392, 16392, 16392, 16392, 16392, 127),
-    (147850, 3624, 525601, 268322, 2162759, 669091, 2833410, 368772, 2700708, 2697221, 18441, 18441, 18441, 18441, 18441, 18441, 18441, 18441, 18441, 247),
-    (69705, 1084777, 2435, 2431048, 2296834, 2957444, 669792, 144424, 2098471, 77094, 21509, 20490, 20490, 20490, 20490, 20490, 20490, 20490, 20490, 91),
-    (1087939, 1138762, 1086826, 4228, 1665353, 2170276, 2168169, 540673, 11297, 340096, 3343525, 2179143, 2110759, 22539, 22539, 22539, 22539, 22539, 22539, 213),
-    (551243, 1155268, 2695853, 1088619, 2168835, 135498, 272390, 2962538, 2435145, 16385, 343145, 1057, 2167840, 2112552, 24588, 24588, 24588, 24588, 24588, 125),
-    (76140, 154700, 205190, 2108582, 279556, 867691, 151619, 2183746, 1250, 1084840, 19491, 2182176, 3079, 27681, 26637, 26637, 26637, 26637, 26637, 251),
-    (1145222, 1731343, 2569325, 803143, 10572, 2964588, 2305448, 1155600, 678016, 8752, 2162985, 265252, 2316291, 2165795, 4106, 2167817, 29738, 28686, 28686, 68),
-    (473480, 13480, 18701, 2713600, 2307241, 2111502, 666784, 545036, 3372, 2173998, 5281, 2166795, 8739, 2186410, 2104356, 30735, 30735, 30735, 30735, 230),
-    (147857, 3097009, 686112, 281711, 146601, 2177290, 2969665, 12622, 2166126, 284674, 6413, 142701, 2098214, 2448418, 8204, 2173987, 2171948, 32784, 32784, 119),
-    (164233, 2444656, 147731, 2969866, 1315944, 2297889, 686219, 1679488, 2448751, 2562051, 8199, 2177094, 91137, 2121742, 2716710, 93220, 2123781, 35877, 34833, 119),
-    (1214867, 1315242, 810353, 893008, 85163, 2118768, 268296, 2310276, 2166956, 2171397, 2121807, 146441, 2324494, 2169133, 2911271, 2172934, 2192422, 36882, 36882, 85),
-    (809554, 2855348, 1121515, 165900, 271363, 2852970, 689324, 272585, 354446, 2172208, 2436237, 1262697, 2978888, 31754, 12295, 2176047, 39975, 38931, 38931, 91),
-    (942675, 2856964, 155052, 1321298, 2855054, 2185357, 2172581, 2978129, 2314442, 2189446, 2438513, 620560, 2195465, 2313231, 81959, 2245639, 40980, 40980, 40980, 181),
-    (92500, 1059214, 2436468, 2977875, 2121836, 2123814, 558214, 23923, 561167, 2317743, 1215858, 343216, 22151, 2722922, 81929, 2114601, 43029, 43029, 43029, 85),
-    (698830, 2338286, 2109478, 696976, 2455695, 28276, 278192, 90195, 16689, 2123123, 88201, 2190375, 2179122, 21521, 2182155, 2184210, 45078, 45078, 45078, 85),
-    (686480, 570607, 2732103, 2309552, 16974, 3371025, 568497, 2179149, 281653, 42221, 2203717, 156713, 563754, 2727050, 2318482, 2199563, 48171, 47127, 47127, 68),
-    (313424, 379424, 17456, 297047, 2340873, 300209, 2179590, 2127919, 2182322, 2338902, 1118218, 159763, 2192426, 88085, 2205805, 2123788, 2120755, 2187284, 50228, 51),
-    (180241, 2198648, 18578, 2181200, 2327074, 179378, 2341011, 21555, 1335467, 162858, 2325643, 176180, 2339860, 2449429, 27701, 2189326, 52270, 51225, 51225, 51),
-    (299522, 2345049, 1070258, 180243, 2184627, 2342961, 32939, 1074315, 2195604, 306257, 2203735, 2342060, 46261, 2127919, 95286, 2123821, 54286, 53274, 53274, 17),
-    (1120346, 2347187, 23044, 183467, 2203796, 306195, 25721, 2449458, 2467928, 2134065, 2189325, 164920, 2131990, 48240, 291894, 2210990, 2193423, 55323, 55323, 17),
-    (303748, 1058907, 306299, 24666, 105653, 2204794, 2187405, 3237913, 37014, 291961, 50226, 2469905, 47759, 33838, 2212913, 2327571, 2210991, 57372, 57372, 17),
-    (305797, 1124444, 2352373, 41510, 187021, 2189462, 2349198, 2470964, 2191450, 2347159, 32783, 104472, 168979, 117944, 2200623, 2149559, 2195505, 60433, 59421, 17),
-    (307878, 2353245, 2469980, 28823, 43160, 2475125, 2351151, 173071, 2473006, 313435, 101499, 2213978, 104464, 2335761, 2348080, 2134066, 62483, 61470, 61470, 17),
-    (440839, 311847, 2603038, 2475070, 313360, 59407, 2223215, 2476118, 58486, 298032, 175153, 1086581, 2221746, 172051, 56371, 54331, 2204730, 63519, 63519, 0),
-    (1130657, 1077775, 858241, 266761, 332334, 1073707, 610860, 66093, 65568, 65568, 65568, 65568, 65568, 65568, 65568, 65568, 65568, 65568, 65568, 119),
-    (197161, 2752898, 1083555, 1399338, 1142946, 1401392, 68492, 67617, 67617, 67617, 67617, 67617, 67617, 67617, 67617, 67617, 67617, 67617, 67617, 119),
-    (1397155, 1398881, 1072449, 1138720, 288064, 69666, 69666, 69666, 69666, 69666, 69666, 69666, 69666, 69666, 69666, 69666, 69666, 69666, 69666, 181),
-    (1137444, 1401186, 200002, 1140876, 537921, 1077312, 1084448, 72207, 71715, 71715, 71715, 71715, 71715, 71715, 71715, 71715, 71715, 71715, 71715, 91),
-    (727333, 1140035, 274572, 201261, 1339957, 328770, 2164737, 1084303, 74752, 73764, 73764, 73764, 73764, 73764, 73764, 73764, 73764, 73764, 73764, 151),
-    (1403270, 1419620, 204100, 1339552, 1342787, 2621538, 2232577, 77089, 75813, 75813, 75813, 75813, 75813, 75813, 75813, 75813, 75813, 75813, 75813, 87),
-    (731694, 1145486, 243525, 852589, 1341540, 2884676, 596501, 2759073, 2361634, 78850, 77862, 77862, 77862, 77862, 77862, 77862, 77862, 77862, 77862, 53),
-    (78511, 1472672, 2635136, 1208872, 600225, 2632240, 1081910, 2361869, 529261, 71716, 2167346, 2104580, 80404, 79911, 79911, 79911, 79911, 79911, 79911, 68),
-    (555488, 1274505, 736512, 2242594, 602497, 2625835, 335174, 75812, 2366625, 349445, 82948, 81960, 81960, 81960, 81960, 81960, 81960, 81960, 81960, 127),
-    (1083496, 1904993, 2245761, 1147051, 196899, 1663854, 212098, 336896, 2890823, 12325, 2107660, 2700676, 84009, 84009, 84009, 84009, 84009, 84009, 84009, 125),
-    (1399202, 1595753, 2771107, 860588, 2365537, 2102273, 196936, 862509, 211246, 2893127, 2229381, 537704, 87462, 86058, 86058, 86058, 86058, 86058, 86058, 93),
-    (217772, 336259, 201802, 740269, 2232485, 2169929, 200069, 2231428, 2371750, 1083656, 604192, 2098439, 89128, 88107, 88107, 88107, 88107, 88107, 88107, 127),
-    (743597, 2251044, 553125, 2894051, 2103402, 2367750, 2962506, 79970, 606313, 2636866, 556105, 68113, 2100488, 2162688, 90156, 90156, 90156, 90156, 90156, 207),
-    (600629, 745774, 2369678, 2437510, 743524, 2251175, 345156, 2252835, 2898947, 2900330, 263498, 70816, 67881, 2100226, 93193, 92205, 92205, 92205, 92205, 95),
-    (1141222, 867661, 10664, 2898453, 328840, 678252, 2316388, 2098252, 18530, 2173954, 86017, 2106401, 7178, 2182150, 95267, 94254, 94254, 94254, 94254, 251),
-    (997742, 3175080, 2901447, 209456, 1081376, 1076224, 806086, 264293, 1152069, 615465, 267309, 22563, 2165028, 2105876, 2186243, 2121738, 2184226, 96303, 96303, 156),
-    (886888, 365896, 2127983, 169, 824352, 210990, 2243105, 2230666, 88098, 2116622, 77859, 2102442, 2381868, 2241548, 93187, 11277, 9253, 99364, 98352, 119),
-    (346546, 1278098, 2261034, 2905353, 331937, 2113640, 465922, 94575, 210987, 2119852, 2128903, 2365476, 617473, 2122766, 2367653, 78853, 2124806, 100401, 100401, 151),
-    (624874, 2788554, 3412002, 84011, 2120048, 7504, 549961, 214060, 2113700, 27683, 97709, 2369765, 618535, 2106375, 13326, 2128934, 102450, 102450, 102450, 119),
-    (350578, 2658339, 91211, 2365482, 2908196, 93258, 1215492, 216205, 272688, 619792, 83057, 2247688, 79878, 2389029, 2112550, 2127919, 104499, 104499, 104499, 85),
-    (352627, 3039277, 1320275, 627853, 75819, 881700, 2126923, 622602, 275461, 80465, 2135206, 84143, 2129960, 2329615, 2114602, 2112521, 106548, 106548, 106548, 85),
-    (762029, 2794893, 356517, 2125939, 884780, 144972, 2792486, 342123, 2119855, 2112656, 2108431, 166058, 2179144, 37898, 2199593, 2116657, 108597, 108597, 108597, 89),
-    (764046, 886357, 2191526, 2916527, 80244, 2793485, 155781, 1133583, 823464, 2986323, 220297, 2333703, 2110508, 87048, 101387, 2118673, 111661, 110646, 110646, 85),
-    (1409135, 3440694, 226582, 362535, 2242613, 2128562, 2664456, 2126505, 2921673, 631848, 1332756, 155661, 2321452, 205994, 2132243, 2119723, 113715, 112695, 112695, 68),
-    (313529, 2261040, 81961, 362615, 102447, 105559, 1209423, 2134170, 2395144, 2115670, 2192170, 108587, 3169290, 2136653, 106540, 2272310, 2122772, 115757, 114744, 51),
-    (245809, 346266, 365656, 32947, 2135185, 349193, 244267, 2249875, 3431472, 2275374, 90292, 2325007, 3175572, 177164, 93238, 110093, 117781, 116793, 116793, 51),
-    (102521, 367106, 2397273, 245802, 2398321, 2512939, 2278417, 90292, 2400304, 44048, 2121847, 2117814, 93271, 228365, 2143413, 2191374, 120335, 118842, 118842, 49),
-    (367139, 2398330, 2282020, 102443, 247988, 2400300, 2280530, 2121877, 92216, 1280182, 2386955, 99416, 2467895, 2130574, 2133014, 1342510, 2194519, 120891, 120891, 17),
-    (368763, 2400772, 236635, 305274, 2187276, 2281654, 93203, 2386041, 2467954, 2405906, 2191374, 113753, 231439, 49200, 2212911, 2145297, 123920, 122940, 122940, 17),
-    (305276, 373852, 92212, 2386043, 2206870, 2139227, 2125870, 98419, 1079479, 2136186, 2456666, 376889, 2148402, 101399, 2393112, 2133010, 124989, 124989, 124989, 17),
-    (897149, 2288790, 375470, 254990, 240303, 1059000, 99420, 1141911, 2408571, 3177616, 107611, 2138169, 236565, 250905, 2150449, 2394258, 2200595, 127038, 127038, 17),
-    (127223, 2537656, 2408559, 3177502, 378941, 2410582, 98830, 240168, 2272272, 363085, 2156572, 2338875, 107053, 53298, 2154129, 2220051, 2139154, 2202682, 129087, 0),
+    (1065223, 854657, 1061385, 332162, 1069317, 1141292, 524, 0, 0, 0, 0, 0, 0, 0, 0, 0, 0, 0, 0, 247),
+    (131593, 1133442, 1069474, 1137760, 1335980, 2049, 2049, 2049, 2049, 2049, 2049, 2049, 2049, 2049, 2049, 2049, 2049, 2049, 2049, 119),
+    (133642, 598307, 656481, 1402208, 1140876, 4660, 4098, 4098, 4098, 4098, 4098, 4098, 4098, 4098, 4098, 4098, 4098, 4098, 4098, 123),
+    (1071170, 1137060, 2822796, 658092, 2820653, 2294016, 6705, 6147, 6147, 6147, 6147, 6147, 6147, 6147, 6147, 6147, 6147, 6147, 6147, 117),
+    (662156, 2824876, 660141, 2822950, 1157377, 590945, 9216, 8196, 8196, 8196, 8196, 8196, 8196, 8196, 8196, 8196, 8196, 8196, 8196, 125),
+    (1075524, 2826662, 1587523, 525411, 1144834, 2163746, 2099233, 10245, 10245, 10245, 10245, 10245, 10245, 10245, 10245, 10245, 10245, 10245, 10245, 85),
+    (665991, 1143310, 787557, 139791, 2949807, 138596, 2689025, 2824450, 13602, 12294, 12294, 12294, 12294, 12294, 12294, 12294, 12294, 12294, 12294, 181),
+    (786502, 2699791, 667040, 2427009, 1082661, 8578, 2696610, 223235, 15395, 14343, 14343, 14343, 14343, 14343, 14343, 14343, 14343, 14343, 14343, 75),
+    (131721, 2294666, 264295, 2952263, 2830406, 268613, 2166786, 2829475, 2171140, 16392, 16392, 16392, 16392, 16392, 16392, 16392, 16392, 16392, 16392, 127),
+    (789130, 2310216, 2820907, 792642, 2955623, 2428960, 668672, 2242724, 2831492, 616517, 19493, 18441, 18441, 18441, 18441, 18441, 18441, 18441, 18441, 223),
+    (673963, 595305, 2955651, 67912, 861288, 1403444, 1412, 2101607, 2100256, 600326, 2176071, 21765, 20490, 20490, 20490, 20490, 20490, 20490, 20490, 91),
+    (151939, 615715, 599402, 354633, 2367522, 265321, 1149256, 2835553, 337920, 2699526, 2111783, 2163714, 23557, 22539, 22539, 22539, 22539, 22539, 22539, 189),
+    (270411, 2171821, 863595, 6709, 2300234, 274697, 2438506, 2494562, 133423, 2296937, 1048583, 2703624, 2370720, 25895, 24588, 24588, 24588, 24588, 24588, 185),
+    (680197, 2842805, 603621, 2371652, 2170955, 2841007, 137351, 540800, 2439242, 2704419, 2838530, 1050633, 2163746, 2165801, 26637, 26637, 26637, 26637, 26637, 125),
+    (158150, 1407759, 15725, 680328, 2439173, 2176364, 2965504, 140325, 2425225, 2123, 2841636, 7201, 544770, 2184227, 2182178, 28686, 28686, 28686, 28686, 204),
+    (997768, 1082792, 524358, 2111625, 552038, 28938, 3763232, 10369, 549989, 2165806, 5164, 6148, 2171939, 2166795, 2186409, 31786, 30735, 30735, 30735, 110),
+    (297032, 2834609, 65615, 281967, 2119, 153001, 2177358, 2166126, 5546, 875520, 2906150, 551942, 2304069, 7213, 2167843, 2170884, 2187276, 32784, 32784, 119),
+    (280656, 2852009, 266666, 630888, 350543, 146799, 2099233, 2114699, 2117763, 29735, 91299, 2323618, 336141, 2105446, 2122797, 76806, 35845, 34833, 34833, 119),
+    (690451, 2328746, 688820, 2851211, 6146, 352361, 2429987, 288808, 336207, 2325636, 2115655, 2117902, 2186279, 2192429, 2114572, 12325, 2108454, 36882, 36882, 85),
+    (692427, 2330804, 559107, 9251, 353905, 86157, 164907, 2122852, 816432, 2312201, 2451464, 2180106, 12325, 556078, 2108454, 80943, 39943, 38931, 38931, 87),
+    (270675, 814451, 88402, 24718, 2251890, 414764, 2977957, 3418417, 558125, 149510, 2184209, 2182192, 30727, 82991, 2171912, 2176039, 40980, 40980, 40980, 117),
+    (289108, 2714996, 272526, 2977875, 25971, 2187398, 2173200, 2174994, 2330767, 2194608, 88263, 2250769, 2177032, 2179082, 19505, 2184233, 43029, 43029, 43029, 212),
+    (764110, 275694, 820774, 96340, 2983055, 93556, 822293, 16723, 2857127, 2983948, 2180204, 102569, 2116615, 23565, 87083, 2135050, 45078, 45078, 45078, 69),
+    (569423, 3111568, 2982471, 16974, 108945, 2460903, 566894, 2208808, 2727945, 38976, 421545, 2140170, 2321459, 3493906, 88140, 2319410, 48139, 47127, 47127, 68),
+    (163993, 2196000, 16569, 1050711, 2179089, 2340873, 300209, 176646, 97458, 21519, 2181267, 160886, 2323635, 2183189, 88108, 224373, 41995, 2124812, 50228, 51),
+    (297048, 2591234, 2343058, 99506, 18579, 179241, 2131063, 218291, 176171, 2117743, 2119828, 2128950, 2466316, 43118, 2187277, 2206734, 52269, 51225, 51225, 51),
+    (1052818, 2592857, 302201, 2464266, 180241, 2197652, 1137784, 90192, 3170391, 306315, 2196599, 93226, 2203663, 46093, 29750, 2206767, 54318, 53274, 53274, 17),
+    (39002, 2348211, 303193, 36875, 2331700, 167595, 1336441, 49301, 1141804, 2342934, 2471053, 2197520, 48240, 2467854, 2192439, 2127919, 55323, 55323, 55323, 17),
+    (303620, 2465883, 2349580, 306732, 184403, 2348083, 182317, 1126550, 2471053, 2134130, 49745, 2346165, 2453518, 2211863, 359537, 33807, 2210928, 57372, 57372, 17),
+    (188629, 2206844, 26774, 172123, 2204854, 1064059, 291885, 2191379, 184472, 359475, 2347159, 2390032, 2471961, 2211890, 2213905, 2135089, 60464, 59421, 59421, 17),
+    (307293, 2601510, 291965, 1222808, 2192501, 188567, 292880, 2473007, 2196604, 107704, 35860, 186393, 2201619, 2350137, 1348657, 2347098, 62514, 61470, 61470, 17),
+    (311815, 61655, 2604216, 314430, 59478, 2193487, 2477686, 2222128, 2197521, 41557, 1348624, 2204789, 59058, 55315, 2202684, 54331, 64570, 63519, 63519, 0),
+    (1065377, 1585679, 487586, 1077667, 1137162, 1134892, 1075492, 65568, 65568, 65568, 65568, 65568, 65568, 65568, 65568, 65568, 65568, 65568, 65568, 119),
+    (331872, 859456, 1401514, 1073710, 67617, 67617, 67617, 67617, 67617, 67617, 67617, 67617, 67617, 67617, 67617, 67617, 67617, 67617, 67617, 87),
+    (723875, 1151658, 1133889, 1401184, 2228755, 69772, 69666, 69666, 69666, 69666, 69666, 69666, 69666, 69666, 69666, 69666, 69666, 69666, 69666, 151),
+    (1136994, 1088834, 199308, 1142081, 1089568, 73024, 71715, 71715, 71715, 71715, 71715, 71715, 71715, 71715, 71715, 71715, 71715, 71715, 71715, 91),
+    (2824515, 201261, 1143444, 593218, 2099488, 1147904, 73764, 73764, 73764, 73764, 73764, 73764, 73764, 73764, 73764, 73764, 73764, 73764, 73764, 213),
+    (1403174, 2236772, 1061389, 1405492, 2824259, 725152, 2757632, 1146913, 77057, 75813, 75813, 75813, 75813, 75813, 75813, 75813, 75813, 75813, 75813, 213),
+    (207534, 2763015, 1144992, 2883940, 1092932, 661665, 594979, 1150274, 79233, 77862, 77862, 77862, 77862, 77862, 77862, 77862, 77862, 77862, 77862, 126),
+    (1145248, 668239, 160896, 330021, 1141765, 1081700, 2175010, 1143812, 71757, 1092867, 2102401, 79911, 79911, 79911, 79911, 79911, 79911, 79911, 79911, 228),
+    (721289, 2884142, 1399143, 2243210, 2951553, 143651, 333158, 2627909, 353637, 74754, 82948, 81960, 81960, 81960, 81960, 81960, 81960, 81960, 81960, 247),
+    (592010, 350312, 2362696, 131490, 597024, 2889831, 2243586, 598086, 2176388, 2697221, 84009, 84009, 84009, 84009, 84009, 84009, 84009, 84009, 84009, 117),
+    (1151403, 1139305, 2247074, 1087587, 198760, 617473, 337027, 605256, 2101344, 601088, 2243716, 2107654, 87078, 86058, 86058, 86058, 86058, 86058, 86058, 125),
+    (741548, 1073811, 2249091, 215725, 860258, 2102537, 134179, 83076, 2165157, 2369600, 2163720, 536839, 2178470, 88107, 88107, 88107, 88107, 88107, 88107, 95),
+    (860333, 2840651, 619028, 2367909, 2369603, 341027, 2642026, 2896169, 866306, 2166880, 199216, 2113832, 2098177, 2112521, 90156, 90156, 90156, 90156, 90156, 119),
+    (356837, 2842700, 1156229, 6566, 2371947, 73895, 869475, 1148039, 2775074, 2900074, 2162688, 19458, 2106378, 2181153, 93185, 92205, 92205, 92205, 92205, 223),
+    (209005, 2372143, 867661, 1092999, 344101, 156741, 74888, 806188, 2162816, 613572, 6705, 2300170, 69665, 2233419, 2444330, 95233, 94254, 94254, 94254, 95),
+    (344551, 3699054, 1142152, 1082439, 1257865, 3697670, 2424832, 2238565, 74261, 283137, 615585, 89257, 70668, 7435, 2102307, 2106410, 96303, 96303, 96303, 142),
+    (887272, 297327, 66568, 870834, 349449, 2118656, 133191, 2309135, 1052718, 71750, 2165862, 2167822, 2103467, 90125, 2189317, 2173963, 74764, 99332, 98352, 55),
+    (229810, 347472, 2771114, 67688, 2246026, 751915, 2429570, 24611, 146447, 2103597, 226348, 336897, 2126887, 13323, 2368614, 2172933, 101389, 100401, 100401, 119),
+    (3035306, 2721873, 754091, 2906754, 2166819, 91472, 19852, 214019, 2312621, 9288, 79983, 2171917, 76807, 29829, 2192463, 2174982, 102450, 102450, 102450, 91),
+    (88434, 877963, 2265123, 218252, 2366474, 270673, 813424, 2786468, 149637, 2197806, 2912296, 2190373, 2245673, 14703, 13327, 2176039, 104499, 104499, 104499, 149),
+    (760236, 2792652, 2367524, 757805, 2910251, 273746, 357413, 2912362, 1147217, 78922, 216400, 2110985, 342024, 97585, 2180103, 2128907, 106548, 106548, 106548, 149),
+    (486004, 2793750, 273549, 2172974, 155763, 2188686, 341331, 1147186, 2790470, 88103, 96362, 2656689, 2373672, 3167435, 2129929, 2182152, 109711, 108597, 108597, 85),
+    (356725, 763477, 78990, 2793648, 2123821, 96423, 1411148, 629895, 2128940, 83283, 168966, 86153, 2656299, 2114634, 2200587, 2130985, 110646, 110646, 110646, 116),
+    (569520, 3178607, 632942, 145841, 3189799, 2126991, 18600, 631953, 889992, 2664105, 2320397, 24851, 88618, 2202642, 2120714, 2188342, 112695, 112695, 112695, 68),
+    (491705, 82073, 100471, 316424, 2395223, 3307567, 102518, 2273798, 85138, 21070, 108723, 1137673, 92212, 1139754, 2131533, 2192907, 2141708, 2137108, 114744, 51),
+    (315512, 2197713, 87128, 2396210, 366711, 18480, 2276368, 369674, 1210411, 2325164, 242222, 2137129, 2382870, 2385486, 2140213, 3172397, 117780, 116793, 116793, 51),
+    (299522, 2345049, 231971, 368819, 1395762, 98424, 91224, 21651, 2185355, 2184209, 2130039, 371279, 2122839, 2402349, 2401327, 95245, 2207766, 119822, 118842, 49),
+    (250403, 2281651, 368690, 2119723, 370777, 2136108, 2403449, 35916, 3246134, 1140784, 2386040, 2131094, 2278548, 2134190, 2125879, 2275407, 121903, 120891, 120891, 17),
+    (252084, 2284036, 370732, 235642, 93333, 2281654, 2405395, 103444, 2123865, 94263, 2397305, 2122766, 34863, 2146360, 2195472, 2198543, 123927, 122940, 122940, 17),
+    (254133, 2402821, 373852, 2404397, 2123899, 1060884, 375899, 94330, 114739, 1408052, 2137166, 2145370, 51250, 2147346, 229425, 3177529, 2130961, 124989, 124989, 17),
+    (504358, 2287741, 95254, 108727, 376956, 1407028, 2407516, 2408571, 2139157, 117851, 2390138, 105486, 2137113, 1344538, 2132017, 2195474, 128050, 127038, 127038, 17),
+    (377079, 1062974, 2409687, 97310, 379510, 3439702, 98333, 240793, 54333, 100973, 2132028, 226512, 300060, 120884, 2462805, 2269747, 2268187, 130106, 129087, 0),
 )
 EVENTS = 2 * (len(PLAN[0]) - 1)
 ROWS = 256

time: 65.5 us -> 67.3 us (1.027)
  Pallas kernels: 63.8 us -> 65.7 us
    pallas_call x1, Pallas kernels: 63.8 us -> 65.7 us  [per_device(): pl.pallas_call(kernel, name='face_attention', out_shape=jax.ShapeDtypeStr...]
where the time goes in v7:
time: 67.3 us; the launch traced here: 67.2 us
  Pallas kernels  65.7 us (98%)
  local copies, waits for them, and re-layouts  1.57 us (2%)
    pallas_call x1, Pallas kernels, per_device(): pl.pallas_call(kernel, name='face_attention', out_shape=jax.ShapeDtypeStr...  65.7 us
    unnamed x1, local copies, waits for them, and re-layouts  1.57 us

profile of v7, /device:TPU:5, one launch (start us, length us, event | category | flops | bytes accessed | tf_op | source)
XLA Modules:
  0.0 67.2 jit_solution(9671526066356705667)
XLA Ops:
  0.0 65.7 %face_attention.1 = bf16[256,256]{1,0:T(8,128)(2,1)} custom-call(bf16[256,256]{1,0:T(8,128)(2,1)} %x_hbm.1, f32[1,1024]{1,0:T(1,128)} %bitcast.4, bf16[3,1024,256]{2,1,0:T(8,128)(2,1)} %bitcast.3, bf16[256,1024]{1,0:T(8,128)(2,1)} %wout_hbm.1, s32[2,128]{1,0:T(2,128)} %bitcast.5), custom_call_target="tpu_custom_call" | custom-call | tf_op jit(solution)/shard_map/face_attention/pallas_call | solution.py:389
  65.7 1.6 %copy.7 = bf16[256,256]{1,0:T(8,128)(2,1)} copy(bf16[256,256]{1,0:T(8,128)(2,1)} %face_attention.1) | data formatting | bytes 262144
